TPU v7x, 1024 devices: a whole 4x8x16 slice. The times are simulated.
1024 devices in a mesh: gx: 32 (over z, core), gy: 4 (over x), gz: 8 (over y).
Axes of the slice: x: 4, y: 8, z: 16, core: 2. Of those that a mesh axis runs over, the one named last changes fastest.
Arguments:
- conductivity: float32 [128, 256, 512], P('gx', 'gz', 'gy'), may hold values from 0.2 to 5
- initial_guess: float32 [128, 256, 512], P('gx', 'gz', 'gy'), may hold values from -6 to 6
- right_side: float32 [128, 256, 512], P('gx', 'gz', 'gy')
Outputs:
- fine_solution: float32 [128, 256, 512], P('gx', 'gz', 'gy')
- level_one_solution: float32 [64, 128, 256], P('gx', 'gz', 'gy')
- level_two_solution: float32 [32, 64, 128], P(None, 'gz', 'gy')
- level_three_solution: float32 [16, 32, 64], P(None, 'gz', 'gy')
- level_three_residual: float32 [16, 32, 64], P(None, 'gz', 'gy')
All inputs are finite; a program needn't handle non-finite values.
Results may differ from a plain program's by a relative error of at most 0.000034.
Values sent between devices are 32-bit elements; how exact they have to be, the bound alone decides.
No kernel may reach another device: no remote copies, remote signals or barrier semaphores. Data moves between devices by JAX's collectives and lax.ppermute only.
A program may use at most 32 MiB of HBM per device.

v0:
```python
import jax
import jax.numpy as jnp
from jax import lax
from jax.sharding import PartitionSpec as P

SWEEPS = 3


lower_bound = 0.25
upper_bound = 2.0


def padded_2(shard, sides, width):
    edges = {}
    for axis, dim in sides:
        peers, length = (lax.axis_size(axis), shard.shape[dim])
        up = [(i, (i + 1) % peers) for i in range(peers - 1)]
        last = lax.slice_in_dim(shard, length - width, length, axis=dim)
        leading = lax.slice_in_dim(shard, 0, width, axis=dim)
        edges[dim] = (
            lax.ppermute(last, axis, up),
            lax.ppermute(leading, axis, [(b, a) for a, b in up]),
        )
    done = []
    for _, dim in sides:
        low, high = edges[dim]
        around = [(width, width) if d in done else (0, 0) for d in range(shard.ndim)]
        shard = jnp.concatenate([jnp.pad(low, around), shard, jnp.pad(high, around)], axis=dim)
        done.append(dim)
    return shard


def with_halo(block, sides, width):
    for axis, dim in sides:
        count = lax.axis_size(axis)
        forward = [(i, i + 1) for i in range(count - 1)]
        backward = [(target, source) for source, target in forward]
        low = lax.ppermute(
            lax.slice_in_dim(block, block.shape[dim] - width, None, axis=dim), axis, forward
        )
        high = lax.ppermute(lax.slice_in_dim(block, 0, width, axis=dim), axis, backward)
        block = jnp.concatenate([low, block, high], axis=dim)
    return block


def in_order(blocks, dim):
    dims = list(blocks.shape[1:])
    dims[dim] *= blocks.shape[0]
    return jnp.moveaxis(blocks, 0, dim).reshape(dims)


def copy_for_each(shard, axis):
    peers = lax.axis_size(axis)
    return lax.all_to_all(
        jnp.broadcast_to(shard[None], (peers, *shard.shape)), axis, 0, 0, tiled=True
    )


def gathered_copies(shard, axis, dim):
    return in_order(copy_for_each(shard, axis), dim)


def extend(bundle):
    return padded_2(bundle, (("gx", 1), ("gy", 3), ("gz", 2)), 1)


def deep_extend(bundle, merged):
    if merged:
        grown = with_halo(bundle, (("gy", 3), ("gz", 2)), 4)
        return jnp.pad(grown, ((0, 0), (4, 4), (0, 0), (0, 0)))
    return with_halo(bundle, (("gx", 1), ("gy", 3), ("gz", 2)), 4)


def neighbours(padded):
    return [
        padded[:-2, 1:-1, 1:-1],
        padded[2:, 1:-1, 1:-1],
        padded[1:-1, :-2, 1:-1],
        padded[1:-1, 2:, 1:-1],
        padded[1:-1, 1:-1, :-2],
        padded[1:-1, 1:-1, 2:],
    ]


def face_terms(conduct):
    others = neighbours(extend(conduct[None])[0])
    weights = [0.5 * (conduct + other) for other in others]
    diagonal = weights[0] + weights[1] + weights[2] + weights[3] + weights[4] + weights[5]
    return (weights, diagonal)


def operate(field, weights, diagonal):
    others = neighbours(extend(field[None])[0])
    result = diagonal * field
    for face_index in range(6):
        result = result - weights[face_index] * others[face_index]
    return result


def smooth(source, conduct):
    theta = 0.5 * (upper_bound + lower_bound)
    delta = 0.5 * (upper_bound - lower_bound)
    sigma = theta / delta
    weights, diagonal = face_terms(conduct)
    solution = jnp.zeros_like(source)
    residual = source
    direction = residual / (theta * diagonal)
    ratio_now = 1.0 / sigma
    for sweep_index in range(SWEEPS):
        solution = solution + direction
        residual = residual - operate(direction, weights, diagonal)
        if sweep_index + 1 < SWEEPS:
            ratio_next = 1.0 / (2.0 * sigma - ratio_now)
            direction = (
                ratio_next * ratio_now * direction + 2.0 * ratio_next / delta * residual / diagonal
            )
            ratio_now = ratio_next
    return (solution, residual)


def local_operate(field, weights, diagonal):
    others = neighbours(jnp.pad(field, 1))
    result = diagonal * field
    for face_index in range(6):
        result = result - weights[face_index] * others[face_index]
    return result


def smooth_deep(source, start, conduct, merged):
    theta = 0.5 * (upper_bound + lower_bound)
    delta = 0.5 * (upper_bound - lower_bound)
    sigma = theta / delta
    members = [conduct, source, jnp.ones_like(source)]
    if start is not None:
        members.append(start)
    grown = deep_extend(jnp.stack(members), merged)
    padded_conduct = grown[0]
    padded_source = grown[1]
    inside = grown[2]
    others = neighbours(jnp.pad(padded_conduct, 1))
    weights = [0.5 * (padded_conduct + other) for other in others]
    diagonal = weights[0] + weights[1] + weights[2] + weights[3] + weights[4] + weights[5]
    safe_diagonal = jnp.where(inside > 0.5, diagonal, 1.0)
    if start is None:
        solution = jnp.zeros_like(padded_source)
        residual = padded_source
    else:
        solution = grown[3]
        residual = padded_source - local_operate(solution, weights, diagonal)
    direction = inside * (residual / (theta * safe_diagonal))
    ratio_now = 1.0 / sigma
    for sweep_index in range(SWEEPS):
        solution = solution + direction
        residual = residual - local_operate(direction, weights, diagonal)
        if sweep_index + 1 < SWEEPS:
            ratio_next = 1.0 / (2.0 * sigma - ratio_now)
            direction = inside * (
                ratio_next * ratio_now * direction
                + 2.0 * ratio_next / delta * residual / safe_diagonal
            )
            ratio_now = ratio_next
    return (solution[4:-4, 4:-4, 4:-4], residual[4:-4, 4:-4, 4:-4])


def level_smooth(source, start, conduct, merged):
    extents = source.shape[1:] if merged else source.shape
    if min(extents) >= 4:
        return smooth_deep(source, start, conduct, merged)
    return smooth(source, conduct)


def coarse_sum(field):
    first, second, third = field.shape
    blocks = field.reshape(first // 2, 2, second // 2, 2, third // 2, 2)
    return jnp.sum(blocks, axis=(1, 3, 5))


def shards(conductivity, initial_guess, right_side):
    fine_solution, residual_zero = level_smooth(right_side, initial_guess, conductivity, False)
    conduct_one = 0.125 * coarse_sum(conductivity)
    level_one_solution, residual_one = level_smooth(
        0.25 * coarse_sum(residual_zero), None, conduct_one, False
    )
    conduct_two = 0.125 * coarse_sum(conduct_one)
    source_two = 0.25 * coarse_sum(residual_one)
    bundle = jnp.stack([source_two, conduct_two])
    bundle = gathered_copies(bundle, "gx", 1)
    level_two_solution, residual_two = level_smooth(bundle[0], None, bundle[1], True)
    conduct_three = 0.125 * coarse_sum(bundle[1])
    level_three_solution, level_three_residual = level_smooth(
        0.25 * coarse_sum(residual_two), None, conduct_three, True
    )
    return (
        fine_solution,
        level_one_solution,
        level_two_solution,
        level_three_solution,
        level_three_residual,
    )


def solution(mesh):
    placed = (P("gx", "gz", "gy"), P("gx", "gz", "gy"), P("gx", "gz", "gy"))
    return jax.shard_map(
        shards,
        mesh=mesh,
        in_specs=placed,
        out_specs=(
            P("gx", "gz", "gy"),
            P("gx", "gz", "gy"),
            P(None, "gz", "gy"),
            P(None, "gz", "gy"),
            P(None, "gz", "gy"),
        ),
        check_vma=False,
    )
```

profile of v0, /device:TPU:46, one launch (start us, length us, event | category | flops | bytes accessed | tf_op | source)
XLA Modules:
  0.0 225.3 jit_solution(14770417011239034058)
XLA Ops:
  2.9 3.0 %collective-permute-start = (f32[4,4,32,128]{3,2,1,0:T(8,128)S(1)}, f32[4,4,32,128]{3,2,1,0:T(8,128)S(1)}, u32[]{:S(2)}, u32[]{:S(2)}) collective-permute-start(f32[4,4,32,128]{3,2,1,0:T(8,128)S(1)} %pad_maximum_fusion.5), channel_id=1, source_target_pairs={{0,32},{32,64},{64,96},{96,128},{128,160},{160,192},{192,224},{224... | collective-permute-start | bytes 786440 | tf_op jit(solution)/shard_map/ppermute | solution.py:38
  5.9 6.3 %reshape.85 = f32[2,2,16,2,64,2]{5,4,3,2,1,0:T(8,128)} reshape(f32[4,32,128]{2,1,0:T(8,128)} %param.3) | data formatting | bytes 131072 | tf_op jit(solution)/shard_map/reshape | solution.py:174
  12.2 2.6 %reduce_sum.69 = f32[2,16,64]{2,1,0:T(8,128)S(1)} reduce(f32[2,2,16,2,64,2]{5,4,3,2,1,0:T(8,128)} %reshape.85, f32[]{:T(128)} %constant.11.clone.1), dimensions={1,3,5}, to_apply=%region_1.2 | reduce | flops 14336 | bytes 73732 | tf_op jit(solution)/shard_map/reduce_sum | solution.py:175
  14.9 3.3 %collective-permute-start.11 = (f32[1,2,1,64]{3,2,1,0:T(1,128)S(1)}, f32[1,2,1,64]{3,2,1,0:T(1,128)S(1)}, u32[]{:S(2)}, u32[]{:S(2)}) collective-permute-start(f32[1,2,1,64]{3,2,1,0:T(1,128)S(1)} %get-tuple-element.116), channel_id=1, source_target_pairs={{1,0},{2,1},{3,2},{4,3},{5,4},{6,5},{7,6},{9,8},{10,9},{11,10},{12... | collective-permute-start | bytes 1544 | tf_op jit(solution)/shard_map/ppermute | solution.py:22
  18.2 2.7 %collective-permute-start.10 = (f32[1,2,16,1]{3,2,1,0:T(8,128)S(1)}, f32[1,2,16,1]{3,2,1,0:T(8,128)S(1)}, u32[]{:S(2)}, u32[]{:S(2)}) collective-permute-start(f32[1,2,16,1]{3,2,1,0:T(8,128)S(1)} %get-tuple-element.118), channel_id=1, source_target_pairs={{8,0},{16,8},{24,16},{9,1},{17,9},{25,17},{10,2},{18,10},{26,18},{... | collective-permute-start | bytes 392 | tf_op jit(solution)/shard_map/ppermute | solution.py:22
  23.0 4.6 %collective-permute-start.3 = (f32[4,12,32,4]{2,3,1,0:T(4,128)S(1)}, f32[4,12,32,4]{2,3,1,0:T(4,128)S(1)}, u32[]{:S(2)}, u32[]{:S(2)}) collective-permute-start(f32[4,12,32,4]{2,3,1,0:T(4,128)S(1)} %copy.20), channel_id=1, source_target_pairs={{8,0},{16,8},{24,16},{9,1},{17,9},{25,17},{10,2},{18,10},{26,18},{... | collective-permute-start | bytes 73736 | tf_op jit(solution)/shard_map/ppermute | solution.py:41
  37.7 3.0 %collective-permute-start.8 = (f32[1,1,16,64]{3,2,1,0:T(8,128)S(1)}, f32[1,1,16,64]{3,2,1,0:T(8,128)S(1)}, u32[]{:S(2)}, u32[]{:S(2)}) collective-permute-start(f32[1,1,16,64]{3,2,1,0:T(8,128)S(1)} %get-tuple-element.113), channel_id=1, source_target_pairs={{0,32},{32,64},{64,96},{96,128},{128,160},{160,192},{192,224},{224... | collective-permute-start | bytes 12296 | tf_op jit(solution)/shard_map/ppermute | solution.py:21
  43.2 3.5 %collective-permute-start.4 = (f32[4,12,4,136]{3,2,1,0:T(4,128)S(1)}, f32[4,12,4,136]{3,2,1,0:T(4,128)S(1)}, u32[]{:S(2)}, u32[]{:S(2)}) collective-permute-start(f32[4,12,4,136]{3,2,1,0:T(4,128)S(1)} %get-tuple-element.61), channel_id=1, source_target_pairs={{0,1},{1,2},{2,3},{3,4},{4,5},{5,6},{6,7},{8,9},{9,10},{10,11},{11... | collective-permute-start | bytes 313352 | tf_op jit(solution)/shard_map/ppermute | solution.py:38
  46.8 2.6 %collective-permute-done.5 = f32[4,12,4,136]{3,2,1,0:T(4,128)S(1)} collective-permute-done((f32[4,12,4,136]{3,2,1,0:T(4,128)S(1)}, f32[4,12,4,136]{3,2,1,0:T(4,128)S(1)}, u32[]{:S(2)}, u32[]{:S(2)}) %collective-permute-start.5) | collective-permute-done | bytes 104480 | tf_op jit(solution)/shard_map/ppermute | solution.py:41
  49.5 2.7 %collective-permute-done.4 = f32[4,12,4,136]{3,2,1,0:T(4,128)S(1)} collective-permute-done((f32[4,12,4,136]{3,2,1,0:T(4,128)S(1)}, f32[4,12,4,136]{3,2,1,0:T(4,128)S(1)}, u32[]{:S(2)}, u32[]{:S(2)}) %collective-permute-start.4) | collective-permute-done | bytes 104480 | tf_op jit(solution)/shard_map/ppermute | solution.py:38
  56.6 5.6 %reshape.84 = f32[2,2,16,2,64,2]{5,4,3,2,1,0:T(8,128)} reshape(f32[4,32,128]{2,1,0:T(8,128)S(1)} %slice_subtract_fusion.2) | data formatting | bytes 131072 | tf_op jit(solution)/shard_map/reshape | solution.py:174
  66.1 3.1 %collective-permute-start.14 = (f32[1,1,16,64]{3,2,1,0:T(8,128)S(1)}, f32[1,1,16,64]{3,2,1,0:T(8,128)S(1)}, u32[]{:S(2)}, u32[]{:S(2)}) collective-permute-start(f32[1,1,16,64]{3,2,1,0:T(8,128)S(1)} %get-tuple-element.107), channel_id=1, source_target_pairs={{0,32},{32,64},{64,96},{96,128},{128,160},{160,192},{192,224},{224... | collective-permute-start | bytes 12296 | tf_op jit(solution)/shard_map/ppermute | solution.py:21
  69.3 3.8 %collective-permute-start.17 = (f32[1,2,1,64]{3,2,1,0:T(1,128)S(1)}, f32[1,2,1,64]{3,2,1,0:T(1,128)S(1)}, u32[]{:S(2)}, u32[]{:S(2)}) collective-permute-start(f32[1,2,1,64]{3,2,1,0:T(1,128)S(1)} %get-tuple-element.110), channel_id=1, source_target_pairs={{1,0},{2,1},{3,2},{4,3},{5,4},{6,5},{7,6},{9,8},{10,9},{11,10},{12... | collective-permute-start | bytes 1544 | tf_op jit(solution)/shard_map/ppermute | solution.py:22
  75.1 4.3 %collective-permute-start.16 = (f32[1,2,16,1]{3,2,1,0:T(8,128)S(1)}, f32[1,2,16,1]{3,2,1,0:T(8,128)S(1)}, u32[]{:S(2)}, u32[]{:S(2)}) collective-permute-start(f32[1,2,16,1]{3,2,1,0:T(8,128)S(1)} %get-tuple-element.112), channel_id=1, source_target_pairs={{8,0},{16,8},{24,16},{9,1},{17,9},{25,17},{10,2},{18,10},{26,18},{... | collective-permute-start | bytes 392 | tf_op jit(solution)/shard_map/ppermute | solution.py:22
  82.1 4.6 %collective-permute-done.13 = f32[1,2,16,1]{3,2,1,0:T(8,128)S(1)} collective-permute-done((f32[1,2,16,1]{3,2,1,0:T(8,128)S(1)}, f32[1,2,16,1]{3,2,1,0:T(8,128)S(1)}, u32[]{:S(2)}, u32[]{:S(2)}) %collective-permute-start.13) | collective-permute-done | bytes 160 | tf_op jit(solution)/shard_map/ppermute | solution.py:21
  88.3 3.0 %collective-permute-start.20 = (f32[1,1,16,64]{3,2,1,0:T(8,128)S(1)}, f32[1,1,16,64]{3,2,1,0:T(8,128)S(1)}, u32[]{:S(2)}, u32[]{:S(2)}) collective-permute-start(f32[1,1,16,64]{3,2,1,0:T(8,128)S(1)} %get-tuple-element.101), channel_id=1, source_target_pairs={{0,32},{32,64},{64,96},{96,128},{128,160},{160,192},{192,224},{224... | collective-permute-start | bytes 12296 | tf_op jit(solution)/shard_map/ppermute | solution.py:21
  91.4 7.3 %collective-permute-start.23 = (f32[1,2,1,64]{3,2,1,0:T(1,128)S(1)}, f32[1,2,1,64]{3,2,1,0:T(1,128)S(1)}, u32[]{:S(2)}, u32[]{:S(2)}) collective-permute-start(f32[1,2,1,64]{3,2,1,0:T(1,128)S(1)} %get-tuple-element.104), channel_id=1, source_target_pairs={{1,0},{2,1},{3,2},{4,3},{5,4},{6,5},{7,6},{9,8},{10,9},{11,10},{12... | collective-permute-start | bytes 1544 | tf_op jit(solution)/shard_map/ppermute | solution.py:22
  100.6 3.9 %collective-permute-start.22 = (f32[1,2,16,1]{3,2,1,0:T(8,128)S(1)}, f32[1,2,16,1]{3,2,1,0:T(8,128)S(1)}, u32[]{:S(2)}, u32[]{:S(2)}) collective-permute-start(f32[1,2,16,1]{3,2,1,0:T(8,128)S(1)} %get-tuple-element.106), channel_id=1, source_target_pairs={{8,0},{16,8},{24,16},{9,1},{17,9},{25,17},{10,2},{18,10},{26,18},{... | collective-permute-start | bytes 392 | tf_op jit(solution)/shard_map/ppermute | solution.py:22
  107.3 4.6 %collective-permute-done.19 = f32[1,2,16,1]{3,2,1,0:T(8,128)S(1)} collective-permute-done((f32[1,2,16,1]{3,2,1,0:T(8,128)S(1)}, f32[1,2,16,1]{3,2,1,0:T(8,128)S(1)}, u32[]{:S(2)}, u32[]{:S(2)}) %collective-permute-start.19) | collective-permute-done | bytes 160 | tf_op jit(solution)/shard_map/ppermute | solution.py:21
  113.5 3.0 %collective-permute-start.26 = (f32[1,1,16,64]{3,2,1,0:T(8,128)S(1)}, f32[1,1,16,64]{3,2,1,0:T(8,128)S(1)}, u32[]{:S(2)}, u32[]{:S(2)}) collective-permute-start(f32[1,1,16,64]{3,2,1,0:T(8,128)S(1)} %get-tuple-element.94), channel_id=1, source_target_pairs={{0,32},{32,64},{64,96},{96,128},{128,160},{160,192},{192,224},{224... | collective-permute-start | bytes 12296 | tf_op jit(solution)/shard_map/ppermute | solution.py:21
  116.5 5.1 %collective-permute-start.29 = (f32[1,2,1,64]{3,2,1,0:T(1,128)S(1)}, f32[1,2,1,64]{3,2,1,0:T(1,128)S(1)}, u32[]{:S(2)}, u32[]{:S(2)}) collective-permute-start(f32[1,2,1,64]{3,2,1,0:T(1,128)S(1)} %get-tuple-element.97), channel_id=1, source_target_pairs={{1,0},{2,1},{3,2},{4,3},{5,4},{6,5},{7,6},{9,8},{10,9},{11,10},{12... | collective-permute-start | bytes 1544 | tf_op jit(solution)/shard_map/ppermute | solution.py:22
  121.7 3.9 %collective-permute-start.28 = (f32[1,2,16,1]{3,2,1,0:T(8,128)S(1)}, f32[1,2,16,1]{3,2,1,0:T(8,128)S(1)}, u32[]{:S(2)}, u32[]{:S(2)}) collective-permute-start(f32[1,2,16,1]{3,2,1,0:T(8,128)S(1)} %get-tuple-element.99), channel_id=1, source_target_pairs={{8,0},{16,8},{24,16},{9,1},{17,9},{25,17},{10,2},{18,10},{26,18},{... | collective-permute-start | bytes 392 | tf_op jit(solution)/shard_map/ppermute | solution.py:22
  129.4 3.8 %collective-permute-done.25 = f32[1,2,16,1]{3,2,1,0:T(8,128)S(1)} collective-permute-done((f32[1,2,16,1]{3,2,1,0:T(8,128)S(1)}, f32[1,2,16,1]{3,2,1,0:T(8,128)S(1)}, u32[]{:S(2)}, u32[]{:S(2)}) %collective-permute-start.25) | collective-permute-done | bytes 160 | tf_op jit(solution)/shard_map/ppermute | solution.py:21
  134.5 29.0 %all_to_all.5 = f32[32,1,512]{2,1,0:T(1,128)S(1)} all-to-all(f32[32,1,512]{2,1,0:T(1,128)S(1)} %reshape.87), channel_id=1, replica_groups=mesh['gx'=32,'gy'=4,'gz'=8] {'gx'}, dimensions={0} | all-to-all | bytes 131072 | tf_op jit(solution)/shard_map/all_to_all | solution.py:54
  166.7 4.2 %collective-permute-start.31 = (f32[3,32,8,4]{3,2,1,0:T(8,128)}, f32[3,32,8,4]{3,2,1,0:T(8,128)}, u32[]{:S(2)}, u32[]{:S(2)}) collective-permute-start(f32[3,32,8,4]{3,2,1,0:T(8,128)} %get-tuple-element.74), channel_id=1, source_target_pairs={{8,0},{16,8},{24,16},{9,1},{17,9},{25,17},{10,2},{18,10},{26,18},{... | collective-permute-start | bytes 36872 | tf_op jit(solution)/shard_map/ppermute | solution.py:41
  174.6 3.3 %collective-permute-done.31 = f32[3,32,8,4]{3,2,1,0:T(8,128)} collective-permute-done((f32[3,32,8,4]{3,2,1,0:T(8,128)}, f32[3,32,8,4]{3,2,1,0:T(8,128)}, u32[]{:S(2)}, u32[]{:S(2)}) %collective-permute-start.31) | collective-permute-done | bytes 12320 | tf_op jit(solution)/shard_map/ppermute | solution.py:41
  177.9 4.9 %collective-permute-done.30 = f32[3,32,8,4]{3,2,1,0:T(8,128)} collective-permute-done((f32[3,32,8,4]{3,2,1,0:T(8,128)}, f32[3,32,8,4]{3,2,1,0:T(8,128)}, u32[]{:S(2)}, u32[]{:S(2)}) %collective-permute-start.30) | collective-permute-done | bytes 12320 | tf_op jit(solution)/shard_map/ppermute | solution.py:38
  184.2 4.4 %collective-permute-start.33 = (f32[3,32,4,40]{3,2,1,0:T(4,128)S(1)}, f32[3,32,4,40]{3,2,1,0:T(4,128)S(1)}, u32[]{:S(2)}, u32[]{:S(2)}) collective-permute-start(f32[3,32,4,40]{3,2,1,0:T(4,128)S(1)} %get-tuple-element.72), channel_id=1, source_target_pairs={{1,0},{2,1},{3,2},{4,3},{5,4},{6,5},{7,6},{9,8},{10,9},{11,10},{12... | collective-permute-start | bytes 184328 | tf_op jit(solution)/shard_map/ppermute | solution.py:41
  191.8 4.4 %collective-permute-done.32 = f32[3,32,4,40]{3,2,1,0:T(4,128)S(1)} collective-permute-done((f32[3,32,4,40]{3,2,1,0:T(4,128)S(1)}, f32[3,32,4,40]{3,2,1,0:T(4,128)S(1)}, u32[]{:S(2)}, u32[]{:S(2)}) %collective-permute-start.32) | collective-permute-done | bytes 61472 | tf_op jit(solution)/shard_map/ppermute | solution.py:38
  207.4 3.4 %collective-permute-done.34 = f32[3,16,4,4]{3,2,1,0:T(4,128)S(1)} collective-permute-done((f32[3,16,4,4]{3,2,1,0:T(4,128)S(1)}, f32[3,16,4,4]{3,2,1,0:T(4,128)S(1)}, u32[]{:S(2)}, u32[]{:S(2)}) %collective-permute-start.34) | collective-permute-done | bytes 3104 | tf_op jit(solution)/shard_map/ppermute | solution.py:38
  211.0 4.9 %collective-permute-start.37 = (f32[3,16,4,24]{3,2,1,0:T(4,128)S(1)}, f32[3,16,4,24]{3,2,1,0:T(4,128)S(1)}, u32[]{:S(2)}, u32[]{:S(2)}) collective-permute-start(f32[3,16,4,24]{3,2,1,0:T(4,128)S(1)} %pad_maximum_fusion.7), channel_id=1, source_target_pairs={{1,0},{2,1},{3,2},{4,3},{5,4},{6,5},{7,6},{9,8},{10,9},{11,10},{12... | collective-permute-start | bytes 55304 | tf_op jit(solution)/shard_map/ppermute | solution.py:41
  219.7 2.7 %collective-permute-done.36 = f32[3,16,4,24]{3,2,1,0:T(4,128)S(1)} collective-permute-done((f32[3,16,4,24]{3,2,1,0:T(4,128)S(1)}, f32[3,16,4,24]{3,2,1,0:T(4,128)S(1)}, u32[]{:S(2)}, u32[]{:S(2)}) %collective-permute-start.36) | collective-permute-done | bytes 18464 | tf_op jit(solution)/shard_map/ppermute | solution.py:38
  (147 shorter events, 72.1 us)
Async XLA Ops:
  1.6 20.7 %collective-permute-start.1 = (f32[4,4,32,128]{3,2,1,0:T(8,128)S(1)}, f32[4,4,32,128]{3,2,1,0:T(8,128)S(1)}, u32[]{:S(2)}, u32[]{:S(2)}) collective-permute-start(f32[4,4,32,128]{3,2,1,0:T(8,128)S(1)} %pad_maximum_fusion.5), channel_id=1, source_target_pairs={{32,0},{64,32},{96,64},{128,96},{160,128},{192,160},{224,192},{256... | collective-permute-start | bytes 786440 | tf_op jit(solution)/shard_map/ppermute | solution.py:41
  2.9 19.4 %collective-permute-start = (f32[4,4,32,128]{3,2,1,0:T(8,128)S(1)}, f32[4,4,32,128]{3,2,1,0:T(8,128)S(1)}, u32[]{:S(2)}, u32[]{:S(2)}) collective-permute-start(f32[4,4,32,128]{3,2,1,0:T(8,128)S(1)} %pad_maximum_fusion.5), channel_id=1, source_target_pairs={{0,32},{32,64},{64,96},{96,128},{128,160},{160,192},{192,224},{224... | collective-permute-start | bytes 786440 | tf_op jit(solution)/shard_map/ppermute | solution.py:38
  14.9 28.3 %collective-permute-start.11 = (f32[1,2,1,64]{3,2,1,0:T(1,128)S(1)}, f32[1,2,1,64]{3,2,1,0:T(1,128)S(1)}, u32[]{:S(2)}, u32[]{:S(2)}) collective-permute-start(f32[1,2,1,64]{3,2,1,0:T(1,128)S(1)} %get-tuple-element.116), channel_id=1, source_target_pairs={{1,0},{2,1},{3,2},{4,3},{5,4},{6,5},{7,6},{9,8},{10,9},{11,10},{12... | collective-permute-start | bytes 1544 | tf_op jit(solution)/shard_map/ppermute | solution.py:22
  18.2 19.5 %collective-permute-start.10 = (f32[1,2,16,1]{3,2,1,0:T(8,128)S(1)}, f32[1,2,16,1]{3,2,1,0:T(8,128)S(1)}, u32[]{:S(2)}, u32[]{:S(2)}) collective-permute-start(f32[1,2,16,1]{3,2,1,0:T(8,128)S(1)} %get-tuple-element.118), channel_id=1, source_target_pairs={{8,0},{16,8},{24,16},{9,1},{17,9},{25,17},{10,2},{18,10},{26,18},{... | collective-permute-start | bytes 392 | tf_op jit(solution)/shard_map/ppermute | solution.py:22
  20.9 19.9 %collective-permute-start.7 = (f32[1,2,16,1]{3,2,1,0:T(8,128)S(1)}, f32[1,2,16,1]{3,2,1,0:T(8,128)S(1)}, u32[]{:S(2)}, u32[]{:S(2)}) collective-permute-start(f32[1,2,16,1]{3,2,1,0:T(8,128)S(1)} %get-tuple-element.117), channel_id=1, source_target_pairs={{0,8},{8,16},{16,24},{1,9},{9,17},{17,25},{2,10},{10,18},{18,26},{... | collective-permute-start | bytes 392 | tf_op jit(solution)/shard_map/ppermute | solution.py:21
  23.0 7.6 %collective-permute-start.3 = (f32[4,12,32,4]{2,3,1,0:T(4,128)S(1)}, f32[4,12,32,4]{2,3,1,0:T(4,128)S(1)}, u32[]{:S(2)}, u32[]{:S(2)}) collective-permute-start(f32[4,12,32,4]{2,3,1,0:T(4,128)S(1)} %copy.20), channel_id=1, source_target_pairs={{8,0},{16,8},{24,16},{9,1},{17,9},{25,17},{10,2},{18,10},{26,18},{... | collective-permute-start | bytes 73736 | tf_op jit(solution)/shard_map/ppermute | solution.py:41
  27.9 7.5 %collective-permute-start.2 = (f32[4,12,32,4]{2,3,1,0:T(4,128)S(1)}, f32[4,12,32,4]{2,3,1,0:T(4,128)S(1)}, u32[]{:S(2)}, u32[]{:S(2)}) collective-permute-start(f32[4,12,32,4]{2,3,1,0:T(4,128)S(1)} %copy.19), channel_id=1, source_target_pairs={{0,8},{8,16},{16,24},{1,9},{9,17},{17,25},{2,10},{10,18},{18,26},{... | collective-permute-start | bytes 73736 | tf_op jit(solution)/shard_map/ppermute | solution.py:38
  30.6 16.2 %collective-permute-start.6 = (f32[1,2,1,64]{3,2,1,0:T(1,128)S(1)}, f32[1,2,1,64]{3,2,1,0:T(1,128)S(1)}, u32[]{:S(2)}, u32[]{:S(2)}) collective-permute-start(f32[1,2,1,64]{3,2,1,0:T(1,128)S(1)} %get-tuple-element.115), channel_id=1, source_target_pairs={{0,1},{1,2},{2,3},{3,4},{4,5},{5,6},{6,7},{8,9},{9,10},{10,11},{11... | collective-permute-start | bytes 1544 | tf_op jit(solution)/shard_map/ppermute | solution.py:21
  35.4 11.4 %collective-permute-start.9 = (f32[1,1,16,64]{3,2,1,0:T(8,128)S(1)}, f32[1,1,16,64]{3,2,1,0:T(8,128)S(1)}, u32[]{:S(2)}, u32[]{:S(2)}) collective-permute-start(f32[1,1,16,64]{3,2,1,0:T(8,128)S(1)} %get-tuple-element.114), channel_id=1, source_target_pairs={{32,0},{64,32},{96,64},{128,96},{160,128},{192,160},{224,192},{256... | collective-permute-start | bytes 12296 | tf_op jit(solution)/shard_map/ppermute | solution.py:22
  37.7 9.0 %collective-permute-start.8 = (f32[1,1,16,64]{3,2,1,0:T(8,128)S(1)}, f32[1,1,16,64]{3,2,1,0:T(8,128)S(1)}, u32[]{:S(2)}, u32[]{:S(2)}) collective-permute-start(f32[1,1,16,64]{3,2,1,0:T(8,128)S(1)} %get-tuple-element.113), channel_id=1, source_target_pairs={{0,32},{32,64},{64,96},{96,128},{128,160},{160,192},{192,224},{224... | collective-permute-start | bytes 12296 | tf_op jit(solution)/shard_map/ppermute | solution.py:21
  40.8 8.6 %collective-permute-start.5 = (f32[4,12,4,136]{3,2,1,0:T(4,128)S(1)}, f32[4,12,4,136]{3,2,1,0:T(4,128)S(1)}, u32[]{:S(2)}, u32[]{:S(2)}) collective-permute-start(f32[4,12,4,136]{3,2,1,0:T(4,128)S(1)} %get-tuple-element.62), channel_id=1, source_target_pairs={{1,0},{2,1},{3,2},{4,3},{5,4},{6,5},{7,6},{9,8},{10,9},{11,10},{12... | collective-permute-start | bytes 313352 | tf_op jit(solution)/shard_map/ppermute | solution.py:41
  43.2 8.9 %collective-permute-start.4 = (f32[4,12,4,136]{3,2,1,0:T(4,128)S(1)}, f32[4,12,4,136]{3,2,1,0:T(4,128)S(1)}, u32[]{:S(2)}, u32[]{:S(2)}) collective-permute-start(f32[4,12,4,136]{3,2,1,0:T(4,128)S(1)} %get-tuple-element.61), channel_id=1, source_target_pairs={{0,1},{1,2},{2,3},{3,4},{4,5},{5,6},{6,7},{8,9},{9,10},{10,11},{11... | collective-permute-start | bytes 313352 | tf_op jit(solution)/shard_map/ppermute | solution.py:38
  64.8 21.9 %collective-permute-start.15 = (f32[1,1,16,64]{3,2,1,0:T(8,128)S(1)}, f32[1,1,16,64]{3,2,1,0:T(8,128)S(1)}, u32[]{:S(2)}, u32[]{:S(2)}) collective-permute-start(f32[1,1,16,64]{3,2,1,0:T(8,128)S(1)} %get-tuple-element.108), channel_id=1, source_target_pairs={{32,0},{64,32},{96,64},{128,96},{160,128},{192,160},{224,192},{256... | collective-permute-start | bytes 12296 | tf_op jit(solution)/shard_map/ppermute | solution.py:22
  66.1 20.6 %collective-permute-start.14 = (f32[1,1,16,64]{3,2,1,0:T(8,128)S(1)}, f32[1,1,16,64]{3,2,1,0:T(8,128)S(1)}, u32[]{:S(2)}, u32[]{:S(2)}) collective-permute-start(f32[1,1,16,64]{3,2,1,0:T(8,128)S(1)} %get-tuple-element.107), channel_id=1, source_target_pairs={{0,32},{32,64},{64,96},{96,128},{128,160},{160,192},{192,224},{224... | collective-permute-start | bytes 12296 | tf_op jit(solution)/shard_map/ppermute | solution.py:21
  69.3 17.5 %collective-permute-start.17 = (f32[1,2,1,64]{3,2,1,0:T(1,128)S(1)}, f32[1,2,1,64]{3,2,1,0:T(1,128)S(1)}, u32[]{:S(2)}, u32[]{:S(2)}) collective-permute-start(f32[1,2,1,64]{3,2,1,0:T(1,128)S(1)} %get-tuple-element.110), channel_id=1, source_target_pairs={{1,0},{2,1},{3,2},{4,3},{5,4},{6,5},{7,6},{9,8},{10,9},{11,10},{12... | collective-permute-start | bytes 1544 | tf_op jit(solution)/shard_map/ppermute | solution.py:22
  73.1 13.7 %collective-permute-start.12 = (f32[1,2,1,64]{3,2,1,0:T(1,128)S(1)}, f32[1,2,1,64]{3,2,1,0:T(1,128)S(1)}, u32[]{:S(2)}, u32[]{:S(2)}) collective-permute-start(f32[1,2,1,64]{3,2,1,0:T(1,128)S(1)} %get-tuple-element.109), channel_id=1, source_target_pairs={{0,1},{1,2},{2,3},{3,4},{4,5},{5,6},{6,7},{8,9},{9,10},{10,11},{11... | collective-permute-start | bytes 1544 | tf_op jit(solution)/shard_map/ppermute | solution.py:21
  80.8 5.9 %collective-permute-start.13 = (f32[1,2,16,1]{3,2,1,0:T(8,128)S(1)}, f32[1,2,16,1]{3,2,1,0:T(8,128)S(1)}, u32[]{:S(2)}, u32[]{:S(2)}) collective-permute-start(f32[1,2,16,1]{3,2,1,0:T(8,128)S(1)} %get-tuple-element.111), channel_id=1, source_target_pairs={{0,8},{8,16},{16,24},{1,9},{9,17},{17,25},{2,10},{10,18},{18,26},{... | collective-permute-start | bytes 392 | tf_op jit(solution)/shard_map/ppermute | solution.py:21
  87.0 24.8 %collective-permute-start.21 = (f32[1,1,16,64]{3,2,1,0:T(8,128)S(1)}, f32[1,1,16,64]{3,2,1,0:T(8,128)S(1)}, u32[]{:S(2)}, u32[]{:S(2)}) collective-permute-start(f32[1,1,16,64]{3,2,1,0:T(8,128)S(1)} %get-tuple-element.102), channel_id=1, source_target_pairs={{32,0},{64,32},{96,64},{128,96},{160,128},{192,160},{224,192},{256... | collective-permute-start | bytes 12296 | tf_op jit(solution)/shard_map/ppermute | solution.py:22
  88.3 23.6 %collective-permute-start.20 = (f32[1,1,16,64]{3,2,1,0:T(8,128)S(1)}, f32[1,1,16,64]{3,2,1,0:T(8,128)S(1)}, u32[]{:S(2)}, u32[]{:S(2)}) collective-permute-start(f32[1,1,16,64]{3,2,1,0:T(8,128)S(1)} %get-tuple-element.101), channel_id=1, source_target_pairs={{0,32},{32,64},{64,96},{96,128},{128,160},{160,192},{192,224},{224... | collective-permute-start | bytes 12296 | tf_op jit(solution)/shard_map/ppermute | solution.py:21
  91.4 20.5 %collective-permute-start.23 = (f32[1,2,1,64]{3,2,1,0:T(1,128)S(1)}, f32[1,2,1,64]{3,2,1,0:T(1,128)S(1)}, u32[]{:S(2)}, u32[]{:S(2)}) collective-permute-start(f32[1,2,1,64]{3,2,1,0:T(1,128)S(1)} %get-tuple-element.104), channel_id=1, source_target_pairs={{1,0},{2,1},{3,2},{4,3},{5,4},{6,5},{7,6},{9,8},{10,9},{11,10},{12... | collective-permute-start | bytes 1544 | tf_op jit(solution)/shard_map/ppermute | solution.py:22
  98.7 13.2 %collective-permute-start.18 = (f32[1,2,1,64]{3,2,1,0:T(1,128)S(1)}, f32[1,2,1,64]{3,2,1,0:T(1,128)S(1)}, u32[]{:S(2)}, u32[]{:S(2)}) collective-permute-start(f32[1,2,1,64]{3,2,1,0:T(1,128)S(1)} %get-tuple-element.103), channel_id=1, source_target_pairs={{0,1},{1,2},{2,3},{3,4},{4,5},{5,6},{6,7},{8,9},{9,10},{10,11},{11... | collective-permute-start | bytes 1544 | tf_op jit(solution)/shard_map/ppermute | solution.py:21
  112.2 21.0 %collective-permute-start.27 = (f32[1,1,16,64]{3,2,1,0:T(8,128)S(1)}, f32[1,1,16,64]{3,2,1,0:T(8,128)S(1)}, u32[]{:S(2)}, u32[]{:S(2)}) collective-permute-start(f32[1,1,16,64]{3,2,1,0:T(8,128)S(1)} %get-tuple-element.95), channel_id=1, source_target_pairs={{32,0},{64,32},{96,64},{128,96},{160,128},{192,160},{224,192},{256... | collective-permute-start | bytes 12296 | tf_op jit(solution)/shard_map/ppermute | solution.py:22
  113.5 19.7 %collective-permute-start.26 = (f32[1,1,16,64]{3,2,1,0:T(8,128)S(1)}, f32[1,1,16,64]{3,2,1,0:T(8,128)S(1)}, u32[]{:S(2)}, u32[]{:S(2)}) collective-permute-start(f32[1,1,16,64]{3,2,1,0:T(8,128)S(1)} %get-tuple-element.94), channel_id=1, source_target_pairs={{0,32},{32,64},{64,96},{96,128},{128,160},{160,192},{192,224},{224... | collective-permute-start | bytes 12296 | tf_op jit(solution)/shard_map/ppermute | solution.py:21
  116.5 16.6 %collective-permute-start.29 = (f32[1,2,1,64]{3,2,1,0:T(1,128)S(1)}, f32[1,2,1,64]{3,2,1,0:T(1,128)S(1)}, u32[]{:S(2)}, u32[]{:S(2)}) collective-permute-start(f32[1,2,1,64]{3,2,1,0:T(1,128)S(1)} %get-tuple-element.97), channel_id=1, source_target_pairs={{1,0},{2,1},{3,2},{4,3},{5,4},{6,5},{7,6},{9,8},{10,9},{11,10},{12... | collective-permute-start | bytes 1544 | tf_op jit(solution)/shard_map/ppermute | solution.py:22
  125.6 7.6 %collective-permute-start.24 = (f32[1,2,1,64]{3,2,1,0:T(1,128)S(1)}, f32[1,2,1,64]{3,2,1,0:T(1,128)S(1)}, u32[]{:S(2)}, u32[]{:S(2)}) collective-permute-start(f32[1,2,1,64]{3,2,1,0:T(1,128)S(1)} %get-tuple-element.96), channel_id=1, source_target_pairs={{0,1},{1,2},{2,3},{3,4},{4,5},{5,6},{6,7},{8,9},{9,10},{10,11},{11... | collective-permute-start | bytes 1544 | tf_op jit(solution)/shard_map/ppermute | solution.py:21
  166.7 11.2 %collective-permute-start.31 = (f32[3,32,8,4]{3,2,1,0:T(8,128)}, f32[3,32,8,4]{3,2,1,0:T(8,128)}, u32[]{:S(2)}, u32[]{:S(2)}) collective-permute-start(f32[3,32,8,4]{3,2,1,0:T(8,128)} %get-tuple-element.74), channel_id=1, source_target_pairs={{8,0},{16,8},{24,16},{9,1},{17,9},{25,17},{10,2},{18,10},{26,18},{... | collective-permute-start | bytes 36872 | tf_op jit(solution)/shard_map/ppermute | solution.py:41
  170.9 11.8 %collective-permute-start.30 = (f32[3,32,8,4]{3,2,1,0:T(8,128)}, f32[3,32,8,4]{3,2,1,0:T(8,128)}, u32[]{:S(2)}, u32[]{:S(2)}) collective-permute-start(f32[3,32,8,4]{3,2,1,0:T(8,128)} %get-tuple-element.73), channel_id=1, source_target_pairs={{0,8},{8,16},{16,24},{1,9},{9,17},{17,25},{2,10},{10,18},{18,26},{... | collective-permute-start | bytes 36872 | tf_op jit(solution)/shard_map/ppermute | solution.py:38
  184.2 7.6 %collective-permute-start.33 = (f32[3,32,4,40]{3,2,1,0:T(4,128)S(1)}, f32[3,32,4,40]{3,2,1,0:T(4,128)S(1)}, u32[]{:S(2)}, u32[]{:S(2)}) collective-permute-start(f32[3,32,4,40]{3,2,1,0:T(4,128)S(1)} %get-tuple-element.72), channel_id=1, source_target_pairs={{1,0},{2,1},{3,2},{4,3},{5,4},{6,5},{7,6},{9,8},{10,9},{11,10},{12... | collective-permute-start | bytes 184328 | tf_op jit(solution)/shard_map/ppermute | solution.py:41
  188.6 7.6 %collective-permute-start.32 = (f32[3,32,4,40]{3,2,1,0:T(4,128)S(1)}, f32[3,32,4,40]{3,2,1,0:T(4,128)S(1)}, u32[]{:S(2)}, u32[]{:S(2)}) collective-permute-start(f32[3,32,4,40]{3,2,1,0:T(4,128)S(1)} %get-tuple-element.71), channel_id=1, source_target_pairs={{0,1},{1,2},{2,3},{3,4},{4,5},{5,6},{6,7},{8,9},{9,10},{10,11},{11... | collective-permute-start | bytes 184328 | tf_op jit(solution)/shard_map/ppermute | solution.py:38
  204.3 6.5 %collective-permute-start.34 = (f32[3,16,4,4]{3,2,1,0:T(4,128)S(1)}, f32[3,16,4,4]{3,2,1,0:T(4,128)S(1)}, u32[]{:S(2)}, u32[]{:S(2)}) collective-permute-start(f32[3,16,4,4]{3,2,1,0:T(4,128)S(1)} %get-tuple-element.90), channel_id=1, source_target_pairs={{0,8},{8,16},{16,24},{1,9},{9,17},{17,25},{2,10},{10,18},{18,26},{... | collective-permute-start | bytes 9224 | tf_op jit(solution)/shard_map/ppermute | solution.py:38
  211.0 8.7 %collective-permute-start.37 = (f32[3,16,4,24]{3,2,1,0:T(4,128)S(1)}, f32[3,16,4,24]{3,2,1,0:T(4,128)S(1)}, u32[]{:S(2)}, u32[]{:S(2)}) collective-permute-start(f32[3,16,4,24]{3,2,1,0:T(4,128)S(1)} %pad_maximum_fusion.7), channel_id=1, source_target_pairs={{1,0},{2,1},{3,2},{4,3},{5,4},{6,5},{7,6},{9,8},{10,9},{11,10},{12... | collective-permute-start | bytes 55304 | tf_op jit(solution)/shard_map/ppermute | solution.py:41
  215.9 6.5 %collective-permute-start.36 = (f32[3,16,4,24]{3,2,1,0:T(4,128)S(1)}, f32[3,16,4,24]{3,2,1,0:T(4,128)S(1)}, u32[]{:S(2)}, u32[]{:S(2)}) collective-permute-start(f32[3,16,4,24]{3,2,1,0:T(4,128)S(1)} %pad_maximum_fusion.7), channel_id=1, source_target_pairs={{0,1},{1,2},{2,3},{3,4},{4,5},{5,6},{6,7},{8,9},{9,10},{10,11},{11... | collective-permute-start | bytes 55304 | tf_op jit(solution)/shard_map/ppermute | solution.py:38
  (14 other events, 67.3 us)
where the time goes:
time: 227 us; the launch traced here: 225 us
  starting transfers between devices  103 us (45%)
  waiting for transfers between devices  43.8 us (19%)
  blocking collectives  29 us (13%)
  other arithmetic  25.8 us (11%)
  local copies, waits for them, and re-layouts  22.1 us (10%)
    ppermute x12, starting transfers between devices, padded_2(): lax.ppermute(leading, axis, [(b, a) for a, b in up])  39.5 us
    all_to_all x1, blocking collectives, copy_for_each(): lax.all_to_all(jnp.broadcast_to(shard[None], (peers, *shard.shape)), axis...  29 us
    ppermute x12, starting transfers between devices, padded_2(): lax.ppermute(last, axis, up)  25.9 us
    ppermute x7, starting transfers between devices, with_halo(): lax.ppermute(lax.slice_in_dim(block, 0, width, axis=dim), axis, backward)  23.4 us
    ppermute x7, waiting for transfers between devices, with_halo(): lax.ppermute(lax.slice_in_dim(block, block.shape[dim] - width, None, axis...  20 us
    ppermute x7, starting transfers between devices, with_halo(): lax.ppermute(lax.slice_in_dim(block, block.shape[dim] - width, None, axis...  14.2 us
    ppermute x12, waiting for transfers between devices, padded_2(): lax.ppermute(last, axis, up)  13 us
    reshape x3, local copies, waits for them, and re-layouts, coarse_sum(): blocks = field.reshape(first // 2, 2, second // 2, 2, third // 2, 2)  13 us
  transfers between devices with their start and end apart: 38, of which 15 were waited for; matrix products, arithmetic and copies ran while one was open for 8% of the time, Pallas kernels for 0%

commit v1 on v0

v1 whole, which is shorter than its diff:
```python
import jax
import jax.numpy as jnp
from jax import lax
from jax.sharding import PartitionSpec as P

SWEEPS = 3

lower_bound = 0.25
upper_bound = 2.0

NEAR = 4
ROWS = 24
COLUMNS = 32


def steps(axis, by):
    count = lax.axis_size(axis)
    forward = [(i, i + by) for i in range(count - by)]
    return forward, [(b, a) for a, b in forward]


def with_halo(block, sides, width):
    for axis, dim in sides:
        forward, backward = steps(axis, 1)
        low = lax.ppermute(
            lax.slice_in_dim(block, block.shape[dim] - width, None, axis=dim), axis, forward
        )
        high = lax.ppermute(lax.slice_in_dim(block, 0, width, axis=dim), axis, backward)
        block = jnp.concatenate([low, block, high], axis=dim)
    return block


def copy_for_each(shard, axis):
    peers = lax.axis_size(axis)
    return lax.all_to_all(
        jnp.broadcast_to(shard[None], (peers, *shard.shape)), axis, 0, 0, tiled=True
    )


def gathered(shard, axis):
    peers = lax.axis_size(axis)
    inner = 4 if peers % 4 == 0 else 1
    outer = peers // inner
    apart = [[i + inner * j for j in range(outer)] for i in range(inner)]
    beside = [[inner * j + i for i in range(inner)] for j in range(outer)]
    for groups in (apart, beside):
        shard = lax.all_to_all(
            jnp.broadcast_to(shard[None], (len(groups[0]), *shard.shape)),
            axis,
            0,
            0,
            axis_index_groups=groups,
            tiled=True,
        )
    return jnp.moveaxis(shard, 0, 1).reshape(peers, *shard.shape[2:])


def inside_mask(shape, sides):
    inside = None
    for axis, dim, own in sides:
        halo = (shape[dim] - own) // 2
        position = lax.axis_index(axis) * own - halo + lax.broadcasted_iota(jnp.int32, shape, dim)
        good = (position >= 0) & (position < lax.axis_size(axis) * own)
        inside = good if inside is None else inside & good
    return inside


def neighbours(padded):
    return [
        padded[:-2, 1:-1, 1:-1],
        padded[2:, 1:-1, 1:-1],
        padded[1:-1, :-2, 1:-1],
        padded[1:-1, 2:, 1:-1],
        padded[1:-1, 1:-1, :-2],
        padded[1:-1, 1:-1, 2:],
    ]


def operate(field, weights, diagonal):
    others = neighbours(jnp.pad(field, 1))
    result = diagonal * field
    for face_index in range(6):
        result = result - weights[face_index] * others[face_index]
    return result


def smooth(source, start, conduct, inside):
    theta = 0.5 * (upper_bound + lower_bound)
    delta = 0.5 * (upper_bound - lower_bound)
    sigma = theta / delta
    others = neighbours(jnp.pad(conduct, 1))
    weights = [0.5 * (conduct + other) for other in others]
    diagonal = weights[0] + weights[1] + weights[2] + weights[3] + weights[4] + weights[5]
    safe_diagonal = jnp.where(inside, diagonal, 1.0)
    if start is None:
        solution = jnp.zeros_like(source)
        residual = source
    else:
        solution = start
        residual = source - operate(solution, weights, diagonal)
    direction = jnp.where(inside, residual / (theta * safe_diagonal), 0.0)
    ratio_now = 1.0 / sigma
    for sweep_index in range(SWEEPS):
        solution = solution + direction
        residual = residual - operate(direction, weights, diagonal)
        if sweep_index + 1 < SWEEPS:
            ratio_next = 1.0 / (2.0 * sigma - ratio_now)
            direction = jnp.where(
                inside,
                ratio_next * ratio_now * direction
                + 2.0 * ratio_next / delta * residual / safe_diagonal,
                0.0,
            )
            ratio_now = ratio_next
    return solution, residual


def pairs(size):
    row = lax.broadcasted_iota(jnp.int32, (size, size // 2), 0)
    column = lax.broadcasted_iota(jnp.int32, (size, size // 2), 1)
    return (row // 2 == column).astype(jnp.float32)


def coarse_sum(field):
    first, second, third = field.shape
    planes = field.reshape(first // 2, 2, second, third)
    planes = planes[:, 0] + planes[:, 1]
    planes = jnp.einsum("xzy,yb->xzb", planes, pairs(third), precision=lax.Precision.HIGHEST)
    return jnp.einsum("xzb,za->xab", planes, pairs(second), precision=lax.Precision.HIGHEST)


def shards(conductivity, initial_guess, right_side):
    grown = with_halo(
        jnp.stack([conductivity, right_side, initial_guess]),
        (("gx", 1), ("gy", 3), ("gz", 2)),
        NEAR,
    )
    inside = inside_mask(
        grown.shape[1:],
        (
            ("gx", 0, conductivity.shape[0]),
            ("gz", 1, conductivity.shape[1]),
            ("gy", 2, conductivity.shape[2]),
        ),
    )
    fine, residual_zero = smooth(grown[1], grown[2], grown[0], inside)
    own = (slice(NEAR, -NEAR),) * 3
    fine_solution = fine[own]

    source = 0.25 * coarse_sum(residual_zero[own])
    conduct = 0.125 * coarse_sum(conductivity)
    planes, rows, columns = source.shape
    packed = jnp.concatenate([source, conduct], axis=2)
    everyone = copy_for_each(packed, "gz")
    everyone = jnp.moveaxis(everyone, 0, 1).reshape(planes, -1, 2 * columns)
    everyone = jnp.pad(everyone, ((0, 0), (ROWS, ROWS), (0, 0)))
    packed = lax.dynamic_slice_in_dim(
        everyone, lax.axis_index("gz") * rows, rows + 2 * ROWS, axis=1
    )
    both = jnp.stack([packed[..., :columns], packed[..., columns:]])
    both = with_halo(both, (("gy", 3),), COLUMNS)
    parts = {0: both}
    for by in (1, 2):
        forward, backward = steps("gx", by)
        parts[-by] = lax.ppermute(both, "gx", forward)
        parts[by] = lax.ppermute(both, "gx", backward)
    both = jnp.concatenate([parts[by] for by in sorted(parts)], axis=1)
    inside = inside_mask(
        both.shape[1:], (("gx", 0, planes), ("gz", 1, rows), ("gy", 2, columns))
    )
    level_one, residual_one = smooth(both[0], None, both[1], inside)
    level_one_solution = level_one[
        2 * planes : -2 * planes, ROWS:-ROWS, COLUMNS:-COLUMNS
    ]

    source = 0.25 * coarse_sum(residual_one[2 * planes : -2 * planes])
    conduct = 0.125 * coarse_sum(both[1, 2 * planes : -2 * planes])
    width = source.shape[2]
    packed = gathered(jnp.concatenate([source, conduct], axis=2)[0], "gx")
    source, conduct = packed[..., :width], packed[..., width:]
    rows, columns = rows // 2, columns // 2
    inside = inside_mask(source.shape, (("gz", 1, rows), ("gy", 2, columns)))
    level_two, residual_two = smooth(source, None, conduct, inside)
    level_two_solution = level_two[:, ROWS // 2 : -ROWS // 2, COLUMNS // 2 : -COLUMNS // 2]

    source = 0.25 * coarse_sum(residual_two)
    conduct = 0.125 * coarse_sum(conduct)
    rows, columns = rows // 2, columns // 2
    inside = inside_mask(source.shape, (("gz", 1, rows), ("gy", 2, columns)))
    level_three, residual_three = smooth(source, None, conduct, inside)
    own = (slice(None), slice(ROWS // 4, -ROWS // 4), slice(COLUMNS // 4, -COLUMNS // 4))
    return (
        fine_solution,
        level_one_solution,
        level_two_solution,
        level_three[own],
        residual_three[own],
    )


def solution(mesh):
    placed = (P("gx", "gz", "gy"), P("gx", "gz", "gy"), P("gx", "gz", "gy"))
    return jax.shard_map(
        shards,
        mesh=mesh,
        in_specs=placed,
        out_specs=(
            P("gx", "gz", "gy"),
            P("gx", "gz", "gy"),
            P(None, "gz", "gy"),
            P(None, "gz", "gy"),
            P(None, "gz", "gy"),
        ),
        check_vma=False,
    )
```

time: 227 us -> 139 us (0.61)
  the two profiles are of different devices: /device:TPU:46 before, /device:TPU:1 now
where the time goes in v1:
time: 139 us; the launch traced here: 137 us
  starting transfers between devices  57.5 us (41%)
  blocking collectives  28.8 us (21%)
  waiting for transfers between devices  27.4 us (20%)
  other arithmetic  15.8 us (11%)
  local copies, waits for them, and re-layouts  3.4 us (2%)
  matrix products  2.96 us (2%)
    all_to_all x1, blocking collectives, gathered(): lax.all_to_all(jnp.broadcast_to(shard[None], (len(groups[0]), *shard.shap...  28.8 us
    ppermute x4, starting transfers between devices, with_halo(): lax.ppermute(lax.slice_in_dim(block, 0, width, axis=dim), axis, backward)  19.9 us
    ppermute x4, starting transfers between devices, with_halo(): lax.ppermute(lax.slice_in_dim(block, block.shape[dim] - width, None, axis...  14.3 us
    ppermute x2, starting transfers between devices, shards(): parts[-by] = lax.ppermute(both, 'gx', forward)  9.85 us
    all_to_all x1, waiting for transfers between devices, copy_for_each(): lax.all_to_all(jnp.broadcast_to(shard[None], (peers, *shard.shape)), axis...  7.91 us
    all_to_all x1, waiting for transfers between devices, gathered(): lax.all_to_all(jnp.broadcast_to(shard[None], (len(groups[0]), *shard.shap...  6.79 us
    all_to_all x1, starting transfers between devices, gathered(): lax.all_to_all(jnp.broadcast_to(shard[None], (len(groups[0]), *shard.shap...  6.71 us
    ppermute x4, waiting for transfers between devices, with_halo(): lax.ppermute(lax.slice_in_dim(block, block.shape[dim] - width, None, axis...  5.46 us
  transfers between devices with their start and end apart: 14, of which 10 were waited for; matrix products, arithmetic and copies ran while one was open for 2% of the time, Pallas kernels for 0%

profile of v1, /device:TPU:1, one launch (start us, length us, event | category | flops | bytes accessed | tf_op | source)
XLA Modules:
  0.0 137.0 jit_solution(15172338066234324460)
XLA Ops:
  0.6 0.9 pad_maximum_fusion.2
  1.6 16.0 %collective-permute-start.1 = (f32[3,4,32,128]{3,2,1,0:T(8,128)S(1)}, f32[3,4,32,128]{3,2,1,0:T(8,128)S(1)}, u32[]{:S(2)}, u32[]{:S(2)}) collective-permute-start(f32[3,4,32,128]{3,2,1,0:T(8,128)S(1)} %pad_maximum_fusion.2), channel_id=1, source_target_pairs={{32,0},{64,32},{96,64},{128,96},{160,128},{192,160},{224,192},{256... | collective-permute-start | bytes 589832 | tf_op jit(solution)/shard_map/ppermute | solution.py:28
  17.6 1.9 %collective-permute-start = (f32[3,4,32,128]{3,2,1,0:T(8,128)S(1)}, f32[3,4,32,128]{3,2,1,0:T(8,128)S(1)}, u32[]{:S(2)}, u32[]{:S(2)}) collective-permute-start(f32[3,4,32,128]{3,2,1,0:T(8,128)S(1)} %pad_maximum_fusion.2), channel_id=1, source_target_pairs={{0,32},{32,64},{64,96},{96,128},{128,160},{160,192},{192,224},{224... | collective-permute-start | bytes 589832 | tf_op jit(solution)/shard_map/ppermute | solution.py:25
  19.6 0.9 fusion.230
  20.7 1.4 %collective-permute-done = f32[3,4,32,128]{3,2,1,0:T(8,128)S(1)} collective-permute-done((f32[3,4,32,128]{3,2,1,0:T(8,128)S(1)}, f32[3,4,32,128]{3,2,1,0:T(8,128)S(1)}, u32[]{:S(2)}, u32[]{:S(2)}) %collective-permute-start) | collective-permute-done | bytes 196640 | tf_op jit(solution)/shard_map/ppermute | solution.py:25
  22.1 0.9 pad_maximum_fusion.1
  23.6 1.3 collective-permute-start.3
  25.2 4.0 %collective-permute-start.2 = (f32[3,12,32,4]{2,3,1,0:T(4,128)S(1)}, f32[3,12,32,4]{2,3,1,0:T(4,128)S(1)}, u32[]{:S(2)}, u32[]{:S(2)}) collective-permute-start(f32[3,12,32,4]{2,3,1,0:T(4,128)S(1)} %copy.40), channel_id=1, source_target_pairs={{0,8},{8,16},{16,24},{1,9},{9,17},{17,25},{2,10},{10,18},{18,26},{... | collective-permute-start | bytes 55304 | tf_op jit(solution)/shard_map/ppermute | solution.py:25
  29.5 1.7 %collective-permute-done.2 = f32[3,12,32,4]{2,3,1,0:T(4,128)S(1)} collective-permute-done((f32[3,12,32,4]{2,3,1,0:T(4,128)S(1)}, f32[3,12,32,4]{2,3,1,0:T(4,128)S(1)}, u32[]{:S(2)}, u32[]{:S(2)}) %collective-permute-start.2) | collective-permute-done | bytes 18464 | tf_op jit(solution)/shard_map/ppermute | solution.py:25
  31.8 1.3 collective-permute-start.5
  33.1 4.0 %collective-permute-start.4 = (f32[3,12,4,136]{3,2,1,0:T(4,128)S(1)}, f32[3,12,4,136]{3,2,1,0:T(4,128)S(1)}, u32[]{:S(2)}, u32[]{:S(2)}) collective-permute-start(f32[3,12,4,136]{3,2,1,0:T(4,128)S(1)} %get-tuple-element.64), channel_id=1, source_target_pairs={{0,1},{1,2},{2,3},{3,4},{4,5},{5,6},{6,7},{8,9},{9,10},{10,11},{11... | collective-permute-start | bytes 235016 | tf_op jit(solution)/shard_map/ppermute | solution.py:25
  37.1 1.8 %collective-permute-done.5 = f32[3,12,4,136]{3,2,1,0:T(4,128)S(1)} collective-permute-done((f32[3,12,4,136]{3,2,1,0:T(4,128)S(1)}, f32[3,12,4,136]{3,2,1,0:T(4,128)S(1)}, u32[]{:S(2)}, u32[]{:S(2)}) %collective-permute-start.5) | collective-permute-done | bytes 78368 | tf_op jit(solution)/shard_map/ppermute | solution.py:28
  38.9 0.9 collective-permute-done.4
  40.5 1.1 divide_select_fusion
  43.6 1.0 slice_subtract_fusion.2
  45.6 3.5 %all-to-all-start = ((f32[8,2,16,128]{3,2,1,0:T(8,128)}), f32[8,2,16,128]{3,2,1,0:T(8,128)S(1)}, u32[]{:S(2)}, u32[]{:S(2)}) async-start(f32[8,2,16,128]{3,2,1,0:T(8,128)} %broadcast_in_dim.57), calls=%async_computation | async-start | bytes 262144 | tf_op jit(solution)/shard_map/all_to_all | solution.py:35
  49.1 7.9 %all-to-all-done = f32[8,2,16,128]{3,2,1,0:T(8,128)S(1)} async-done(((f32[8,2,16,128]{3,2,1,0:T(8,128)}), f32[8,2,16,128]{3,2,1,0:T(8,128)S(1)}, u32[]{:S(2)}, u32[]{:S(2)}) %all-to-all-start) | async-done | bytes 131104 | tf_op jit(solution)/shard_map/all_to_all | solution.py:35
  57.3 1.3 collective-permute-start.7
  58.6 4.4 %collective-permute-start.6 = (f32[2,2,64,32]{3,2,1,0:T(8,128)S(1)}, f32[2,2,64,32]{3,2,1,0:T(8,128)S(1)}, u32[]{:S(2)}, u32[]{:S(2)}) collective-permute-start(f32[2,2,64,32]{3,2,1,0:T(8,128)S(1)} %get-tuple-element.88), channel_id=1, source_target_pairs={{0,8},{8,16},{16,24},{1,9},{9,17},{17,25},{2,10},{10,18},{18,26},{... | collective-permute-start | bytes 98312 | tf_op jit(solution)/shard_map/ppermute | solution.py:25
  63.4 1.5 %collective-permute-done.6 = f32[2,2,64,32]{3,2,1,0:T(8,128)S(1)} collective-permute-done((f32[2,2,64,32]{3,2,1,0:T(8,128)S(1)}, f32[2,2,64,32]{3,2,1,0:T(8,128)S(1)}, u32[]{:S(2)}, u32[]{:S(2)}) %collective-permute-start.6) | collective-permute-done | bytes 32800 | tf_op jit(solution)/shard_map/ppermute | solution.py:25
  65.0 1.3 collective-permute-start.8
  66.3 8.5 %collective-permute-start.9 = (f32[2,2,64,128]{3,2,1,0:T(8,128)S(1)}, f32[2,2,64,128]{3,2,1,0:T(8,128)S(1)}, u32[]{:S(2)}, u32[]{:S(2)}) collective-permute-start(f32[2,2,64,128]{3,2,1,0:T(8,128)S(1)} %maximum_maximum_fusion), channel_id=1, source_target_pairs={{0,32},{32,64},{64,96},{96,128},{128,160},{160,192},{192,224},{224... | collective-permute-start | bytes 393224 | tf_op jit(solution)/shard_map/ppermute | solution.py:165
  74.9 1.9 %collective-permute-start.10 = (f32[2,2,64,128]{3,2,1,0:T(8,128)S(1)}, f32[2,2,64,128]{3,2,1,0:T(8,128)S(1)}, u32[]{:S(2)}, u32[]{:S(2)}) collective-permute-start(f32[2,2,64,128]{3,2,1,0:T(8,128)S(1)} %maximum_maximum_fusion), channel_id=1, source_target_pairs={{32,0},{64,32},{96,64},{128,96},{160,128},{192,160},{224,192},{256... | collective-permute-start | bytes 393224 | tf_op jit(solution)/shard_map/ppermute | solution.py:166
  76.8 1.3 collective-permute-start.11
  78.6 2.6 %collective-permute-done.10 = f32[2,2,64,128]{3,2,1,0:T(8,128)S(1)} collective-permute-done((f32[2,2,64,128]{3,2,1,0:T(8,128)S(1)}, f32[2,2,64,128]{3,2,1,0:T(8,128)S(1)}, u32[]{:S(2)}, u32[]{:S(2)}) %collective-permute-start.10) | collective-permute-done | bytes 131104 | tf_op jit(solution)/shard_map/ppermute | solution.py:166
  81.2 2.5 %collective-permute-done.11 = f32[2,2,64,128]{3,2,1,0:T(8,128)S(1)} collective-permute-done((f32[2,2,64,128]{3,2,1,0:T(8,128)S(1)}, f32[2,2,64,128]{3,2,1,0:T(8,128)S(1)}, u32[]{:S(2)}, u32[]{:S(2)}) %collective-permute-start.11) | collective-permute-done | bytes 131104 | tf_op jit(solution)/shard_map/ppermute | solution.py:166
  86.0 28.8 %all_to_all.15 = f32[8,32,128]{2,1,0:T(8,128)S(1)} all-to-all(f32[8,32,128]{2,1,0:T(8,128)S(1)} %broadcast_in_dim.61), channel_id=1, replica_groups={{0,128,256,384,512,640,768,896},{32,160,288,416,544,672,800,928},{64,19..., dimensions={0} | all-to-all | bytes 262144 | tf_op jit(solution)/shard_map/all_to_all | solution.py:47
  114.8 0.8 broadcast_in_dim.62
  115.7 6.7 %all-to-all-start.2 = ((f32[4,8,32,128]{3,2,1,0:T(8,128)}), f32[4,8,32,128]{3,2,1,0:T(8,128)S(1)}, u32[]{:S(2)}, u32[]{:S(2)}) async-start(f32[4,8,32,128]{3,2,1,0:T(8,128)} %broadcast_in_dim.62), calls=%async_computation.2 | async-start | bytes 1048576 | tf_op jit(solution)/shard_map/all_to_all | solution.py:47
  123.1 6.8 %all-to-all-done.2 = f32[4,8,32,128]{3,2,1,0:T(8,128)S(1)} async-done(((f32[4,8,32,128]{3,2,1,0:T(8,128)}), f32[4,8,32,128]{3,2,1,0:T(8,128)S(1)}, u32[]{:S(2)}, u32[]{:S(2)}) %all-to-all-start.2) | async-done | bytes 524320 | tf_op jit(solution)/shard_map/all_to_all | solution.py:47
  132.4 0.8 slice_add_fusion
  136.2 0.9 slice_subtract_fusion.4
  (79 shorter events, 15.2 us)
Async XLA Ops:
  1.6 19.2 %collective-permute-start.1 = (f32[3,4,32,128]{3,2,1,0:T(8,128)S(1)}, f32[3,4,32,128]{3,2,1,0:T(8,128)S(1)}, u32[]{:S(2)}, u32[]{:S(2)}) collective-permute-start(f32[3,4,32,128]{3,2,1,0:T(8,128)S(1)} %pad_maximum_fusion.2), channel_id=1, source_target_pairs={{32,0},{64,32},{96,64},{128,96},{160,128},{192,160},{224,192},{256... | collective-permute-start | bytes 589832 | tf_op jit(solution)/shard_map/ppermute | solution.py:28
  17.6 4.5 %collective-permute-start = (f32[3,4,32,128]{3,2,1,0:T(8,128)S(1)}, f32[3,4,32,128]{3,2,1,0:T(8,128)S(1)}, u32[]{:S(2)}, u32[]{:S(2)}) collective-permute-start(f32[3,4,32,128]{3,2,1,0:T(8,128)S(1)} %pad_maximum_fusion.2), channel_id=1, source_target_pairs={{0,32},{32,64},{64,96},{96,128},{128,160},{160,192},{192,224},{224... | collective-permute-start | bytes 589832 | tf_op jit(solution)/shard_map/ppermute | solution.py:25
  23.3 8.2 %copy-start = (f32[4,32,128]{2,1,0:T(8,128)S(1)}, f32[4,32,128]{2,1,0:T(8,128)}, u32[]{:S(2)}) copy-start(f32[4,32,128]{2,1,0:T(8,128)} %param.3) | copy-start | bytes 196612
  23.3 8.2 %copy-start.1 = (f32[4,32,128]{2,1,0:T(8,128)S(1)}, f32[4,32,128]{2,1,0:T(8,128)}, u32[]{:S(2)}) copy-start(f32[4,32,128]{2,1,0:T(8,128)} %param.4) | copy-start | bytes 196612
  23.3 8.2 %copy-start.2 = (f32[4,32,128]{2,1,0:T(8,128)S(1)}, f32[4,32,128]{2,1,0:T(8,128)}, u32[]{:S(2)}) copy-start(f32[4,32,128]{2,1,0:T(8,128)} %param.5) | copy-start | bytes 196612
  23.6 5.6 %collective-permute-start.3 = (f32[3,12,32,4]{2,3,1,0:T(4,128)S(1)}, f32[3,12,32,4]{2,3,1,0:T(4,128)S(1)}, u32[]{:S(2)}, u32[]{:S(2)}) collective-permute-start(f32[3,12,32,4]{2,3,1,0:T(4,128)S(1)} %copy.41), channel_id=1, source_target_pairs={{8,0},{16,8},{24,16},{9,1},{17,9},{25,17},{10,2},{18,10},{26,18},{... | collective-permute-start | bytes 55304 | tf_op jit(solution)/shard_map/ppermute | solution.py:28
  25.2 6.0 %collective-permute-start.2 = (f32[3,12,32,4]{2,3,1,0:T(4,128)S(1)}, f32[3,12,32,4]{2,3,1,0:T(4,128)S(1)}, u32[]{:S(2)}, u32[]{:S(2)}) collective-permute-start(f32[3,12,32,4]{2,3,1,0:T(4,128)S(1)} %copy.40), channel_id=1, source_target_pairs={{0,8},{8,16},{16,24},{1,9},{9,17},{17,25},{2,10},{10,18},{18,26},{... | collective-permute-start | bytes 55304 | tf_op jit(solution)/shard_map/ppermute | solution.py:25
  31.8 7.1 %collective-permute-start.5 = (f32[3,12,4,136]{3,2,1,0:T(4,128)S(1)}, f32[3,12,4,136]{3,2,1,0:T(4,128)S(1)}, u32[]{:S(2)}, u32[]{:S(2)}) collective-permute-start(f32[3,12,4,136]{3,2,1,0:T(4,128)S(1)} %get-tuple-element.65), channel_id=1, source_target_pairs={{1,0},{2,1},{3,2},{4,3},{5,4},{6,5},{7,6},{9,8},{10,9},{11,10},{12... | collective-permute-start | bytes 235016 | tf_op jit(solution)/shard_map/ppermute | solution.py:28
  33.1 6.7 %collective-permute-start.4 = (f32[3,12,4,136]{3,2,1,0:T(4,128)S(1)}, f32[3,12,4,136]{3,2,1,0:T(4,128)S(1)}, u32[]{:S(2)}, u32[]{:S(2)}) collective-permute-start(f32[3,12,4,136]{3,2,1,0:T(4,128)S(1)} %get-tuple-element.64), channel_id=1, source_target_pairs={{0,1},{1,2},{2,3},{3,4},{4,5},{5,6},{6,7},{8,9},{9,10},{10,11},{11... | collective-permute-start | bytes 235016 | tf_op jit(solution)/shard_map/ppermute | solution.py:25
  45.6 11.4 %all-to-all-start = ((f32[8,2,16,128]{3,2,1,0:T(8,128)}), f32[8,2,16,128]{3,2,1,0:T(8,128)S(1)}, u32[]{:S(2)}, u32[]{:S(2)}) async-start(f32[8,2,16,128]{3,2,1,0:T(8,128)} %broadcast_in_dim.57), calls=%async_computation | async-start | bytes 262144 | tf_op jit(solution)/shard_map/all_to_all | solution.py:35
  57.3 6.1 %collective-permute-start.7 = (f32[2,2,64,32]{3,2,1,0:T(8,128)S(1)}, f32[2,2,64,32]{3,2,1,0:T(8,128)S(1)}, u32[]{:S(2)}, u32[]{:S(2)}) collective-permute-start(f32[2,2,64,32]{3,2,1,0:T(8,128)S(1)} %get-tuple-element.89), channel_id=1, source_target_pairs={{8,0},{16,8},{24,16},{9,1},{17,9},{25,17},{10,2},{18,10},{26,18},{... | collective-permute-start | bytes 98312 | tf_op jit(solution)/shard_map/ppermute | solution.py:28
  58.6 6.3 %collective-permute-start.6 = (f32[2,2,64,32]{3,2,1,0:T(8,128)S(1)}, f32[2,2,64,32]{3,2,1,0:T(8,128)S(1)}, u32[]{:S(2)}, u32[]{:S(2)}) collective-permute-start(f32[2,2,64,32]{3,2,1,0:T(8,128)S(1)} %get-tuple-element.88), channel_id=1, source_target_pairs={{0,8},{8,16},{16,24},{1,9},{9,17},{17,25},{2,10},{10,18},{18,26},{... | collective-permute-start | bytes 98312 | tf_op jit(solution)/shard_map/ppermute | solution.py:25
  65.0 13.4 %collective-permute-start.8 = (f32[2,2,64,128]{3,2,1,0:T(8,128)S(1)}, f32[2,2,64,128]{3,2,1,0:T(8,128)S(1)}, u32[]{:S(2)}, u32[]{:S(2)}) collective-permute-start(f32[2,2,64,128]{3,2,1,0:T(8,128)S(1)} %maximum_maximum_fusion), channel_id=1, source_target_pairs={{0,64},{32,96},{64,128},{96,160},{128,192},{160,224},{192,256},{22... | collective-permute-start | bytes 393224 | tf_op jit(solution)/shard_map/ppermute | solution.py:165
  66.3 12.1 %collective-permute-start.9 = (f32[2,2,64,128]{3,2,1,0:T(8,128)S(1)}, f32[2,2,64,128]{3,2,1,0:T(8,128)S(1)}, u32[]{:S(2)}, u32[]{:S(2)}) collective-permute-start(f32[2,2,64,128]{3,2,1,0:T(8,128)S(1)} %maximum_maximum_fusion), channel_id=1, source_target_pairs={{0,32},{32,64},{64,96},{96,128},{128,160},{160,192},{192,224},{224... | collective-permute-start | bytes 393224 | tf_op jit(solution)/shard_map/ppermute | solution.py:165
  74.9 6.3 %collective-permute-start.10 = (f32[2,2,64,128]{3,2,1,0:T(8,128)S(1)}, f32[2,2,64,128]{3,2,1,0:T(8,128)S(1)}, u32[]{:S(2)}, u32[]{:S(2)}) collective-permute-start(f32[2,2,64,128]{3,2,1,0:T(8,128)S(1)} %maximum_maximum_fusion), channel_id=1, source_target_pairs={{32,0},{64,32},{96,64},{128,96},{160,128},{192,160},{224,192},{256... | collective-permute-start | bytes 393224 | tf_op jit(solution)/shard_map/ppermute | solution.py:166
  76.8 6.9 %collective-permute-start.11 = (f32[2,2,64,128]{3,2,1,0:T(8,128)S(1)}, f32[2,2,64,128]{3,2,1,0:T(8,128)S(1)}, u32[]{:S(2)}, u32[]{:S(2)}) collective-permute-start(f32[2,2,64,128]{3,2,1,0:T(8,128)S(1)} %maximum_maximum_fusion), channel_id=1, source_target_pairs={{64,0},{96,32},{128,64},{160,96},{192,128},{224,160},{256,192},{28... | collective-permute-start | bytes 393224 | tf_op jit(solution)/shard_map/ppermute | solution.py:166
  115.7 14.2 %all-to-all-start.2 = ((f32[4,8,32,128]{3,2,1,0:T(8,128)}), f32[4,8,32,128]{3,2,1,0:T(8,128)S(1)}, u32[]{:S(2)}, u32[]{:S(2)}) async-start(f32[4,8,32,128]{3,2,1,0:T(8,128)} %broadcast_in_dim.62), calls=%async_computation.2 | async-start | bytes 1048576 | tf_op jit(solution)/shard_map/all_to_all | solution.py:47

commit v2 on v1

--- a/solution.py
+++ b/solution.py
@@ -1,6 +1,8 @@
 import jax
 import jax.numpy as jnp
 from jax import lax
+from jax.experimental import pallas as pl
+from jax.experimental.pallas import tpu as pltpu
 from jax.sharding import PartitionSpec as P
 
 SWEEPS = 3
@@ -52,7 +54,7 @@
             axis_index_groups=groups,
             tiled=True,
         )
-    return jnp.moveaxis(shard, 0, 1).reshape(peers, *shard.shape[2:])
+    return shard
 
 
 def inside_mask(shape, sides):
@@ -115,6 +117,240 @@
     return solution, residual
 
 
+THETA = 0.5 * (upper_bound + lower_bound)
+DELTA = 0.5 * (upper_bound - lower_bound)
+
+
+def mixes():
+    sigma = THETA / DELTA
+    ratio_now = 1.0 / sigma
+    for _ in range(SWEEPS - 1):
+        ratio_next = 1.0 / (2.0 * sigma - ratio_now)
+        yield ratio_next * ratio_now, 2.0 * ratio_next / DELTA
+        ratio_now = ratio_next
+
+
+def after(plane, dim):
+    return pltpu.roll(plane, plane.shape[dim] - 1, dim)
+
+
+def before(plane, dim):
+    return pltpu.roll(plane, 1, dim)
+
+
+def set_faces(p, c, wx_low, wx_high, wz, wy, inv):
+    face_z = 0.5 * (c + after(c, 0))
+    face_y = 0.5 * (c + after(c, 1))
+    wz[p] = face_z
+    wy[p] = face_y
+    diagonal = (
+        (wx_low + wx_high) + (face_z + before(face_z, 0)) + (face_y + before(face_y, 1))
+    )
+    inside = c > 0.0
+    inverse = jnp.where(inside, 1.0 / jnp.where(inside, diagonal, 1.0), 0.0)
+    inv[p] = inverse
+    return inverse
+
+
+def gained(p, here, flow_low, flow_high, wz, wy):
+    flow_z = wz[p] * (after(here, 0) - here)
+    flow_y = wy[p] * (after(here, 1) - here)
+    return (
+        (flow_high - flow_low)
+        + (flow_z - before(flow_z, 0))
+        + (flow_y - before(flow_y, 1))
+    )
+
+
+def pairing(shift):
+    row = lax.broadcasted_iota(jnp.int32, (128, 128), 0)
+    column = lax.broadcasted_iota(jnp.int32, (128, 128), 1)
+    return jnp.where((row >> 1) + shift == column, 1.0, 0.0)
+
+
+def paired(left, right):
+    return jnp.dot(
+        left, right, precision=lax.Precision.HIGHEST, preferred_element_type=jnp.float32
+    )
+
+
+def level_one_kernel(
+    far_low, low, own, high, far_high, solution_ref, packed_ref, d, r, wx, wz, wy, inv, both
+):
+    parts = (far_low, low, own, high, far_high)
+    planes = own.shape[1]
+    total = planes * len(parts)
+    first = 2 * planes
+    last = first + planes
+
+    def conduct(p):
+        return parts[p // planes][1, p % planes]
+
+    def flow(p):
+        return wx[p] * (d[p + 1] - d[p])
+
+    reach = SWEEPS
+    for p in range(first - reach - 1, last + reach):
+        wx[p] = 0.5 * (conduct(p) + conduct(p + 1))
+    for p in range(first - reach, last + reach):
+        inverse = set_faces(p, conduct(p), wx[p - 1], wx[p], wz, wy, inv)
+        source = parts[p // planes][0, p % planes]
+        r[p] = source
+        d[p] = source * inverse * (1.0 / THETA)
+    answers = [d[p] for p in range(first, last)]
+    mix = list(mixes())
+    for sweep in range(SWEEPS):
+        reach -= 1
+        flow_low = flow(first - reach - 1)
+        for p in range(first - reach, last + reach):
+            flow_high = flow(p)
+            here = d[p]
+            residual = r[p] + gained(p, here, flow_low, flow_high, wz, wy)
+            r[p] = residual
+            flow_low = flow_high
+            if sweep + 1 < SWEEPS:
+                here = mix[sweep][0] * here + mix[sweep][1] * (residual * inv[p])
+                d[p] = here
+                if first <= p < last:
+                    answers[p - first] = answers[p - first] + here
+    rows, columns = solution_ref.shape[1:]
+    for p in range(planes):
+        answer = answers[p][ROWS : ROWS + rows]
+        solution_ref[p] = pltpu.roll(answer, 128 - COLUMNS, 1)[:, :columns]
+    tall = d.shape[1]
+    both[:tall] = 0.25 * (r[first] + r[first + 1])
+    both[tall:] = 0.125 * (conduct(first) + conduct(first + 1))
+    halved = both[pl.ds(0, tall, stride=2)] + both[pl.ds(1, tall, stride=2)]
+    packed_ref[...] = paired(halved[: tall // 2], pairing(0)) + paired(
+        halved[tall // 2 :], pairing(64)
+    )
+
+
+def smooth_folded(half, c, r, d, s, wx, wz, wy, inv):
+    count = c.shape[0]
+    lane = lax.broadcasted_iota(jnp.int32, c.shape[1:], 1)
+
+    def ahead(plane):
+        return jnp.where(lane < half, pltpu.roll(plane, 128 - half, 1), 0.0)
+
+    def behind(plane):
+        return jnp.where((lane >= half) & (lane < 2 * half), pltpu.roll(plane, half, 1), 0.0)
+
+    wx[0] = 0.5 * (behind(c[count - 1]) + c[0])
+    for p in range(count):
+        there = c[p + 1] if p + 1 < count else ahead(c[0])
+        wx[p + 1] = 0.5 * (c[p] + there)
+    for p in range(count):
+        inverse = set_faces(p, c[p], wx[p], wx[p + 1], wz, wy, inv)
+        direction = r[p] * inverse * (1.0 / THETA)
+        d[p] = direction
+        s[p] = direction
+    mix = list(mixes())
+    for sweep in range(SWEEPS):
+        beyond = ahead(d[0])
+        flow_low = wx[0] * (d[0] - behind(d[count - 1]))
+        for p in range(count):
+            here = d[p]
+            there = d[p + 1] if p + 1 < count else beyond
+            flow_high = wx[p + 1] * (there - here)
+            residual = r[p] + gained(p, here, flow_low, flow_high, wz, wy)
+            r[p] = residual
+            flow_low = flow_high
+            if sweep + 1 < SWEEPS:
+                here = mix[sweep][0] * here + mix[sweep][1] * (residual * inv[p])
+                d[p] = here
+                s[p] = s[p] + here
+
+
+def unfold(planes, half, row, column, out_ref):
+    count = planes.shape[0]
+    rows, columns = out_ref.shape[1:]
+    for p in range(count):
+        answer = planes[p][row : row + rows]
+        out_ref[p] = pltpu.roll(answer, 128 - column, 1)[:, :columns]
+        out_ref[p + count] = pltpu.roll(answer, 128 - half - column, 1)[:, :columns]
+
+
+def coarse_kernel(
+    gathered_ref,
+    two_ref,
+    three_ref,
+    residual_ref,
+    c, r, d, s, wx, wz, wy, inv, both,
+    c3, r3, d3, s3, wx3, wz3, wy3, inv3,
+):
+    inner = gathered_ref.shape[0]
+    count = c.shape[0]
+    lane = lax.broadcasted_iota(jnp.int32, c.shape[1:], 1)
+    for p in range(count):
+        front = gathered_ref[p % inner, p // inner]
+        back = gathered_ref[(p + count) % inner, (p + count) // inner]
+        r[p] = jnp.where(lane < 64, front, pltpu.roll(back, 64, 1))
+        c[p] = jnp.where(lane < 64, pltpu.roll(front, 64, 1), back)
+    smooth_folded(64, c, r, d, s, wx, wz, wy, inv)
+    unfold(s, 64, ROWS // 2, COLUMNS // 2, two_ref)
+    tall = c.shape[1]
+    half = count // 2
+    for p in range(half):
+        both[p * tall : (p + 1) * tall] = 0.25 * (r[2 * p] + r[2 * p + 1])
+        both[(half + p) * tall : (half + p + 1) * tall] = 0.125 * (c[2 * p] + c[2 * p + 1])
+    length = half * tall
+    halved = both[pl.ds(0, length, stride=2)] + both[pl.ds(1, length, stride=2)]
+    coarse = paired(halved, pairing(0))
+    low = tall // 2
+    for p in range(half):
+        r3[p] = coarse[p * low : (p + 1) * low]
+        c3[p] = coarse[(half + p) * low : (half + p + 1) * low]
+    smooth_folded(32, c3, r3, d3, s3, wx3, wz3, wy3, inv3)
+    unfold(s3, 32, ROWS // 4, COLUMNS // 4, three_ref)
+    unfold(r3, 32, ROWS // 4, COLUMNS // 4, residual_ref)
+
+
+def f32(*shape):
+    return jax.ShapeDtypeStruct(shape, jnp.float32)
+
+
+def in_vmem(count):
+    return [pl.BlockSpec(memory_space=pltpu.VMEM)] * count
+
+
+def level_one_call(parts, rows, columns):
+    _, planes, tall, wide = parts[0].shape
+    total = planes * len(parts)
+    return pl.pallas_call(
+        level_one_kernel,
+        out_shape=(f32(planes, rows, columns), f32(tall // 2, wide)),
+        in_specs=in_vmem(5),
+        out_specs=tuple(in_vmem(2)),
+        scratch_shapes=[pltpu.VMEM((total, tall, wide), jnp.float32)] * 6
+        + [pltpu.VMEM((2 * tall, wide), jnp.float32)],
+    )(*parts)
+
+
+def coarse_call(everyone, rows, columns):
+    inner, outer, tall, wide = everyone.shape
+    count = inner * outer // 2
+
+    def scratch(planes, height):
+        field = pltpu.VMEM((planes, height, wide), jnp.float32)
+        faces = pltpu.VMEM((planes + 1, height, wide), jnp.float32)
+        return [field] * 4 + [faces] + [field] * 3
+
+    return pl.pallas_call(
+        coarse_kernel,
+        out_shape=(
+            f32(2 * count, rows, columns),
+            f32(count, rows // 2, columns // 2),
+            f32(count, rows // 2, columns // 2),
+        ),
+        in_specs=in_vmem(1),
+        out_specs=tuple(in_vmem(3)),
+        scratch_shapes=scratch(count, tall)
+        + [pltpu.VMEM((count * tall, wide), jnp.float32)]
+        + scratch(count // 2, tall // 2),
+    )(everyone)
+
+
 def pairs(size):
     row = lax.broadcasted_iota(jnp.int32, (size, size // 2), 0)
     column = lax.broadcasted_iota(jnp.int32, (size, size // 2), 1)
@@ -164,37 +400,19 @@
         forward, backward = steps("gx", by)
         parts[-by] = lax.ppermute(both, "gx", forward)
         parts[by] = lax.ppermute(both, "gx", backward)
-    both = jnp.concatenate([parts[by] for by in sorted(parts)], axis=1)
-    inside = inside_mask(
-        both.shape[1:], (("gx", 0, planes), ("gz", 1, rows), ("gy", 2, columns))
-    )
-    level_one, residual_one = smooth(both[0], None, both[1], inside)
-    level_one_solution = level_one[
-        2 * planes : -2 * planes, ROWS:-ROWS, COLUMNS:-COLUMNS
-    ]
-
-    source = 0.25 * coarse_sum(residual_one[2 * planes : -2 * planes])
-    conduct = 0.125 * coarse_sum(both[1, 2 * planes : -2 * planes])
-    width = source.shape[2]
-    packed = gathered(jnp.concatenate([source, conduct], axis=2)[0], "gx")
-    source, conduct = packed[..., :width], packed[..., width:]
-    rows, columns = rows // 2, columns // 2
-    inside = inside_mask(source.shape, (("gz", 1, rows), ("gy", 2, columns)))
-    level_two, residual_two = smooth(source, None, conduct, inside)
-    level_two_solution = level_two[:, ROWS // 2 : -ROWS // 2, COLUMNS // 2 : -COLUMNS // 2]
-
-    source = 0.25 * coarse_sum(residual_two)
-    conduct = 0.125 * coarse_sum(conduct)
-    rows, columns = rows // 2, columns // 2
-    inside = inside_mask(source.shape, (("gz", 1, rows), ("gy", 2, columns)))
-    level_three, residual_three = smooth(source, None, conduct, inside)
-    own = (slice(None), slice(ROWS // 4, -ROWS // 4), slice(COLUMNS // 4, -COLUMNS // 4))
+    level_one_solution, packed = level_one_call(
+        [parts[by] for by in sorted(parts)], rows, columns
+    )
+    everyone = gathered(packed, "gx")
+    level_two_solution, level_three_solution, level_three_residual = coarse_call(
+        everyone, rows // 2, columns // 2
+    )
     return (
         fine_solution,
         level_one_solution,
         level_two_solution,
-        level_three[own],
-        residual_three[own],
+        level_three_solution,
+        level_three_residual,
     )
 
 

time: 139 us -> 138 us (level)
  other arithmetic: 15.8 us -> 7.29 us
  Pallas kernels: 0 us -> 6.35 us
  local copies, waits for them, and re-layouts: 3.4 us -> 5.28 us
  matrix products: 2.96 us -> 1.37 us
    pallas_call x0 -> x2, Pallas kernels: none -> 6.35 us  [the longest x1 3.6 us: coarse_call(): pl.pallas_call(coarse_kernel, out_shape=(f32(2 * count, rows, columns), f...]
    select_n x8 -> x2, other arithmetic: 4.41 us -> 1.53 us  [smooth(): jnp.where(inside, ratio_next * ratio_now * direction + 2.0 * ratio_next /...]
    sub x3 -> x1, other arithmetic: 2.51 us -> 0.32 us  [smooth(): residual = residual - operate(direction, weights, diagonal)]
    add x3 -> x1, other arithmetic: 2.25 us -> 0.77 us  [smooth(): solution = solution + direction]
    unnamed x11 -> x20, local copies, waits for them, and re-layouts: 0.62 us -> 2.04 us
where the time goes in v2:
time: 138 us; the launch traced here: 136 us
  starting transfers between devices  57.4 us (42%)
  blocking collectives  28.8 us (21%)
  waiting for transfers between devices  28.2 us (20%)
  other arithmetic  7.29 us (5%)
  Pallas kernels  6.35 us (5%)
  local copies, waits for them, and re-layouts  5.28 us (4%)
    all_to_all x1, blocking collectives, gathered(): lax.all_to_all(jnp.broadcast_to(shard[None], (len(groups[0]), *shard.shap...  28.8 us
    ppermute x4, starting transfers between devices, with_halo(): lax.ppermute(lax.slice_in_dim(block, 0, width, axis=dim), axis, backward)  19.9 us
    ppermute x4, starting transfers between devices, with_halo(): lax.ppermute(lax.slice_in_dim(block, block.shape[dim] - width, None, axis...  14.2 us
    ppermute x2, starting transfers between devices, shards(): parts[-by] = lax.ppermute(both, 'gx', forward)  9.94 us
    all_to_all x1, waiting for transfers between devices, copy_for_each(): lax.all_to_all(jnp.broadcast_to(shard[None], (peers, *shard.shape)), axis...  7.96 us
    all_to_all x1, waiting for transfers between devices, gathered(): lax.all_to_all(jnp.broadcast_to(shard[None], (len(groups[0]), *shard.shap...  6.92 us
    all_to_all x1, starting transfers between devices, gathered(): lax.all_to_all(jnp.broadcast_to(shard[None], (len(groups[0]), *shard.shap...  6.71 us
    ppermute x2, waiting for transfers between devices, shards(): parts[by] = lax.ppermute(both, 'gx', backward)  5.59 us
  transfers between devices with their start and end apart: 14, of which 10 were waited for; matrix products, arithmetic and copies ran while one was open for 2% of the time, Pallas kernels for 0%

profile of v2, /device:TPU:1, one launch (start us, length us, event | category | flops | bytes accessed | tf_op | source)
XLA Modules:
  0.0 135.7 jit_solution(506193808319946786)
XLA Ops:
  0.6 0.9 pad_maximum_fusion.2
  1.6 16.0 %collective-permute-start.1 = (f32[3,4,32,128]{3,2,1,0:T(8,128)S(1)}, f32[3,4,32,128]{3,2,1,0:T(8,128)S(1)}, u32[]{:S(2)}, u32[]{:S(2)}) collective-permute-start(f32[3,4,32,128]{3,2,1,0:T(8,128)S(1)} %pad_maximum_fusion.2), channel_id=1, source_target_pairs={{32,0},{64,32},{96,64},{128,96},{160,128},{192,160},{224,192},{256... | collective-permute-start | bytes 589832 | tf_op jit(solution)/shard_map/ppermute | solution.py:30
  17.6 1.9 %collective-permute-start = (f32[3,4,32,128]{3,2,1,0:T(8,128)S(1)}, f32[3,4,32,128]{3,2,1,0:T(8,128)S(1)}, u32[]{:S(2)}, u32[]{:S(2)}) collective-permute-start(f32[3,4,32,128]{3,2,1,0:T(8,128)S(1)} %pad_maximum_fusion.2), channel_id=1, source_target_pairs={{0,32},{32,64},{64,96},{96,128},{128,160},{160,192},{192,224},{224... | collective-permute-start | bytes 589832 | tf_op jit(solution)/shard_map/ppermute | solution.py:27
  19.6 0.9 fusion.65
  20.7 1.4 %collective-permute-done = f32[3,4,32,128]{3,2,1,0:T(8,128)S(1)} collective-permute-done((f32[3,4,32,128]{3,2,1,0:T(8,128)S(1)}, f32[3,4,32,128]{3,2,1,0:T(8,128)S(1)}, u32[]{:S(2)}, u32[]{:S(2)}) %collective-permute-start) | collective-permute-done | bytes 196640 | tf_op jit(solution)/shard_map/ppermute | solution.py:27
  22.1 0.9 pad_maximum_fusion.1
  23.6 1.3 collective-permute-start.3
  25.2 4.0 %collective-permute-start.2 = (f32[3,12,32,4]{2,3,1,0:T(4,128)S(1)}, f32[3,12,32,4]{2,3,1,0:T(4,128)S(1)}, u32[]{:S(2)}, u32[]{:S(2)}) collective-permute-start(f32[3,12,32,4]{2,3,1,0:T(4,128)S(1)} %copy.22), channel_id=1, source_target_pairs={{0,8},{8,16},{16,24},{1,9},{9,17},{17,25},{2,10},{10,18},{18,26},{... | collective-permute-start | bytes 55304 | tf_op jit(solution)/shard_map/ppermute | solution.py:27
  29.5 1.7 %collective-permute-done.2 = f32[3,12,32,4]{2,3,1,0:T(4,128)S(1)} collective-permute-done((f32[3,12,32,4]{2,3,1,0:T(4,128)S(1)}, f32[3,12,32,4]{2,3,1,0:T(4,128)S(1)}, u32[]{:S(2)}, u32[]{:S(2)}) %collective-permute-start.2) | collective-permute-done | bytes 18464 | tf_op jit(solution)/shard_map/ppermute | solution.py:27
  31.8 1.3 collective-permute-start.5
  33.1 4.0 %collective-permute-start.4 = (f32[3,12,4,136]{3,2,1,0:T(4,128)S(1)}, f32[3,12,4,136]{3,2,1,0:T(4,128)S(1)}, u32[]{:S(2)}, u32[]{:S(2)}) collective-permute-start(f32[3,12,4,136]{3,2,1,0:T(4,128)S(1)} %get-tuple-element.33), channel_id=1, source_target_pairs={{0,1},{1,2},{2,3},{3,4},{4,5},{5,6},{6,7},{8,9},{9,10},{10,11},{11... | collective-permute-start | bytes 235016 | tf_op jit(solution)/shard_map/ppermute | solution.py:27
  37.1 1.8 %collective-permute-done.5 = f32[3,12,4,136]{3,2,1,0:T(4,128)S(1)} collective-permute-done((f32[3,12,4,136]{3,2,1,0:T(4,128)S(1)}, f32[3,12,4,136]{3,2,1,0:T(4,128)S(1)}, u32[]{:S(2)}, u32[]{:S(2)}) %collective-permute-start.5) | collective-permute-done | bytes 78368 | tf_op jit(solution)/shard_map/ppermute | solution.py:30
  38.9 0.9 collective-permute-done.4
  40.5 1.0 divide_select_fusion
  42.3 0.8 add_select_fusion
  45.0 3.5 %all-to-all-start = ((f32[8,2,16,128]{3,2,1,0:T(8,128)}), f32[8,2,16,128]{3,2,1,0:T(8,128)S(1)}, u32[]{:S(2)}, u32[]{:S(2)}) async-start(f32[8,2,16,128]{3,2,1,0:T(8,128)} %broadcast_in_dim.29), calls=%async_computation | async-start | bytes 262144 | tf_op jit(solution)/shard_map/all_to_all | solution.py:37
  48.5 8.0 %all-to-all-done = f32[8,2,16,128]{3,2,1,0:T(8,128)S(1)} async-done(((f32[8,2,16,128]{3,2,1,0:T(8,128)}), f32[8,2,16,128]{3,2,1,0:T(8,128)S(1)}, u32[]{:S(2)}, u32[]{:S(2)}) %all-to-all-start) | async-done | bytes 131104 | tf_op jit(solution)/shard_map/all_to_all | solution.py:37
  56.6 1.3 collective-permute-start.7
  57.9 4.3 %collective-permute-start.6 = (f32[2,2,64,32]{3,2,1,0:T(8,128)S(1)}, f32[2,2,64,32]{3,2,1,0:T(8,128)S(1)}, u32[]{:S(2)}, u32[]{:S(2)}) collective-permute-start(f32[2,2,64,32]{3,2,1,0:T(8,128)S(1)} %get-tuple-element.45), channel_id=1, source_target_pairs={{0,8},{8,16},{16,24},{1,9},{9,17},{17,25},{2,10},{10,18},{18,26},{... | collective-permute-start | bytes 98312 | tf_op jit(solution)/shard_map/ppermute | solution.py:27
  62.6 1.5 %collective-permute-done.6 = f32[2,2,64,32]{3,2,1,0:T(8,128)S(1)} collective-permute-done((f32[2,2,64,32]{3,2,1,0:T(8,128)S(1)}, f32[2,2,64,32]{3,2,1,0:T(8,128)S(1)}, u32[]{:S(2)}, u32[]{:S(2)}) %collective-permute-start.6) | collective-permute-done | bytes 32800 | tf_op jit(solution)/shard_map/ppermute | solution.py:27
  64.3 1.3 collective-permute-start.8
  65.6 8.6 %collective-permute-start.9 = (f32[2,2,64,128]{3,2,1,0:T(8,128)S(1)}, f32[2,2,64,128]{3,2,1,0:T(8,128)S(1)}, u32[]{:S(2)}, u32[]{:S(2)}) collective-permute-start(f32[2,2,64,128]{3,2,1,0:T(8,128)S(1)} %pad_maximum_fusion.11.own), channel_id=1, source_target_pairs={{0,32},{32,64},{64,96},{96,128},{128,160},{160,192},{192,224},{224... | collective-permute-start | bytes 393224 | tf_op jit(solution)/shard_map/ppermute | solution.py:401
  74.2 1.9 %collective-permute-start.10 = (f32[2,2,64,128]{3,2,1,0:T(8,128)S(1)}, f32[2,2,64,128]{3,2,1,0:T(8,128)S(1)}, u32[]{:S(2)}, u32[]{:S(2)}) collective-permute-start(f32[2,2,64,128]{3,2,1,0:T(8,128)S(1)} %pad_maximum_fusion.11.own), channel_id=1, source_target_pairs={{32,0},{64,32},{96,64},{128,96},{160,128},{192,160},{224,192},{256... | collective-permute-start | bytes 393224 | tf_op jit(solution)/shard_map/ppermute | solution.py:402
  76.2 1.3 collective-permute-start.11
  77.5 3.1 %collective-permute-done.10.high = f32[2,2,64,128]{3,2,1,0:T(8,128)S(1)} collective-permute-done((f32[2,2,64,128]{3,2,1,0:T(8,128)S(1)}, f32[2,2,64,128]{3,2,1,0:T(8,128)S(1)}, u32[]{:S(2)}, u32[]{:S(2)}) %collective-permute-start.10) | collective-permute-done | bytes 131104 | tf_op jit(solution)/shard_map/ppermute | solution.py:402
  80.6 2.5 %collective-permute-done.11.far_high = f32[2,2,64,128]{3,2,1,0:T(8,128)S(1)} collective-permute-done((f32[2,2,64,128]{3,2,1,0:T(8,128)S(1)}, f32[2,2,64,128]{3,2,1,0:T(8,128)S(1)}, u32[]{:S(2)}, u32[]{:S(2)}) %collective-permute-start.11) | collective-permute-done | bytes 131104 | tf_op jit(solution)/shard_map/ppermute | solution.py:402
  83.8 2.7 %shard_map.74 = (f32[2,16,64]{2,1,0:T(8,128)}, f32[32,128]{1,0:T(8,128)}) custom-call(f32[2,2,64,128]{3,2,1,0:T(8,128)} %copy-done.5, f32[2,2,64,128]{3,2,1,0:T(8,128)} %copy-done.6, f32[2,2,64,128]{3,2,1,0:T(8,128)} %copy-done.4, f32[2,2,64,128]{3,2,1,0:T(8,128)} %copy-done.7, f32[2,2,64,128]{3,2,1,0:T(8,128)} %copy-done.8), custom_call_target="tpu_custom_call" | custom-call | tf_op jit(solution)/shard_map/pallas_call | solution.py:320
  87.2 28.8 %all_to_all.15 = f32[8,32,128]{2,1,0:T(8,128)S(1)} all-to-all(f32[8,32,128]{2,1,0:T(8,128)S(1)} %broadcast_in_dim.30), channel_id=1, replica_groups={{0,128,256,384,512,640,768,896},{32,160,288,416,544,672,800,928},{64,19..., dimensions={0} | all-to-all | bytes 262144 | tf_op jit(solution)/shard_map/all_to_all | solution.py:49
  116.1 0.9 broadcast_in_dim.31
  116.9 6.7 %all-to-all-start.2 = ((f32[4,8,32,128]{3,2,1,0:T(8,128)}), f32[4,8,32,128]{3,2,1,0:T(8,128)S(1)}, u32[]{:S(2)}, u32[]{:S(2)}) async-start(f32[4,8,32,128]{3,2,1,0:T(8,128)} %broadcast_in_dim.31), calls=%async_computation.2 | async-start | bytes 1048576 | tf_op jit(solution)/shard_map/all_to_all | solution.py:49
  124.4 6.9 %all-to-all-done.2.gathered_ref = f32[4,8,32,128]{3,2,1,0:T(8,128)S(1)} async-done(((f32[4,8,32,128]{3,2,1,0:T(8,128)}), f32[4,8,32,128]{3,2,1,0:T(8,128)S(1)}, u32[]{:S(2)}, u32[]{:S(2)}) %all-to-all-start.2) | async-done | bytes 524320 | tf_op jit(solution)/shard_map/all_to_all | solution.py:49
  132.1 3.6 %shard_map.75 = (f32[32,8,32]{2,1,0:T(8,128)}, f32[16,4,16]{2,1,0:T(4,128)}, f32[16,4,16]{2,1,0:T(4,128)}) custom-call(f32[4,8,32,128]{3,2,1,0:T(8,128)} %copy-done), custom_call_target="tpu_custom_call" | custom-call | tf_op jit(solution)/shard_map/pallas_call | solution.py:339
  (52 shorter events, 8.9 us)
Async XLA Ops:
  1.6 19.1 %collective-permute-start.1 = (f32[3,4,32,128]{3,2,1,0:T(8,128)S(1)}, f32[3,4,32,128]{3,2,1,0:T(8,128)S(1)}, u32[]{:S(2)}, u32[]{:S(2)}) collective-permute-start(f32[3,4,32,128]{3,2,1,0:T(8,128)S(1)} %pad_maximum_fusion.2), channel_id=1, source_target_pairs={{32,0},{64,32},{96,64},{128,96},{160,128},{192,160},{224,192},{256... | collective-permute-start | bytes 589832 | tf_op jit(solution)/shard_map/ppermute | solution.py:30
  17.6 4.5 %collective-permute-start = (f32[3,4,32,128]{3,2,1,0:T(8,128)S(1)}, f32[3,4,32,128]{3,2,1,0:T(8,128)S(1)}, u32[]{:S(2)}, u32[]{:S(2)}) collective-permute-start(f32[3,4,32,128]{3,2,1,0:T(8,128)S(1)} %pad_maximum_fusion.2), channel_id=1, source_target_pairs={{0,32},{32,64},{64,96},{96,128},{128,160},{160,192},{192,224},{224... | collective-permute-start | bytes 589832 | tf_op jit(solution)/shard_map/ppermute | solution.py:27
  23.3 8.2 %copy-start.1 = (f32[4,32,128]{2,1,0:T(8,128)S(1)}, f32[4,32,128]{2,1,0:T(8,128)}, u32[]{:S(2)}) copy-start(f32[4,32,128]{2,1,0:T(8,128)} %param.3) | copy-start | bytes 196612
  23.3 8.2 %copy-start.2 = (f32[4,32,128]{2,1,0:T(8,128)S(1)}, f32[4,32,128]{2,1,0:T(8,128)}, u32[]{:S(2)}) copy-start(f32[4,32,128]{2,1,0:T(8,128)} %param.4) | copy-start | bytes 196612
  23.3 8.2 %copy-start.3 = (f32[4,32,128]{2,1,0:T(8,128)S(1)}, f32[4,32,128]{2,1,0:T(8,128)}, u32[]{:S(2)}) copy-start(f32[4,32,128]{2,1,0:T(8,128)} %param.5) | copy-start | bytes 196612
  23.6 5.6 %collective-permute-start.3 = (f32[3,12,32,4]{2,3,1,0:T(4,128)S(1)}, f32[3,12,32,4]{2,3,1,0:T(4,128)S(1)}, u32[]{:S(2)}, u32[]{:S(2)}) collective-permute-start(f32[3,12,32,4]{2,3,1,0:T(4,128)S(1)} %copy.23), channel_id=1, source_target_pairs={{8,0},{16,8},{24,16},{9,1},{17,9},{25,17},{10,2},{18,10},{26,18},{... | collective-permute-start | bytes 55304 | tf_op jit(solution)/shard_map/ppermute | solution.py:30
  25.2 6.0 %collective-permute-start.2 = (f32[3,12,32,4]{2,3,1,0:T(4,128)S(1)}, f32[3,12,32,4]{2,3,1,0:T(4,128)S(1)}, u32[]{:S(2)}, u32[]{:S(2)}) collective-permute-start(f32[3,12,32,4]{2,3,1,0:T(4,128)S(1)} %copy.22), channel_id=1, source_target_pairs={{0,8},{8,16},{16,24},{1,9},{9,17},{17,25},{2,10},{10,18},{18,26},{... | collective-permute-start | bytes 55304 | tf_op jit(solution)/shard_map/ppermute | solution.py:27
  31.8 7.1 %collective-permute-start.5 = (f32[3,12,4,136]{3,2,1,0:T(4,128)S(1)}, f32[3,12,4,136]{3,2,1,0:T(4,128)S(1)}, u32[]{:S(2)}, u32[]{:S(2)}) collective-permute-start(f32[3,12,4,136]{3,2,1,0:T(4,128)S(1)} %get-tuple-element.34), channel_id=1, source_target_pairs={{1,0},{2,1},{3,2},{4,3},{5,4},{6,5},{7,6},{9,8},{10,9},{11,10},{12... | collective-permute-start | bytes 235016 | tf_op jit(solution)/shard_map/ppermute | solution.py:30
  33.1 6.7 %collective-permute-start.4 = (f32[3,12,4,136]{3,2,1,0:T(4,128)S(1)}, f32[3,12,4,136]{3,2,1,0:T(4,128)S(1)}, u32[]{:S(2)}, u32[]{:S(2)}) collective-permute-start(f32[3,12,4,136]{3,2,1,0:T(4,128)S(1)} %get-tuple-element.33), channel_id=1, source_target_pairs={{0,1},{1,2},{2,3},{3,4},{4,5},{5,6},{6,7},{8,9},{9,10},{10,11},{11... | collective-permute-start | bytes 235016 | tf_op jit(solution)/shard_map/ppermute | solution.py:27
  45.0 11.4 %all-to-all-start = ((f32[8,2,16,128]{3,2,1,0:T(8,128)}), f32[8,2,16,128]{3,2,1,0:T(8,128)S(1)}, u32[]{:S(2)}, u32[]{:S(2)}) async-start(f32[8,2,16,128]{3,2,1,0:T(8,128)} %broadcast_in_dim.29), calls=%async_computation | async-start | bytes 262144 | tf_op jit(solution)/shard_map/all_to_all | solution.py:37
  56.6 6.0 %collective-permute-start.7 = (f32[2,2,64,32]{3,2,1,0:T(8,128)S(1)}, f32[2,2,64,32]{3,2,1,0:T(8,128)S(1)}, u32[]{:S(2)}, u32[]{:S(2)}) collective-permute-start(f32[2,2,64,32]{3,2,1,0:T(8,128)S(1)} %get-tuple-element.46), channel_id=1, source_target_pairs={{8,0},{16,8},{24,16},{9,1},{17,9},{25,17},{10,2},{18,10},{26,18},{... | collective-permute-start | bytes 98312 | tf_op jit(solution)/shard_map/ppermute | solution.py:30
  57.9 6.2 %collective-permute-start.6 = (f32[2,2,64,32]{3,2,1,0:T(8,128)S(1)}, f32[2,2,64,32]{3,2,1,0:T(8,128)S(1)}, u32[]{:S(2)}, u32[]{:S(2)}) collective-permute-start(f32[2,2,64,32]{3,2,1,0:T(8,128)S(1)} %get-tuple-element.45), channel_id=1, source_target_pairs={{0,8},{8,16},{16,24},{1,9},{9,17},{17,25},{2,10},{10,18},{18,26},{... | collective-permute-start | bytes 98312 | tf_op jit(solution)/shard_map/ppermute | solution.py:27
  64.3 18.8 %copy-start.4 = (f32[2,2,64,128]{3,2,1,0:T(8,128)}, f32[2,2,64,128]{3,2,1,0:T(8,128)S(1)}, u32[]{:S(2)}) copy-start(f32[2,2,64,128]{3,2,1,0:T(8,128)S(1)} %pad_maximum_fusion.11.own) | copy-start | bytes 393220
  64.3 13.2 %collective-permute-start.8 = (f32[2,2,64,128]{3,2,1,0:T(8,128)S(1)}, f32[2,2,64,128]{3,2,1,0:T(8,128)S(1)}, u32[]{:S(2)}, u32[]{:S(2)}) collective-permute-start(f32[2,2,64,128]{3,2,1,0:T(8,128)S(1)} %pad_maximum_fusion.11.own), channel_id=1, source_target_pairs={{0,64},{32,96},{64,128},{96,160},{128,192},{160,224},{192,256},{22... | collective-permute-start | bytes 393224 | tf_op jit(solution)/shard_map/ppermute | solution.py:401
  65.6 11.9 %collective-permute-start.9 = (f32[2,2,64,128]{3,2,1,0:T(8,128)S(1)}, f32[2,2,64,128]{3,2,1,0:T(8,128)S(1)}, u32[]{:S(2)}, u32[]{:S(2)}) collective-permute-start(f32[2,2,64,128]{3,2,1,0:T(8,128)S(1)} %pad_maximum_fusion.11.own), channel_id=1, source_target_pairs={{0,32},{32,64},{64,96},{96,128},{128,160},{160,192},{192,224},{224... | collective-permute-start | bytes 393224 | tf_op jit(solution)/shard_map/ppermute | solution.py:401
  74.2 6.3 %collective-permute-start.10 = (f32[2,2,64,128]{3,2,1,0:T(8,128)S(1)}, f32[2,2,64,128]{3,2,1,0:T(8,128)S(1)}, u32[]{:S(2)}, u32[]{:S(2)}) collective-permute-start(f32[2,2,64,128]{3,2,1,0:T(8,128)S(1)} %pad_maximum_fusion.11.own), channel_id=1, source_target_pairs={{32,0},{64,32},{96,64},{128,96},{160,128},{192,160},{224,192},{256... | collective-permute-start | bytes 393224 | tf_op jit(solution)/shard_map/ppermute | solution.py:402
  76.2 6.9 %collective-permute-start.11 = (f32[2,2,64,128]{3,2,1,0:T(8,128)S(1)}, f32[2,2,64,128]{3,2,1,0:T(8,128)S(1)}, u32[]{:S(2)}, u32[]{:S(2)}) collective-permute-start(f32[2,2,64,128]{3,2,1,0:T(8,128)S(1)} %pad_maximum_fusion.11.own), channel_id=1, source_target_pairs={{64,0},{96,32},{128,64},{160,96},{192,128},{224,160},{256,192},{28... | collective-permute-start | bytes 393224 | tf_op jit(solution)/shard_map/ppermute | solution.py:402
  77.5 5.6 %copy-start.5 = (f32[2,2,64,128]{3,2,1,0:T(8,128)}, f32[2,2,64,128]{3,2,1,0:T(8,128)S(1)}, u32[]{:S(2)}) copy-start(f32[2,2,64,128]{3,2,1,0:T(8,128)S(1)} %collective-permute-done.8.far_low) | copy-start | bytes 393220
  77.5 5.6 %copy-start.6 = (f32[2,2,64,128]{3,2,1,0:T(8,128)}, f32[2,2,64,128]{3,2,1,0:T(8,128)S(1)}, u32[]{:S(2)}) copy-start(f32[2,2,64,128]{3,2,1,0:T(8,128)S(1)} %collective-permute-done.9.low) | copy-start | bytes 393220
  80.6 2.5 %copy-start.7 = (f32[2,2,64,128]{3,2,1,0:T(8,128)}, f32[2,2,64,128]{3,2,1,0:T(8,128)S(1)}, u32[]{:S(2)}) copy-start(f32[2,2,64,128]{3,2,1,0:T(8,128)S(1)} %collective-permute-done.10.high) | copy-start | bytes 393220
  83.1 0.7 copy-start.8
  116.9 14.4 %all-to-all-start.2 = ((f32[4,8,32,128]{3,2,1,0:T(8,128)}), f32[4,8,32,128]{3,2,1,0:T(8,128)S(1)}, u32[]{:S(2)}, u32[]{:S(2)}) async-start(f32[4,8,32,128]{3,2,1,0:T(8,128)} %broadcast_in_dim.31), calls=%async_computation.2 | async-start | bytes 1048576 | tf_op jit(solution)/shard_map/all_to_all | solution.py:49
  131.3 0.8 copy-start

commit v3 on v2

--- a/solution.py
+++ b/solution.py
@@ -13,6 +13,7 @@
 NEAR = 4
 ROWS = 24
 COLUMNS = 32
+INNER = 4
 
 
 def steps(axis, by):
@@ -21,15 +22,30 @@
     return forward, [(b, a) for a, b in forward]
 
 
-def with_halo(block, sides, width):
-    for axis, dim in sides:
-        forward, backward = steps(axis, 1)
-        low = lax.ppermute(
-            lax.slice_in_dim(block, block.shape[dim] - width, None, axis=dim), axis, forward
-        )
-        high = lax.ppermute(lax.slice_in_dim(block, 0, width, axis=dim), axis, backward)
-        block = jnp.concatenate([low, block, high], axis=dim)
-    return block
+def shifted(low_side, high_side, axis, by=1):
+    forward, backward = steps(axis, by)
+    return lax.ppermute(low_side, axis, forward), lax.ppermute(high_side, axis, backward)
+
+
+def near_halo(bundle):
+    low, high = shifted(bundle, bundle, "gx")
+    parts = (low, bundle, high)
+
+    def joined(pick):
+        return jnp.concatenate([pick(part) for part in parts], axis=1)
+
+    left, right = shifted(
+        joined(lambda part: part[..., -NEAR:]), joined(lambda part: part[..., :NEAR]), "gy"
+    )
+    up = jnp.concatenate(
+        [left[:, :, -NEAR:], joined(lambda part: part[:, :, -NEAR:]), right[:, :, -NEAR:]], axis=3
+    )
+    down = jnp.concatenate(
+        [left[:, :, :NEAR], joined(lambda part: part[:, :, :NEAR]), right[:, :, :NEAR]], axis=3
+    )
+    below, above = shifted(up, down, "gz")
+    middle = jnp.concatenate([left, joined(lambda part: part), right], axis=3)
+    return jnp.concatenate([below, middle, above], axis=2)
 
 
 def copy_for_each(shard, axis):
@@ -39,22 +55,13 @@
     )
 
 
-def gathered(shard, axis):
-    peers = lax.axis_size(axis)
-    inner = 4 if peers % 4 == 0 else 1
-    outer = peers // inner
-    apart = [[i + inner * j for j in range(outer)] for i in range(inner)]
-    beside = [[inner * j + i for i in range(inner)] for j in range(outer)]
-    for groups in (apart, beside):
-        shard = lax.all_to_all(
-            jnp.broadcast_to(shard[None], (len(groups[0]), *shard.shape)),
-            axis,
-            0,
-            0,
-            axis_index_groups=groups,
-            tiled=True,
-        )
-    return shard
+def gathered(copies, axis):
+    outer = copies.shape[0]
+    apart = [[i + INNER * j for j in range(outer)] for i in range(INNER)]
+    beside = [[INNER * j + i for i in range(INNER)] for j in range(outer)]
+    shard = lax.all_to_all(copies, axis, 0, 0, axis_index_groups=apart, tiled=True)
+    copies = jnp.broadcast_to(shard[None], (INNER, *shard.shape))
+    return lax.all_to_all(copies, axis, 0, 0, axis_index_groups=beside, tiled=True)
 
 
 def inside_mask(shape, sides):
@@ -177,14 +184,20 @@
 def level_one_kernel(
     far_low, low, own, high, far_high, solution_ref, packed_ref, d, r, wx, wz, wy, inv, both
 ):
-    parts = (far_low, low, own, high, far_high)
-    planes = own.shape[1]
-    total = planes * len(parts)
+    planes = own.shape[0] // 2
     first = 2 * planes
     last = first + planes
+    whole = {1: low, 2: own, 3: high}
 
     def conduct(p):
-        return parts[p // planes][1, p % planes]
+        if p // planes in whole:
+            return whole[p // planes][planes + p % planes]
+        return (far_low if p < first else far_high)[1 + p % planes]
+
+    def origin(p):
+        if p // planes in whole:
+            return whole[p // planes][p % planes]
+        return (far_low if p < first else far_high)[0]
 
     def flow(p):
         return wx[p] * (d[p + 1] - d[p])
@@ -194,7 +207,7 @@
         wx[p] = 0.5 * (conduct(p) + conduct(p + 1))
     for p in range(first - reach, last + reach):
         inverse = set_faces(p, conduct(p), wx[p - 1], wx[p], wz, wy, inv)
-        source = parts[p // planes][0, p % planes]
+        source = origin(p)
         r[p] = source
         d[p] = source * inverse * (1.0 / THETA)
     answers = [d[p] for p in range(first, last)]
@@ -221,9 +234,9 @@
     both[:tall] = 0.25 * (r[first] + r[first + 1])
     both[tall:] = 0.125 * (conduct(first) + conduct(first + 1))
     halved = both[pl.ds(0, tall, stride=2)] + both[pl.ds(1, tall, stride=2)]
-    packed_ref[...] = paired(halved[: tall // 2], pairing(0)) + paired(
-        halved[tall // 2 :], pairing(64)
-    )
+    packed = paired(halved[: tall // 2], pairing(0)) + paired(halved[tall // 2 :], pairing(64))
+    for copy in range(packed_ref.shape[0]):
+        packed_ref[copy] = packed
 
 
 def smooth_folded(half, c, r, d, s, wx, wz, wy, inv):
@@ -315,15 +328,17 @@
 
 
 def level_one_call(parts, rows, columns):
-    _, planes, tall, wide = parts[0].shape
+    planes, tall, wide = parts[2].shape
+    planes //= 2
     total = planes * len(parts)
     return pl.pallas_call(
         level_one_kernel,
-        out_shape=(f32(planes, rows, columns), f32(tall // 2, wide)),
+        out_shape=(f32(planes, rows, columns), f32(lax.axis_size("gx") // INNER, tall // 2, wide)),
         in_specs=in_vmem(5),
         out_specs=tuple(in_vmem(2)),
         scratch_shapes=[pltpu.VMEM((total, tall, wide), jnp.float32)] * 6
         + [pltpu.VMEM((2 * tall, wide), jnp.float32)],
+        compiler_params=pltpu.CompilerParams(vmem_limit_bytes=8 * 2**20),
     )(*parts)
 
 
@@ -348,6 +363,7 @@
         scratch_shapes=scratch(count, tall)
         + [pltpu.VMEM((count * tall, wide), jnp.float32)]
         + scratch(count // 2, tall // 2),
+        compiler_params=pltpu.CompilerParams(vmem_limit_bytes=8 * 2**20),
     )(everyone)
 
 
@@ -366,11 +382,7 @@
 
 
 def shards(conductivity, initial_guess, right_side):
-    grown = with_halo(
-        jnp.stack([conductivity, right_side, initial_guess]),
-        (("gx", 1), ("gy", 3), ("gz", 2)),
-        NEAR,
-    )
+    grown = near_halo(jnp.stack([conductivity, right_side, initial_guess]))
     inside = inside_mask(
         grown.shape[1:],
         (
@@ -393,15 +405,31 @@
     packed = lax.dynamic_slice_in_dim(
         everyone, lax.axis_index("gz") * rows, rows + 2 * ROWS, axis=1
     )
-    both = jnp.stack([packed[..., :columns], packed[..., columns:]])
-    both = with_halo(both, (("gy", 3),), COLUMNS)
-    parts = {0: both}
-    for by in (1, 2):
-        forward, backward = steps("gx", by)
-        parts[-by] = lax.ppermute(both, "gx", forward)
-        parts[by] = lax.ppermute(both, "gx", backward)
+    pieces = [packed[p, :, q * columns : (q + 1) * columns] for q in (0, 1) for p in range(planes)]
+    left, right = shifted(
+        jnp.concatenate([piece[:, -COLUMNS:] for piece in pieces], axis=1),
+        jnp.concatenate([piece[:, :COLUMNS] for piece in pieces], axis=1),
+        "gy",
+    )
+    pieces = [
+        jnp.concatenate(
+            [
+                left[:, i * COLUMNS : (i + 1) * COLUMNS],
+                piece,
+                right[:, i * COLUMNS : (i + 1) * COLUMNS],
+            ],
+            axis=1,
+        )
+        for i, piece in enumerate(pieces)
+    ]
+    source, conduct = pieces[:planes], pieces[planes:]
+    far = shifted(
+        jnp.stack([source[-1], *conduct]), jnp.stack([source[0], *conduct]), "gx", 2
+    )
+    own = jnp.stack(source + conduct)
+    near = shifted(own, own, "gx")
     level_one_solution, packed = level_one_call(
-        [parts[by] for by in sorted(parts)], rows, columns
+        (far[0], near[0], own, near[1], far[1]), rows, columns
     )
     everyone = gathered(packed, "gx")
     level_two_solution, level_three_solution, level_three_residual = coarse_call(

time: 138 us -> 132 us (0.957)
  waiting for transfers between devices: 28.2 us -> 24.8 us
  Pallas kernels: 6.35 us -> 3.97 us
    ppermute x12, waiting for transfers between devices: 13.3 us -> 9.92 us  [the longest x6 5.8 us: shifted(): lax.ppermute(low_side, axis, forward)]
    slice x1 -> x24, local copies, waits for them, and re-layouts: 0.22 us -> 3.19 us  [the longest x6 0.76 us: near_halo(): part[..., -NEAR:]]
    unnamed x20 -> x6, local copies, waits for them, and re-layouts: 2.04 us -> 0.02 us
  transfers between devices with their start and end apart: 14 -> 14, of which waited for: 10 -> 9; matrix products, arithmetic and copies ran while one was open for 2% -> 3% of each run, Pallas kernels for 0% -> 0%
where the time goes in v3:
time: 132 us; the launch traced here: 131 us
  starting transfers between devices  58.2 us (44%)
  blocking collectives  29.6 us (22%)
  waiting for transfers between devices  24.8 us (19%)
  other arithmetic  6.83 us (5%)
  local copies, waits for them, and re-layouts  5.5 us (4%)
  Pallas kernels  3.97 us (3%)
    all_to_all x1, blocking collectives, gathered(): lax.all_to_all(copies, axis, 0, 0, axis_index_groups=apart, tiled=True)  29.6 us
    ppermute x6, starting transfers between devices, shifted(): lax.ppermute(low_side, axis, forward)  24.3 us
    ppermute x6, starting transfers between devices, shifted(): lax.ppermute(high_side, axis, backward)  23.1 us
    all_to_all x1, waiting for transfers between devices, copy_for_each(): lax.all_to_all(jnp.broadcast_to(shard[None], (peers, *shard.shape)), axis...  7.96 us
    all_to_all x1, starting transfers between devices, gathered(): lax.all_to_all(copies, axis, 0, 0, axis_index_groups=beside, tiled=True)  7.28 us
    all_to_all x1, waiting for transfers between devices, gathered(): lax.all_to_all(copies, axis, 0, 0, axis_index_groups=beside, tiled=True)  6.92 us
    ppermute x6, waiting for transfers between devices, shifted(): lax.ppermute(low_side, axis, forward)  5.8 us
    ppermute x6, waiting for transfers between devices, shifted(): lax.ppermute(high_side, axis, backward)  4.13 us
  transfers between devices with their start and end apart: 14, of which 9 were waited for; matrix products, arithmetic and copies ran while one was open for 3% of the time, Pallas kernels for 0%

profile of v3, /device:TPU:1, one launch (start us, length us, event | category | flops | bytes accessed | tf_op | source)
XLA Modules:
  0.0 130.6 jit_solution(4488541783031455419)
XLA Ops:
  0.6 0.9 pad_maximum_fusion.1
  1.6 16.0 %collective-permute-start.1 = (f32[3,4,32,128]{3,2,1,0:T(8,128)S(1)}, f32[3,4,32,128]{3,2,1,0:T(8,128)S(1)}, u32[]{:S(2)}, u32[]{:S(2)}) collective-permute-start(f32[3,4,32,128]{3,2,1,0:T(8,128)S(1)} %pad_maximum_fusion.1), channel_id=1, source_target_pairs={{32,0},{64,32},{96,64},{128,96},{160,128},{192,160},{224,192},{256... | collective-permute-start | bytes 589832 | tf_op jit(solution)/shard_map/ppermute | solution.py:27
  17.6 1.9 %collective-permute-start = (f32[3,4,32,128]{3,2,1,0:T(8,128)S(1)}, f32[3,4,32,128]{3,2,1,0:T(8,128)S(1)}, u32[]{:S(2)}, u32[]{:S(2)}) collective-permute-start(f32[3,4,32,128]{3,2,1,0:T(8,128)S(1)} %pad_maximum_fusion.1), channel_id=1, source_target_pairs={{0,32},{32,64},{64,96},{96,128},{128,160},{160,192},{192,224},{224... | collective-permute-start | bytes 589832 | tf_op jit(solution)/shard_map/ppermute | solution.py:27
  20.7 1.5 %collective-permute-done = f32[3,4,32,128]{3,2,1,0:T(8,128)S(1)} collective-permute-done((f32[3,4,32,128]{3,2,1,0:T(8,128)S(1)}, f32[3,4,32,128]{3,2,1,0:T(8,128)S(1)}, u32[]{:S(2)}, u32[]{:S(2)}) %collective-permute-start) | collective-permute-done | bytes 196640 | tf_op jit(solution)/shard_map/ppermute | solution.py:27
  22.4 1.3 collective-permute-start.3
  24.1 4.0 %collective-permute-start.2 = (f32[3,12,32,4]{2,3,1,0:T(4,128)S(1)}, f32[3,12,32,4]{2,3,1,0:T(4,128)S(1)}, u32[]{:S(2)}, u32[]{:S(2)}) collective-permute-start(f32[3,12,32,4]{2,3,1,0:T(4,128)S(1)} %pad_maximum_fusion.9), channel_id=1, source_target_pairs={{0,8},{8,16},{16,24},{1,9},{9,17},{17,25},{2,10},{10,18},{18,26},{... | collective-permute-start | bytes 55304 | tf_op jit(solution)/shard_map/ppermute | solution.py:27
  28.6 1.3 %collective-permute-done.2 = f32[3,12,32,4]{2,3,1,0:T(4,128)S(1)} collective-permute-done((f32[3,12,32,4]{2,3,1,0:T(4,128)S(1)}, f32[3,12,32,4]{2,3,1,0:T(4,128)S(1)}, u32[]{:S(2)}, u32[]{:S(2)}) %collective-permute-start.2) | collective-permute-done | bytes 18464 | tf_op jit(solution)/shard_map/ppermute | solution.py:27
  30.5 1.3 collective-permute-start.5
  32.7 4.0 %collective-permute-start.4 = (f32[3,12,4,136]{3,2,1,0:T(4,128)S(1)}, f32[3,12,4,136]{3,2,1,0:T(4,128)S(1)}, u32[]{:S(2)}, u32[]{:S(2)}) collective-permute-start(f32[3,12,4,136]{3,2,1,0:T(4,128)S(1)} %pad_maximum_fusion.2), channel_id=1, source_target_pairs={{0,1},{1,2},{2,3},{3,4},{4,5},{5,6},{6,7},{8,9},{9,10},{10,11},{11... | collective-permute-start | bytes 235016 | tf_op jit(solution)/shard_map/ppermute | solution.py:27
  37.7 1.8 %collective-permute-done.4 = f32[3,12,4,136]{3,2,1,0:T(4,128)S(1)} collective-permute-done((f32[3,12,4,136]{3,2,1,0:T(4,128)S(1)}, f32[3,12,4,136]{3,2,1,0:T(4,128)S(1)}, u32[]{:S(2)}, u32[]{:S(2)}) %collective-permute-start.4) | collective-permute-done | bytes 78368 | tf_op jit(solution)/shard_map/ppermute | solution.py:27
  39.4 0.7 pad_maximum_fusion
  40.2 1.0 divide_select_fusion
  41.2 0.7 add_select_fusion.1
  41.9 0.8 add_select_fusion
  43.9 0.7 broadcast_in_dim.23
  44.6 3.5 %all-to-all-start = ((f32[8,2,16,128]{3,2,1,0:T(8,128)}), f32[8,2,16,128]{3,2,1,0:T(8,128)S(1)}, u32[]{:S(2)}, u32[]{:S(2)}) async-start(f32[8,2,16,128]{3,2,1,0:T(8,128)} %broadcast_in_dim.23), calls=%async_computation | async-start | bytes 262144 | tf_op jit(solution)/shard_map/all_to_all | solution.py:53
  48.1 8.0 %all-to-all-done = f32[8,2,16,128]{3,2,1,0:T(8,128)S(1)} async-done(((f32[8,2,16,128]{3,2,1,0:T(8,128)}), f32[8,2,16,128]{3,2,1,0:T(8,128)S(1)}, u32[]{:S(2)}, u32[]{:S(2)}) %all-to-all-start) | async-done | bytes 131104 | tf_op jit(solution)/shard_map/all_to_all | solution.py:53
  56.6 1.3 collective-permute-start.7
  58.0 4.3 %collective-permute-start.6 = (f32[64,128]{1,0:T(8,128)S(1)}, f32[64,128]{1,0:T(8,128)S(1)}, u32[]{:S(2)}, u32[]{:S(2)}) collective-permute-start(f32[64,128]{1,0:T(8,128)S(1)} %pad_maximum_fusion.11), channel_id=1, source_target_pairs={{0,8},{8,16},{16,24},{1,9},{9,17},{17,25},{2,10},{10,18},{18,26},{... | collective-permute-start | bytes 98312 | tf_op jit(solution)/shard_map/ppermute | solution.py:27
  62.3 0.9 collective-permute-done.6
  63.7 8.1 %collective-permute-start.9 = (f32[4,64,128]{2,1,0:T(8,128)S(1)}, f32[4,64,128]{2,1,0:T(8,128)S(1)}, u32[]{:S(2)}, u32[]{:S(2)}) collective-permute-start(f32[4,64,128]{2,1,0:T(8,128)S(1)} %pad_maximum_fusion.4.own), channel_id=1, source_target_pairs={{0,32},{32,64},{64,96},{96,128},{128,160},{160,192},{192,224},{224... | collective-permute-start | bytes 393224 | tf_op jit(solution)/shard_map/ppermute | solution.py:27
  71.9 1.9 %collective-permute-start.10 = (f32[4,64,128]{2,1,0:T(8,128)S(1)}, f32[4,64,128]{2,1,0:T(8,128)S(1)}, u32[]{:S(2)}, u32[]{:S(2)}) collective-permute-start(f32[4,64,128]{2,1,0:T(8,128)S(1)} %pad_maximum_fusion.4.own), channel_id=1, source_target_pairs={{32,0},{64,32},{96,64},{128,96},{160,128},{192,160},{224,192},{256... | collective-permute-start | bytes 393224 | tf_op jit(solution)/shard_map/ppermute | solution.py:27
  73.8 2.0 %collective-permute-start.8 = (f32[3,64,128]{2,1,0:T(8,128)S(1)}, f32[3,64,128]{2,1,0:T(8,128)S(1)}, u32[]{:S(2)}, u32[]{:S(2)}) collective-permute-start(f32[3,64,128]{2,1,0:T(8,128)S(1)} %get-tuple-element.62), channel_id=1, source_target_pairs={{0,64},{32,96},{64,128},{96,160},{128,192},{160,224},{192,256},{22... | collective-permute-start | bytes 294920 | tf_op jit(solution)/shard_map/ppermute | solution.py:27
  75.8 1.3 collective-permute-start.11
  77.5 3.7 %collective-permute-done.11.far_high = f32[3,64,128]{2,1,0:T(8,128)S(1)} collective-permute-done((f32[3,64,128]{2,1,0:T(8,128)S(1)}, f32[3,64,128]{2,1,0:T(8,128)S(1)}, u32[]{:S(2)}, u32[]{:S(2)}) %collective-permute-start.11) | collective-permute-done | bytes 98336 | tf_op jit(solution)/shard_map/ppermute | solution.py:27
  81.2 1.4 %shard_map.74 = (f32[2,16,64]{2,1,0:T(8,128)}, f32[8,32,128]{2,1,0:T(8,128)S(1)}) custom-call(f32[3,64,128]{2,1,0:T(8,128)S(1)} %collective-permute-done.8.far_low, f32[4,64,128]{2,1,0:T(8,128)S(1)} %collective-permute-done.9.low, f32[4,64,128]{2,1,0:T(8,128)S(1)} %pad_maximum_fusion.4.own, f32[4,64,128]{2,1,0:T(8,128)S(1)} %collective-permute-done.10.high, ...), custom_call_target="tpu_custom_call" | custom-call | tf_op jit(solution)/shard_map/pallas_call | solution.py:334
  82.6 29.6 %all_to_all.15 = f32[8,32,128]{2,1,0:T(8,128)S(1)} all-to-all(f32[8,32,128]{2,1,0:T(8,128)S(1)} %get-tuple-element.11), channel_id=1, replica_groups={{0,128,256,384,512,640,768,896},{32,160,288,416,544,672,800,928},{64,19..., dimensions={0} | all-to-all | bytes 262144 | tf_op jit(solution)/shard_map/all_to_all | solution.py:62
  112.2 0.8 broadcast_in_dim.24
  113.1 7.3 %all-to-all-start.2 = ((f32[4,8,32,128]{3,2,1,0:T(8,128)}), f32[4,8,32,128]{3,2,1,0:T(8,128)S(1)}, u32[]{:S(2)}, u32[]{:S(2)}) async-start(f32[4,8,32,128]{3,2,1,0:T(8,128)} %broadcast_in_dim.24), calls=%async_computation.2 | async-start | bytes 1048576 | tf_op jit(solution)/shard_map/all_to_all | solution.py:64
  120.3 0.8 slice_add_fusion
  121.1 6.9 %all-to-all-done.2.gathered_ref = f32[4,8,32,128]{3,2,1,0:T(8,128)S(1)} async-done(((f32[4,8,32,128]{3,2,1,0:T(8,128)}), f32[4,8,32,128]{3,2,1,0:T(8,128)S(1)}, u32[]{:S(2)}, u32[]{:S(2)}) %all-to-all-start.2) | async-done | bytes 524320 | tf_op jit(solution)/shard_map/all_to_all | solution.py:64
  128.0 2.6 %shard_map.75 = (f32[32,8,32]{2,1,0:T(8,128)}, f32[16,4,16]{2,1,0:T(4,128)}, f32[16,4,16]{2,1,0:T(4,128)}) custom-call(f32[4,8,32,128]{3,2,1,0:T(8,128)S(1)} %all-to-all-done.2.gathered_ref), custom_call_target="tpu_custom_call" | custom-call | tf_op jit(solution)/shard_map/pallas_call | solution.py:354
  (68 shorter events, 7.2 us)
Async XLA Ops:
  0.6 19.4 %copy-start = (f32[4,32,128]{2,1,0:T(8,128)S(1)}, f32[4,32,128]{2,1,0:T(8,128)}, u32[]{:S(2)}) copy-start(f32[4,32,128]{2,1,0:T(8,128)} %param.3) | copy-start | bytes 196612
  1.6 18.8 %collective-permute-start.1 = (f32[3,4,32,128]{3,2,1,0:T(8,128)S(1)}, f32[3,4,32,128]{3,2,1,0:T(8,128)S(1)}, u32[]{:S(2)}, u32[]{:S(2)}) collective-permute-start(f32[3,4,32,128]{3,2,1,0:T(8,128)S(1)} %pad_maximum_fusion.1), channel_id=1, source_target_pairs={{32,0},{64,32},{96,64},{128,96},{160,128},{192,160},{224,192},{256... | collective-permute-start | bytes 589832 | tf_op jit(solution)/shard_map/ppermute | solution.py:27
  17.6 4.5 %collective-permute-start = (f32[3,4,32,128]{3,2,1,0:T(8,128)S(1)}, f32[3,4,32,128]{3,2,1,0:T(8,128)S(1)}, u32[]{:S(2)}, u32[]{:S(2)}) collective-permute-start(f32[3,4,32,128]{3,2,1,0:T(8,128)S(1)} %pad_maximum_fusion.1), channel_id=1, source_target_pairs={{0,32},{32,64},{64,96},{96,128},{128,160},{160,192},{192,224},{224... | collective-permute-start | bytes 589832 | tf_op jit(solution)/shard_map/ppermute | solution.py:27
  22.4 5.7 %collective-permute-start.3 = (f32[3,12,32,4]{2,3,1,0:T(4,128)S(1)}, f32[3,12,32,4]{2,3,1,0:T(4,128)S(1)}, u32[]{:S(2)}, u32[]{:S(2)}) collective-permute-start(f32[3,12,32,4]{2,3,1,0:T(4,128)S(1)} %pad_maximum_fusion.10), channel_id=1, source_target_pairs={{8,0},{16,8},{24,16},{9,1},{17,9},{25,17},{10,2},{18,10},{26,18},{... | collective-permute-start | bytes 55304 | tf_op jit(solution)/shard_map/ppermute | solution.py:27
  24.1 5.8 %collective-permute-start.2 = (f32[3,12,32,4]{2,3,1,0:T(4,128)S(1)}, f32[3,12,32,4]{2,3,1,0:T(4,128)S(1)}, u32[]{:S(2)}, u32[]{:S(2)}) collective-permute-start(f32[3,12,32,4]{2,3,1,0:T(4,128)S(1)} %pad_maximum_fusion.9), channel_id=1, source_target_pairs={{0,8},{8,16},{16,24},{1,9},{9,17},{17,25},{2,10},{10,18},{18,26},{... | collective-permute-start | bytes 55304 | tf_op jit(solution)/shard_map/ppermute | solution.py:27
  28.2 11.2 %copy-start.1 = (f32[4,32,128]{2,1,0:T(8,128)S(1)}, f32[4,32,128]{2,1,0:T(8,128)}, u32[]{:S(2)}) copy-start(f32[4,32,128]{2,1,0:T(8,128)} %param.4) | copy-start | bytes 196612
  28.2 11.2 %copy-start.2 = (f32[4,32,128]{2,1,0:T(8,128)S(1)}, f32[4,32,128]{2,1,0:T(8,128)}, u32[]{:S(2)}) copy-start(f32[4,32,128]{2,1,0:T(8,128)} %param.5) | copy-start | bytes 196612
  30.5 7.1 %collective-permute-start.5 = (f32[3,12,4,136]{3,2,1,0:T(4,128)S(1)}, f32[3,12,4,136]{3,2,1,0:T(4,128)S(1)}, u32[]{:S(2)}, u32[]{:S(2)}) collective-permute-start(f32[3,12,4,136]{3,2,1,0:T(4,128)S(1)} %pad_maximum_fusion.3), channel_id=1, source_target_pairs={{1,0},{2,1},{3,2},{4,3},{5,4},{6,5},{7,6},{9,8},{10,9},{11,10},{12... | collective-permute-start | bytes 235016 | tf_op jit(solution)/shard_map/ppermute | solution.py:27
  32.7 6.7 %collective-permute-start.4 = (f32[3,12,4,136]{3,2,1,0:T(4,128)S(1)}, f32[3,12,4,136]{3,2,1,0:T(4,128)S(1)}, u32[]{:S(2)}, u32[]{:S(2)}) collective-permute-start(f32[3,12,4,136]{3,2,1,0:T(4,128)S(1)} %pad_maximum_fusion.2), channel_id=1, source_target_pairs={{0,1},{1,2},{2,3},{3,4},{4,5},{5,6},{6,7},{8,9},{9,10},{10,11},{11... | collective-permute-start | bytes 235016 | tf_op jit(solution)/shard_map/ppermute | solution.py:27
  44.6 11.4 %all-to-all-start = ((f32[8,2,16,128]{3,2,1,0:T(8,128)}), f32[8,2,16,128]{3,2,1,0:T(8,128)S(1)}, u32[]{:S(2)}, u32[]{:S(2)}) async-start(f32[8,2,16,128]{3,2,1,0:T(8,128)} %broadcast_in_dim.23), calls=%async_computation | async-start | bytes 262144 | tf_op jit(solution)/shard_map/all_to_all | solution.py:53
  56.6 5.7 %collective-permute-start.7 = (f32[64,128]{1,0:T(8,128)S(1)}, f32[64,128]{1,0:T(8,128)S(1)}, u32[]{:S(2)}, u32[]{:S(2)}) collective-permute-start(f32[64,128]{1,0:T(8,128)S(1)} %pad_maximum_fusion.12), channel_id=1, source_target_pairs={{8,0},{16,8},{24,16},{9,1},{17,9},{25,17},{10,2},{18,10},{26,18},{... | collective-permute-start | bytes 98312 | tf_op jit(solution)/shard_map/ppermute | solution.py:27
  58.0 5.3 %collective-permute-start.6 = (f32[64,128]{1,0:T(8,128)S(1)}, f32[64,128]{1,0:T(8,128)S(1)}, u32[]{:S(2)}, u32[]{:S(2)}) collective-permute-start(f32[64,128]{1,0:T(8,128)S(1)} %pad_maximum_fusion.11), channel_id=1, source_target_pairs={{0,8},{8,16},{16,24},{1,9},{9,17},{17,25},{2,10},{10,18},{18,26},{... | collective-permute-start | bytes 98312 | tf_op jit(solution)/shard_map/ppermute | solution.py:27
  63.7 17.5 %collective-permute-start.9 = (f32[4,64,128]{2,1,0:T(8,128)S(1)}, f32[4,64,128]{2,1,0:T(8,128)S(1)}, u32[]{:S(2)}, u32[]{:S(2)}) collective-permute-start(f32[4,64,128]{2,1,0:T(8,128)S(1)} %pad_maximum_fusion.4.own), channel_id=1, source_target_pairs={{0,32},{32,64},{64,96},{96,128},{128,160},{160,192},{192,224},{224... | collective-permute-start | bytes 393224 | tf_op jit(solution)/shard_map/ppermute | solution.py:27
  71.9 9.4 %collective-permute-start.10 = (f32[4,64,128]{2,1,0:T(8,128)S(1)}, f32[4,64,128]{2,1,0:T(8,128)S(1)}, u32[]{:S(2)}, u32[]{:S(2)}) collective-permute-start(f32[4,64,128]{2,1,0:T(8,128)S(1)} %pad_maximum_fusion.4.own), channel_id=1, source_target_pairs={{32,0},{64,32},{96,64},{128,96},{160,128},{192,160},{224,192},{256... | collective-permute-start | bytes 393224 | tf_op jit(solution)/shard_map/ppermute | solution.py:27
  73.8 3.6 %collective-permute-start.8 = (f32[3,64,128]{2,1,0:T(8,128)S(1)}, f32[3,64,128]{2,1,0:T(8,128)S(1)}, u32[]{:S(2)}, u32[]{:S(2)}) collective-permute-start(f32[3,64,128]{2,1,0:T(8,128)S(1)} %get-tuple-element.62), channel_id=1, source_target_pairs={{0,64},{32,96},{64,128},{96,160},{128,192},{160,224},{192,256},{22... | collective-permute-start | bytes 294920 | tf_op jit(solution)/shard_map/ppermute | solution.py:27
  75.8 5.4 %collective-permute-start.11 = (f32[3,64,128]{2,1,0:T(8,128)S(1)}, f32[3,64,128]{2,1,0:T(8,128)S(1)}, u32[]{:S(2)}, u32[]{:S(2)}) collective-permute-start(f32[3,64,128]{2,1,0:T(8,128)S(1)} %get-tuple-element.61), channel_id=1, source_target_pairs={{64,0},{96,32},{128,64},{160,96},{192,128},{224,160},{256,192},{28... | collective-permute-start | bytes 294920 | tf_op jit(solution)/shard_map/ppermute | solution.py:27
  113.1 15.0 %all-to-all-start.2 = ((f32[4,8,32,128]{3,2,1,0:T(8,128)}), f32[4,8,32,128]{3,2,1,0:T(8,128)S(1)}, u32[]{:S(2)}, u32[]{:S(2)}) async-start(f32[4,8,32,128]{3,2,1,0:T(8,128)} %broadcast_in_dim.24), calls=%async_computation.2 | async-start | bytes 1048576 | tf_op jit(solution)/shard_map/all_to_all | solution.py:64

commit v4 on v3

--- a/solution.py
+++ b/solution.py
@@ -30,29 +30,14 @@
 def near_halo(bundle):
     low, high = shifted(bundle, bundle, "gx")
     parts = (low, bundle, high)
-
-    def joined(pick):
-        return jnp.concatenate([pick(part) for part in parts], axis=1)
-
-    left, right = shifted(
-        joined(lambda part: part[..., -NEAR:]), joined(lambda part: part[..., :NEAR]), "gy"
-    )
-    up = jnp.concatenate(
-        [left[:, :, -NEAR:], joined(lambda part: part[:, :, -NEAR:]), right[:, :, -NEAR:]], axis=3
-    )
-    down = jnp.concatenate(
-        [left[:, :, :NEAR], joined(lambda part: part[:, :, :NEAR]), right[:, :, :NEAR]], axis=3
-    )
-    below, above = shifted(up, down, "gz")
-    middle = jnp.concatenate([left, joined(lambda part: part), right], axis=3)
-    return jnp.concatenate([below, middle, above], axis=2)
-
-
-def copy_for_each(shard, axis):
-    peers = lax.axis_size(axis)
-    return lax.all_to_all(
-        jnp.broadcast_to(shard[None], (peers, *shard.shape)), axis, 0, 0, tiled=True
-    )
+    below, above = shifted(
+        jnp.concatenate([part[:, :, -NEAR:] for part in parts], axis=1),
+        jnp.concatenate([part[:, :, :NEAR] for part in parts], axis=1),
+        "gz",
+    )
+    seen = (*parts, below, above)
+    right_edge, left_edge = edges_call(seen)
+    return (*seen, *shifted(right_edge, left_edge, "gy"))
 
 
 def gathered(copies, axis):
@@ -64,66 +49,6 @@
     return lax.all_to_all(copies, axis, 0, 0, axis_index_groups=beside, tiled=True)
 
 
-def inside_mask(shape, sides):
-    inside = None
-    for axis, dim, own in sides:
-        halo = (shape[dim] - own) // 2
-        position = lax.axis_index(axis) * own - halo + lax.broadcasted_iota(jnp.int32, shape, dim)
-        good = (position >= 0) & (position < lax.axis_size(axis) * own)
-        inside = good if inside is None else inside & good
-    return inside
-
-
-def neighbours(padded):
-    return [
-        padded[:-2, 1:-1, 1:-1],
-        padded[2:, 1:-1, 1:-1],
-        padded[1:-1, :-2, 1:-1],
-        padded[1:-1, 2:, 1:-1],
-        padded[1:-1, 1:-1, :-2],
-        padded[1:-1, 1:-1, 2:],
-    ]
-
-
-def operate(field, weights, diagonal):
-    others = neighbours(jnp.pad(field, 1))
-    result = diagonal * field
-    for face_index in range(6):
-        result = result - weights[face_index] * others[face_index]
-    return result
-
-
-def smooth(source, start, conduct, inside):
-    theta = 0.5 * (upper_bound + lower_bound)
-    delta = 0.5 * (upper_bound - lower_bound)
-    sigma = theta / delta
-    others = neighbours(jnp.pad(conduct, 1))
-    weights = [0.5 * (conduct + other) for other in others]
-    diagonal = weights[0] + weights[1] + weights[2] + weights[3] + weights[4] + weights[5]
-    safe_diagonal = jnp.where(inside, diagonal, 1.0)
-    if start is None:
-        solution = jnp.zeros_like(source)
-        residual = source
-    else:
-        solution = start
-        residual = source - operate(solution, weights, diagonal)
-    direction = jnp.where(inside, residual / (theta * safe_diagonal), 0.0)
-    ratio_now = 1.0 / sigma
-    for sweep_index in range(SWEEPS):
-        solution = solution + direction
-        residual = residual - operate(direction, weights, diagonal)
-        if sweep_index + 1 < SWEEPS:
-            ratio_next = 1.0 / (2.0 * sigma - ratio_now)
-            direction = jnp.where(
-                inside,
-                ratio_next * ratio_now * direction
-                + 2.0 * ratio_next / delta * residual / safe_diagonal,
-                0.0,
-            )
-            ratio_now = ratio_next
-    return solution, residual
-
-
 THETA = 0.5 * (upper_bound + lower_bound)
 DELTA = 0.5 * (upper_bound - lower_bound)
 
@@ -179,6 +104,106 @@
     return jnp.dot(
         left, right, precision=lax.Precision.HIGHEST, preferred_element_type=jnp.float32
     )
+
+
+def fine_tiles(low, own, high, below, above, corner):
+    arrays, planes, rows, _ = own.shape
+    parts = (low, own, high)
+    for a in range(arrays):
+        for p in range(planes * len(parts)):
+            part = parts[p // planes]
+            for row in range(0, rows, 8):
+                yield a, p, row, part[a, p % planes, row : row + 8]
+            corner[:NEAR] = above[a, p]
+            corner[NEAR:] = below[a, p]
+            yield a, p, rows, corner[...]
+
+
+def edges_kernel(low, own, high, below, above, right_edge, left_edge, corner):
+    lane = lax.broadcasted_iota(jnp.int32, (8, 128), 1)
+    slots = 128 // NEAR
+    for t, (_, _, _, tile) in enumerate(fine_tiles(low, own, high, below, above, corner)):
+        k = t % slots
+        if k == 0:
+            right = left = jnp.zeros((8, 128), jnp.float32)
+        here = (lane >= NEAR * k) & (lane < NEAR * (k + 1))
+        right = jnp.where(here, turned(tile, NEAR * (k + 1)), right)
+        left = jnp.where(here, turned(tile, NEAR * k), left)
+        place = pl.ds(8 * (t // slots), 8)
+        right_edge[place] = right
+        left_edge[place] = left
+
+
+def turned(tile, shift):
+    return pltpu.roll(tile, shift % 128, 1) if shift % 128 else tile
+
+
+def fine_kernel(
+    low, own, high, below, above, left, right, solution_ref, packed_ref,
+    c, r, u, d, wx, wz, wy, inv, both, corner,
+):
+    planes, rows = own.shape[1:3]
+    first, last = planes, 2 * planes
+    lane = lax.broadcasted_iota(jnp.int32, (8, 128), 1)
+    slots = 128 // NEAR
+    for t, (a, p, row, tile) in enumerate(fine_tiles(low, own, high, below, above, corner)):
+        k = t % slots
+        place = pl.ds(8 * (t // slots), 8)
+        near = jnp.where(lane < NEAR, turned(right[place], -NEAR * k), 0.0)
+        near = jnp.where(lane >= 128 - NEAR, turned(left[place], -NEAR * (k + 1)), near)
+        field = (c, r, u)[a]
+        field[p, row : row + 8, :128] = tile
+        field[p, row : row + 8, 128:] = near
+
+    def flow(p, field):
+        return wx[p] * (field[p + 1] - field[p])
+
+    reach = SWEEPS
+    for p in range(first - reach - 1, last + reach):
+        wx[p] = 0.5 * (c[p] + c[p + 1])
+    flow_low = flow(first - reach - 1, u)
+    for p in range(first - reach, last + reach):
+        inverse = set_faces(p, c[p], wx[p - 1], wx[p], wz, wy, inv)
+        flow_high = flow(p, u)
+        here = u[p]
+        residual = r[p] + gained(p, here, flow_low, flow_high, wz, wy)
+        r[p] = residual
+        flow_low = flow_high
+        direction = residual * inverse * (1.0 / THETA)
+        d[p] = direction
+        if first <= p < last:
+            solution_ref[p - first] = here[:rows, :128] + direction[:rows, :128]
+    mix = list(mixes())
+    for sweep in range(SWEEPS):
+        reach -= 1
+        flow_low = flow(first - reach - 1, d)
+        for p in range(first - reach, last + reach):
+            flow_high = flow(p, d)
+            here = d[p]
+            residual = r[p] + gained(p, here, flow_low, flow_high, wz, wy)
+            r[p] = residual
+            flow_low = flow_high
+            if sweep + 1 < SWEEPS:
+                here = mix[sweep][0] * here + mix[sweep][1] * (residual * inv[p])
+                d[p] = here
+                if first <= p < last:
+                    solution_ref[p - first] = solution_ref[p - first] + here[:rows, :128]
+    half = planes // 2
+    for q in range(half):
+        p = first + 2 * q
+        both[q * rows : (q + 1) * rows] = 0.25 * (r[p, :rows, :128] + r[p + 1, :rows, :128])
+        both[(half + q) * rows : (half + q + 1) * rows] = 0.125 * (
+            c[p, :rows, :128] + c[p + 1, :rows, :128]
+        )
+    length = half * rows
+    halved = both[pl.ds(0, length, stride=2)] + both[pl.ds(1, length, stride=2)]
+    packed = paired(halved[: length // 2], pairing(0)) + paired(
+        halved[length // 2 :], pairing(64)
+    )
+    low_rows = rows // 2
+    for copy in range(packed_ref.shape[0]):
+        for q in range(half):
+            packed_ref[copy, q] = packed[q * low_rows : (q + 1) * low_rows]
 
 
 def level_one_kernel(
@@ -327,6 +352,44 @@
     return [pl.BlockSpec(memory_space=pltpu.VMEM)] * count
 
 
+def tight(mebibytes):
+    return pltpu.CompilerParams(vmem_limit_bytes=mebibytes * 2**20)
+
+
+def edges_call(seen):
+    arrays, planes, rows, _ = seen[1].shape
+    tiles = arrays * planes * 3 * (rows // 8 + 1)
+    edge = f32(-(-tiles * NEAR // 128) * 8, 128)
+    return pl.pallas_call(
+        edges_kernel,
+        out_shape=(edge, edge),
+        in_specs=in_vmem(5),
+        out_specs=tuple(in_vmem(2)),
+        scratch_shapes=[pltpu.VMEM((8, 128), jnp.float32)],
+        compiler_params=tight(4),
+    )(*seen)
+
+
+def fine_call(seen, peers):
+    _, planes, rows, columns = seen[1].shape
+    field = pltpu.VMEM((3 * planes, rows + 2 * NEAR, 2 * columns), jnp.float32)
+    return pl.pallas_call(
+        fine_kernel,
+        out_shape=(
+            f32(planes, rows, columns),
+            f32(peers, planes // 2, rows // 2, columns),
+        ),
+        in_specs=in_vmem(7),
+        out_specs=tuple(in_vmem(2)),
+        scratch_shapes=[field] * 8
+        + [
+            pltpu.VMEM((planes * rows, columns), jnp.float32),
+            pltpu.VMEM((8, 128), jnp.float32),
+        ],
+        compiler_params=tight(12),
+    )(*seen)
+
+
 def level_one_call(parts, rows, columns):
     planes, tall, wide = parts[2].shape
     planes //= 2
@@ -367,39 +430,12 @@
     )(everyone)
 
 
-def pairs(size):
-    row = lax.broadcasted_iota(jnp.int32, (size, size // 2), 0)
-    column = lax.broadcasted_iota(jnp.int32, (size, size // 2), 1)
-    return (row // 2 == column).astype(jnp.float32)
-
-
-def coarse_sum(field):
-    first, second, third = field.shape
-    planes = field.reshape(first // 2, 2, second, third)
-    planes = planes[:, 0] + planes[:, 1]
-    planes = jnp.einsum("xzy,yb->xzb", planes, pairs(third), precision=lax.Precision.HIGHEST)
-    return jnp.einsum("xzb,za->xab", planes, pairs(second), precision=lax.Precision.HIGHEST)
-
-
 def shards(conductivity, initial_guess, right_side):
-    grown = near_halo(jnp.stack([conductivity, right_side, initial_guess]))
-    inside = inside_mask(
-        grown.shape[1:],
-        (
-            ("gx", 0, conductivity.shape[0]),
-            ("gz", 1, conductivity.shape[1]),
-            ("gy", 2, conductivity.shape[2]),
-        ),
-    )
-    fine, residual_zero = smooth(grown[1], grown[2], grown[0], inside)
-    own = (slice(NEAR, -NEAR),) * 3
-    fine_solution = fine[own]
-
-    source = 0.25 * coarse_sum(residual_zero[own])
-    conduct = 0.125 * coarse_sum(conductivity)
-    planes, rows, columns = source.shape
-    packed = jnp.concatenate([source, conduct], axis=2)
-    everyone = copy_for_each(packed, "gz")
+    seen = near_halo(jnp.stack([conductivity, right_side, initial_guess]))
+    fine_solution, copies = fine_call(seen, lax.axis_size("gz"))
+    planes, rows, columns = copies.shape[1:]
+    columns //= 2
+    everyone = lax.all_to_all(copies, "gz", 0, 0, tiled=True)
     everyone = jnp.moveaxis(everyone, 0, 1).reshape(planes, -1, 2 * columns)
     everyone = jnp.pad(everyone, ((0, 0), (ROWS, ROWS), (0, 0)))
     packed = lax.dynamic_slice_in_dim(

time: 132 us -> 125 us (0.947)
  blocking collectives: 29.6 us -> 45 us
  starting transfers between devices: 58.2 us -> 47.6 us
  other arithmetic: 6.83 us -> 1.38 us
  local copies, waits for them, and re-layouts: 5.5 us -> 0.66 us
  waiting for transfers between devices: 24.8 us -> 20.9 us
  Pallas kernels: 3.97 us -> 7.71 us
    all_to_all x0 -> x1, blocking collectives: none -> 10.6 us  [gathered(): lax.all_to_all(copies, axis, 0, 0, axis_index_groups=beside, tiled=True)]
    all_to_all x2 -> x1, starting transfers between devices: 10.8 us -> 3.37 us  [shards(): everyone = lax.all_to_all(copies, 'gz', 0, 0, tiled=True)]
    all_to_all x2 -> x1, waiting for transfers between devices: 14.9 us -> 7.93 us  [shards(): everyone = lax.all_to_all(copies, 'gz', 0, 0, tiled=True)]
    ppermute x6, starting transfers between devices: 24.3 us -> 17.7 us  [shifted(): lax.ppermute(low_side, axis, forward)]
    all_to_all x1, blocking collectives: 29.6 us -> 34.4 us  [gathered(): lax.all_to_all(copies, axis, 0, 0, axis_index_groups=apart, tiled=True)]
    pallas_call x0 -> x2, Pallas kernels: none -> 3.74 us  [the longest x1 3.27 us: fine_call(): pl.pallas_call(fine_kernel, out_shape=(f32(planes, rows, columns), f32(pe...]
    ppermute x6, waiting for transfers between devices: 4.13 us -> 7.66 us  [shifted(): lax.ppermute(high_side, axis, backward)]
    ppermute x6, starting transfers between devices: 23.1 us -> 26.5 us  [shifted(): lax.ppermute(high_side, axis, backward)]
  transfers between devices with their start and end apart: 14 -> 13, of which waited for: 9 -> 8; matrix products, arithmetic and copies ran while one was open for 3% -> 0% of each run, Pallas kernels for 0% -> 0%
where the time goes in v4:
time: 125 us; the launch traced here: 124 us
  starting transfers between devices  47.6 us (38%)
  blocking collectives  45 us (36%)
  waiting for transfers between devices  20.9 us (17%)
  Pallas kernels  7.71 us (6%)
  other arithmetic  1.38 us (1%)
    all_to_all x1, blocking collectives, gathered(): lax.all_to_all(copies, axis, 0, 0, axis_index_groups=apart, tiled=True)  34.4 us
    ppermute x6, starting transfers between devices, shifted(): lax.ppermute(high_side, axis, backward)  26.5 us
    ppermute x6, starting transfers between devices, shifted(): lax.ppermute(low_side, axis, forward)  17.7 us
    all_to_all x1, blocking collectives, gathered(): lax.all_to_all(copies, axis, 0, 0, axis_index_groups=beside, tiled=True)  10.6 us
    all_to_all x1, waiting for transfers between devices, shards(): everyone = lax.all_to_all(copies, 'gz', 0, 0, tiled=True)  7.93 us
    ppermute x6, waiting for transfers between devices, shifted(): lax.ppermute(high_side, axis, backward)  7.66 us
    ppermute x6, waiting for transfers between devices, shifted(): lax.ppermute(low_side, axis, forward)  5.27 us
    all_to_all x1, starting transfers between devices, shards(): everyone = lax.all_to_all(copies, 'gz', 0, 0, tiled=True)  3.37 us
  transfers between devices with their start and end apart: 13, of which 8 were waited for; matrix products, arithmetic and copies ran while one was open for 0% of the time, Pallas kernels for 0%

profile of v4, /device:TPU:1, one launch (start us, length us, event | category | flops | bytes accessed | tf_op | source)
XLA Modules:
  0.0 124.1 jit_solution(13903588514671316613)
XLA Ops:
  0.6 0.9 pad_maximum_fusion.own
  1.6 16.0 %collective-permute-start.1 = (f32[3,4,32,128]{3,2,1,0:T(8,128)S(1)}, f32[3,4,32,128]{3,2,1,0:T(8,128)S(1)}, u32[]{:S(2)}, u32[]{:S(2)}) collective-permute-start(f32[3,4,32,128]{3,2,1,0:T(8,128)S(1)} %pad_maximum_fusion.own), channel_id=1, source_target_pairs={{32,0},{64,32},{96,64},{128,96},{160,128},{192,160},{224,192},{256... | collective-permute-start | bytes 589832 | tf_op jit(solution)/shard_map/ppermute | solution.py:27
  17.6 1.9 %collective-permute-start = (f32[3,4,32,128]{3,2,1,0:T(8,128)S(1)}, f32[3,4,32,128]{3,2,1,0:T(8,128)S(1)}, u32[]{:S(2)}, u32[]{:S(2)}) collective-permute-start(f32[3,4,32,128]{3,2,1,0:T(8,128)S(1)} %pad_maximum_fusion.own), channel_id=1, source_target_pairs={{0,32},{32,64},{64,96},{96,128},{128,160},{160,192},{192,224},{224... | collective-permute-start | bytes 589832 | tf_op jit(solution)/shard_map/ppermute | solution.py:27
  19.6 2.5 %collective-permute-done.low = f32[3,4,32,128]{3,2,1,0:T(8,128)S(1)} collective-permute-done((f32[3,4,32,128]{3,2,1,0:T(8,128)S(1)}, f32[3,4,32,128]{3,2,1,0:T(8,128)S(1)}, u32[]{:S(2)}, u32[]{:S(2)}) %collective-permute-start) | collective-permute-done | bytes 196640 | tf_op jit(solution)/shard_map/ppermute | solution.py:27
  22.1 1.3 %collective-permute-start.2 = (f32[3,12,4,128]{3,2,1,0:T(4,128)S(1)}, f32[3,12,4,128]{3,2,1,0:T(4,128)S(1)}, u32[]{:S(2)}, u32[]{:S(2)}) collective-permute-start(f32[3,12,4,128]{3,2,1,0:T(4,128)S(1)} %pad_maximum_fusion.6), channel_id=1, source_target_pairs={{0,1},{1,2},{2,3},{3,4},{4,5},{5,6},{6,7},{8,9},{9,10},{10,11},{11... | collective-permute-start | bytes 221192 | tf_op jit(solution)/shard_map/ppermute | solution.py:27
  23.5 1.3 %collective-permute-start.3 = (f32[3,12,4,128]{3,2,1,0:T(4,128)S(1)}, f32[3,12,4,128]{3,2,1,0:T(4,128)S(1)}, u32[]{:S(2)}, u32[]{:S(2)}) collective-permute-start(f32[3,12,4,128]{3,2,1,0:T(4,128)S(1)} %pad_maximum_fusion.7), channel_id=1, source_target_pairs={{1,0},{2,1},{3,2},{4,3},{5,4},{6,5},{7,6},{9,8},{10,9},{11,10},{12... | collective-permute-start | bytes 221192 | tf_op jit(solution)/shard_map/ppermute | solution.py:27
  24.8 3.9 %collective-permute-done.3.above = f32[3,12,4,128]{3,2,1,0:T(4,128)S(1)} collective-permute-done((f32[3,12,4,128]{3,2,1,0:T(4,128)S(1)}, f32[3,12,4,128]{3,2,1,0:T(4,128)S(1)}, u32[]{:S(2)}, u32[]{:S(2)}) %collective-permute-start.3) | collective-permute-done | bytes 73760 | tf_op jit(solution)/shard_map/ppermute | solution.py:27
  28.8 0.5 shard_map.74
  29.3 1.3 %collective-permute-start.4 = (f32[48,128]{1,0:T(8,128)S(1)}, f32[48,128]{1,0:T(8,128)S(1)}, u32[]{:S(2)}, u32[]{:S(2)}) collective-permute-start(f32[48,128]{1,0:T(8,128)S(1)} %get-tuple-element.14), channel_id=1, source_target_pairs={{0,8},{8,16},{16,24},{1,9},{9,17},{17,25},{2,10},{10,18},{18,26},{... | collective-permute-start | bytes 73736 | tf_op jit(solution)/shard_map/ppermute | solution.py:27
  30.6 1.3 %collective-permute-start.5 = (f32[48,128]{1,0:T(8,128)S(1)}, f32[48,128]{1,0:T(8,128)S(1)}, u32[]{:S(2)}, u32[]{:S(2)}) collective-permute-start(f32[48,128]{1,0:T(8,128)S(1)} %get-tuple-element.15), channel_id=1, source_target_pairs={{8,0},{16,8},{24,16},{9,1},{17,9},{25,17},{10,2},{18,10},{26,18},{... | collective-permute-start | bytes 73736 | tf_op jit(solution)/shard_map/ppermute | solution.py:27
  31.9 3.3 %collective-permute-done.5.right = f32[48,128]{1,0:T(8,128)S(1)} collective-permute-done((f32[48,128]{1,0:T(8,128)S(1)}, f32[48,128]{1,0:T(8,128)S(1)}, u32[]{:S(2)}, u32[]{:S(2)}) %collective-permute-start.5) | collective-permute-done | bytes 24608 | tf_op jit(solution)/shard_map/ppermute | solution.py:27
  35.1 3.3 %shard_map.75 = (f32[4,32,128]{2,1,0:T(8,128)}, f32[8,2,16,128]{3,2,1,0:T(8,128)}) custom-call(f32[3,4,32,128]{3,2,1,0:T(8,128)S(1)} %collective-permute-done.low, f32[3,4,32,128]{3,2,1,0:T(8,128)S(1)} %pad_maximum_fusion.own, f32[3,4,32,128]{3,2,1,0:T(8,128)S(1)} %collective-permute-done.1.high, f32[3,12,4,128]{3,2,1,0:T(4,128)S(1)} %collective-permute-done.2.below, ...), custom_call_target="tpu_custom_call" | custom-call | tf_op jit(solution)/shard_map/pallas_call | solution.py:376
  38.4 3.4 %all-to-all-start = ((f32[8,2,16,128]{3,2,1,0:T(8,128)}), f32[8,2,16,128]{3,2,1,0:T(8,128)S(1)}, u32[]{:S(2)}, u32[]{:S(2)}) async-start(f32[8,2,16,128]{3,2,1,0:T(8,128)} %get-tuple-element.17), calls=%async_computation | async-start | bytes 262144 | tf_op jit(solution)/shard_map/all_to_all | solution.py:438
  41.8 7.9 %all-to-all-done = f32[8,2,16,128]{3,2,1,0:T(8,128)S(1)} async-done(((f32[8,2,16,128]{3,2,1,0:T(8,128)}), f32[8,2,16,128]{3,2,1,0:T(8,128)S(1)}, u32[]{:S(2)}, u32[]{:S(2)}) %all-to-all-start) | async-done | bytes 131104 | tf_op jit(solution)/shard_map/all_to_all | solution.py:438
  49.7 0.1 fusion.1
  50.1 0.1 pad_maximum_fusion.9
  50.2 1.3 %collective-permute-start.7 = (f32[64,128]{1,0:T(8,128)S(1)}, f32[64,128]{1,0:T(8,128)S(1)}, u32[]{:S(2)}, u32[]{:S(2)}) collective-permute-start(f32[64,128]{1,0:T(8,128)S(1)} %pad_maximum_fusion.9), channel_id=1, source_target_pairs={{8,0},{16,8},{24,16},{9,1},{17,9},{25,17},{10,2},{18,10},{26,18},{... | collective-permute-start | bytes 98312 | tf_op jit(solution)/shard_map/ppermute | solution.py:27
  51.5 0.1 pad_maximum_fusion.8
  51.6 4.0 %collective-permute-start.6 = (f32[64,128]{1,0:T(8,128)S(1)}, f32[64,128]{1,0:T(8,128)S(1)}, u32[]{:S(2)}, u32[]{:S(2)}) collective-permute-start(f32[64,128]{1,0:T(8,128)S(1)} %pad_maximum_fusion.8), channel_id=1, source_target_pairs={{0,8},{8,16},{16,24},{1,9},{9,17},{17,25},{2,10},{10,18},{18,26},{... | collective-permute-start | bytes 98312 | tf_op jit(solution)/shard_map/ppermute | solution.py:27
  55.7 0.9 collective-permute-done.6
  56.7 0.1 maximum_bitcast_fusion
  56.8 0.1 maximum_bitcast_fusion.2
  57.0 5.4 %collective-permute-start.10 = (f32[4,64,128]{2,1,0:T(8,128)S(1)}, f32[4,64,128]{2,1,0:T(8,128)S(1)}, u32[]{:S(2)}, u32[]{:S(2)}) collective-permute-start(f32[4,64,128]{2,1,0:T(8,128)S(1)} %pad_maximum_fusion.1.own), channel_id=1, source_target_pairs={{32,0},{64,32},{96,64},{128,96},{160,128},{192,160},{224,192},{256... | collective-permute-start | bytes 393224 | tf_op jit(solution)/shard_map/ppermute | solution.py:27
  62.3 5.2 %collective-permute-start.9 = (f32[4,64,128]{2,1,0:T(8,128)S(1)}, f32[4,64,128]{2,1,0:T(8,128)S(1)}, u32[]{:S(2)}, u32[]{:S(2)}) collective-permute-start(f32[4,64,128]{2,1,0:T(8,128)S(1)} %pad_maximum_fusion.1.own), channel_id=1, source_target_pairs={{0,32},{32,64},{64,96},{96,128},{128,160},{160,192},{192,224},{224... | collective-permute-start | bytes 393224 | tf_op jit(solution)/shard_map/ppermute | solution.py:27
  67.6 1.3 %collective-permute-start.11 = (f32[3,64,128]{2,1,0:T(8,128)S(1)}, f32[3,64,128]{2,1,0:T(8,128)S(1)}, u32[]{:S(2)}, u32[]{:S(2)}) collective-permute-start(f32[3,64,128]{2,1,0:T(8,128)S(1)} %get-tuple-element.33), channel_id=1, source_target_pairs={{64,0},{96,32},{128,64},{160,96},{192,128},{224,160},{256,192},{28... | collective-permute-start | bytes 294920 | tf_op jit(solution)/shard_map/ppermute | solution.py:27
  68.9 4.0 %collective-permute-start.8 = (f32[3,64,128]{2,1,0:T(8,128)S(1)}, f32[3,64,128]{2,1,0:T(8,128)S(1)}, u32[]{:S(2)}, u32[]{:S(2)}) collective-permute-start(f32[3,64,128]{2,1,0:T(8,128)S(1)} %get-tuple-element.34), channel_id=1, source_target_pairs={{0,64},{32,96},{64,128},{96,160},{128,192},{160,224},{192,256},{22... | collective-permute-start | bytes 294920 | tf_op jit(solution)/shard_map/ppermute | solution.py:27
  72.9 0.5 collective-permute-done.11.far_high
  73.4 1.8 %collective-permute-done.8.far_low = f32[3,64,128]{2,1,0:T(8,128)S(1)} collective-permute-done((f32[3,64,128]{2,1,0:T(8,128)S(1)}, f32[3,64,128]{2,1,0:T(8,128)S(1)}, u32[]{:S(2)}, u32[]{:S(2)}) %collective-permute-start.8) | collective-permute-done | bytes 98336 | tf_op jit(solution)/shard_map/ppermute | solution.py:27
  75.1 1.4 %shard_map.76 = (f32[2,16,64]{2,1,0:T(8,128)}, f32[8,32,128]{2,1,0:T(8,128)S(1)}) custom-call(f32[3,64,128]{2,1,0:T(8,128)S(1)} %collective-permute-done.8.far_low, f32[4,64,128]{2,1,0:T(8,128)S(1)} %collective-permute-done.9.low, f32[4,64,128]{2,1,0:T(8,128)S(1)} %pad_maximum_fusion.1.own, f32[4,64,128]{2,1,0:T(8,128)S(1)} %collective-permute-done.10.high, ...), custom_call_target="tpu_custom_call" | custom-call | tf_op jit(solution)/shard_map/pallas_call | solution.py:397
  76.5 34.4 %all_to_all.15 = f32[8,32,128]{2,1,0:T(8,128)S(1)} all-to-all(f32[8,32,128]{2,1,0:T(8,128)S(1)} %get-tuple-element.19), channel_id=1, replica_groups={{0,128,256,384,512,640,768,896},{32,160,288,416,544,672,800,928},{64,19..., dimensions={0} | all-to-all | bytes 262144 | tf_op jit(solution)/shard_map/all_to_all | solution.py:47
  111.0 10.6 %all_to_all.16.gathered_ref = f32[4,8,32,128]{3,2,1,0:T(8,128)S(1)} all-to-all(f32[4,8,32,128]{3,2,1,0:T(8,128)S(1)} %broadcast_in_dim.2), channel_id=1, replica_groups={{0,32,64,96},{128,160,192,224},{256,288,320,352},{384,416,448,480},{512..., dimensions={0} | all-to-all | bytes 1048576 | tf_op jit(solution)/shard_map/all_to_all | solution.py:49
  121.6 2.6 %shard_map.77 = (f32[32,8,32]{2,1,0:T(8,128)}, f32[16,4,16]{2,1,0:T(4,128)}, f32[16,4,16]{2,1,0:T(4,128)}) custom-call(f32[4,8,32,128]{3,2,1,0:T(8,128)S(1)} %all_to_all.16.gathered_ref), custom_call_target="tpu_custom_call" | custom-call | tf_op jit(solution)/shard_map/pallas_call | solution.py:417
  (21 shorter events, 0.7 us)
Async XLA Ops:
  1.6 18.0 %collective-permute-start.1 = (f32[3,4,32,128]{3,2,1,0:T(8,128)S(1)}, f32[3,4,32,128]{3,2,1,0:T(8,128)S(1)}, u32[]{:S(2)}, u32[]{:S(2)}) collective-permute-start(f32[3,4,32,128]{3,2,1,0:T(8,128)S(1)} %pad_maximum_fusion.own), channel_id=1, source_target_pairs={{32,0},{64,32},{96,64},{128,96},{160,128},{192,160},{224,192},{256... | collective-permute-start | bytes 589832 | tf_op jit(solution)/shard_map/ppermute | solution.py:27
  17.6 4.5 %collective-permute-start = (f32[3,4,32,128]{3,2,1,0:T(8,128)S(1)}, f32[3,4,32,128]{3,2,1,0:T(8,128)S(1)}, u32[]{:S(2)}, u32[]{:S(2)}) collective-permute-start(f32[3,4,32,128]{3,2,1,0:T(8,128)S(1)} %pad_maximum_fusion.own), channel_id=1, source_target_pairs={{0,32},{32,64},{64,96},{96,128},{128,160},{160,192},{192,224},{224... | collective-permute-start | bytes 589832 | tf_op jit(solution)/shard_map/ppermute | solution.py:27
  22.1 2.7 %collective-permute-start.2 = (f32[3,12,4,128]{3,2,1,0:T(4,128)S(1)}, f32[3,12,4,128]{3,2,1,0:T(4,128)S(1)}, u32[]{:S(2)}, u32[]{:S(2)}) collective-permute-start(f32[3,12,4,128]{3,2,1,0:T(4,128)S(1)} %pad_maximum_fusion.6), channel_id=1, source_target_pairs={{0,1},{1,2},{2,3},{3,4},{4,5},{5,6},{6,7},{8,9},{9,10},{10,11},{11... | collective-permute-start | bytes 221192 | tf_op jit(solution)/shard_map/ppermute | solution.py:27
  23.5 5.3 %collective-permute-start.3 = (f32[3,12,4,128]{3,2,1,0:T(4,128)S(1)}, f32[3,12,4,128]{3,2,1,0:T(4,128)S(1)}, u32[]{:S(2)}, u32[]{:S(2)}) collective-permute-start(f32[3,12,4,128]{3,2,1,0:T(4,128)S(1)} %pad_maximum_fusion.7), channel_id=1, source_target_pairs={{1,0},{2,1},{3,2},{4,3},{5,4},{6,5},{7,6},{9,8},{10,9},{11,10},{12... | collective-permute-start | bytes 221192 | tf_op jit(solution)/shard_map/ppermute | solution.py:27
  29.3 2.6 %collective-permute-start.4 = (f32[48,128]{1,0:T(8,128)S(1)}, f32[48,128]{1,0:T(8,128)S(1)}, u32[]{:S(2)}, u32[]{:S(2)}) collective-permute-start(f32[48,128]{1,0:T(8,128)S(1)} %get-tuple-element.14), channel_id=1, source_target_pairs={{0,8},{8,16},{16,24},{1,9},{9,17},{17,25},{2,10},{10,18},{18,26},{... | collective-permute-start | bytes 73736 | tf_op jit(solution)/shard_map/ppermute | solution.py:27
  30.6 4.6 %collective-permute-start.5 = (f32[48,128]{1,0:T(8,128)S(1)}, f32[48,128]{1,0:T(8,128)S(1)}, u32[]{:S(2)}, u32[]{:S(2)}) collective-permute-start(f32[48,128]{1,0:T(8,128)S(1)} %get-tuple-element.15), channel_id=1, source_target_pairs={{8,0},{16,8},{24,16},{9,1},{17,9},{25,17},{10,2},{18,10},{26,18},{... | collective-permute-start | bytes 73736 | tf_op jit(solution)/shard_map/ppermute | solution.py:27
  38.4 11.3 %all-to-all-start = ((f32[8,2,16,128]{3,2,1,0:T(8,128)}), f32[8,2,16,128]{3,2,1,0:T(8,128)S(1)}, u32[]{:S(2)}, u32[]{:S(2)}) async-start(f32[8,2,16,128]{3,2,1,0:T(8,128)} %get-tuple-element.17), calls=%async_computation | async-start | bytes 262144 | tf_op jit(solution)/shard_map/all_to_all | solution.py:438
  50.2 5.4 %collective-permute-start.7 = (f32[64,128]{1,0:T(8,128)S(1)}, f32[64,128]{1,0:T(8,128)S(1)}, u32[]{:S(2)}, u32[]{:S(2)}) collective-permute-start(f32[64,128]{1,0:T(8,128)S(1)} %pad_maximum_fusion.9), channel_id=1, source_target_pairs={{8,0},{16,8},{24,16},{9,1},{17,9},{25,17},{10,2},{18,10},{26,18},{... | collective-permute-start | bytes 98312 | tf_op jit(solution)/shard_map/ppermute | solution.py:27
  51.6 5.0 %collective-permute-start.6 = (f32[64,128]{1,0:T(8,128)S(1)}, f32[64,128]{1,0:T(8,128)S(1)}, u32[]{:S(2)}, u32[]{:S(2)}) collective-permute-start(f32[64,128]{1,0:T(8,128)S(1)} %pad_maximum_fusion.8), channel_id=1, source_target_pairs={{0,8},{8,16},{16,24},{1,9},{9,17},{17,25},{2,10},{10,18},{18,26},{... | collective-permute-start | bytes 98312 | tf_op jit(solution)/shard_map/ppermute | solution.py:27
  57.0 18.1 %collective-permute-start.10 = (f32[4,64,128]{2,1,0:T(8,128)S(1)}, f32[4,64,128]{2,1,0:T(8,128)S(1)}, u32[]{:S(2)}, u32[]{:S(2)}) collective-permute-start(f32[4,64,128]{2,1,0:T(8,128)S(1)} %pad_maximum_fusion.1.own), channel_id=1, source_target_pairs={{32,0},{64,32},{96,64},{128,96},{160,128},{192,160},{224,192},{256... | collective-permute-start | bytes 393224 | tf_op jit(solution)/shard_map/ppermute | solution.py:27
  62.3 12.8 %collective-permute-start.9 = (f32[4,64,128]{2,1,0:T(8,128)S(1)}, f32[4,64,128]{2,1,0:T(8,128)S(1)}, u32[]{:S(2)}, u32[]{:S(2)}) collective-permute-start(f32[4,64,128]{2,1,0:T(8,128)S(1)} %pad_maximum_fusion.1.own), channel_id=1, source_target_pairs={{0,32},{32,64},{64,96},{96,128},{128,160},{160,192},{192,224},{224... | collective-permute-start | bytes 393224 | tf_op jit(solution)/shard_map/ppermute | solution.py:27
  67.6 5.8 %collective-permute-start.11 = (f32[3,64,128]{2,1,0:T(8,128)S(1)}, f32[3,64,128]{2,1,0:T(8,128)S(1)}, u32[]{:S(2)}, u32[]{:S(2)}) collective-permute-start(f32[3,64,128]{2,1,0:T(8,128)S(1)} %get-tuple-element.33), channel_id=1, source_target_pairs={{64,0},{96,32},{128,64},{160,96},{192,128},{224,160},{256,192},{28... | collective-permute-start | bytes 294920 | tf_op jit(solution)/shard_map/ppermute | solution.py:27
  68.9 6.2 %collective-permute-start.8 = (f32[3,64,128]{2,1,0:T(8,128)S(1)}, f32[3,64,128]{2,1,0:T(8,128)S(1)}, u32[]{:S(2)}, u32[]{:S(2)}) collective-permute-start(f32[3,64,128]{2,1,0:T(8,128)S(1)} %get-tuple-element.34), channel_id=1, source_target_pairs={{0,64},{32,96},{64,128},{96,160},{128,192},{160,224},{192,256},{22... | collective-permute-start | bytes 294920 | tf_op jit(solution)/shard_map/ppermute | solution.py:27

commit v5 on v4

--- a/solution.py
+++ b/solution.py
@@ -13,7 +13,9 @@
 NEAR = 4
 ROWS = 24
 COLUMNS = 32
-INNER = 4
+REACH = 10
+SKIP = ROWS // 2 - REACH
+EDGE = COLUMNS // 2 - REACH
 
 
 def steps(axis, by):
@@ -22,8 +24,14 @@
     return forward, [(b, a) for a, b in forward]
 
 
+def around(axis, by):
+    count = lax.axis_size(axis)
+    forward = [(i, (i + by) % count) for i in range(count)]
+    return forward, [(b, a) for a, b in forward]
+
+
 def shifted(low_side, high_side, axis, by=1):
-    forward, backward = steps(axis, by)
+    forward, backward = around(axis, by) if axis == "gx" else steps(axis, by)
     return lax.ppermute(low_side, axis, forward), lax.ppermute(high_side, axis, backward)
 
 
@@ -42,11 +50,9 @@
 
 def gathered(copies, axis):
     outer = copies.shape[0]
-    apart = [[i + INNER * j for j in range(outer)] for i in range(INNER)]
-    beside = [[INNER * j + i for i in range(INNER)] for j in range(outer)]
-    shard = lax.all_to_all(copies, axis, 0, 0, axis_index_groups=apart, tiled=True)
-    copies = jnp.broadcast_to(shard[None], (INNER, *shard.shape))
-    return lax.all_to_all(copies, axis, 0, 0, axis_index_groups=beside, tiled=True)
+    apart = [[i + 2 * j for j in range(outer)] for i in range(2)]
+    mine = lax.all_to_all(copies, axis, 0, 0, axis_index_groups=apart, tiled=True)
+    return mine, lax.ppermute(mine, axis, [(i, i ^ 1) for i in range(2 * outer)])
 
 
 THETA = 0.5 * (upper_bound + lower_bound)
@@ -94,10 +100,25 @@
     )
 
 
-def pairing(shift):
-    row = lax.broadcasted_iota(jnp.int32, (128, 128), 0)
+def pairing(shift, skip=0):
+    half = lax.broadcasted_iota(jnp.int32, (128, 128), 0) >> 1
     column = lax.broadcasted_iota(jnp.int32, (128, 128), 1)
-    return jnp.where((row >> 1) + shift == column, 1.0, 0.0)
+    kept = (half >= skip) & (half < 64 - skip) & (half + shift - skip == column)
+    return jnp.where(kept, 1.0, 0.0)
+
+
+def turned(tile, shift):
+    return pltpu.roll(tile, shift % 128, 1) if shift % 128 else tile
+
+
+def message_shape(rows):
+    wide = 64 - 2 * EDGE
+    spare = 128 - 2 * wide
+    kept = rows - 2 * SKIP
+    body = kept // 8 * 8
+    pieces = -(-2 * wide // spare)
+    assert pieces * (kept - body) <= body
+    return wide, spare, kept, body, pieces
 
 
 def paired(left, right):
@@ -117,6 +138,11 @@
             corner[:NEAR] = above[a, p]
             corner[NEAR:] = below[a, p]
             yield a, p, rows, corner[...]
+
+
+def exists(step):
+    index = lax.axis_index("gx") + step
+    return (index >= 0) & (index < lax.axis_size("gx"))
 
 
 def edges_kernel(low, own, high, below, above, right_edge, left_edge, corner):
@@ -134,10 +160,6 @@
         left_edge[place] = left
 
 
-def turned(tile, shift):
-    return pltpu.roll(tile, shift % 128, 1) if shift % 128 else tile
-
-
 def fine_kernel(
     low, own, high, below, above, left, right, solution_ref, packed_ref,
     c, r, u, d, wx, wz, wy, inv, both, corner,
@@ -151,6 +173,10 @@
         place = pl.ds(8 * (t // slots), 8)
         near = jnp.where(lane < NEAR, turned(right[place], -NEAR * k), 0.0)
         near = jnp.where(lane >= 128 - NEAR, turned(left[place], -NEAR * (k + 1)), near)
+        if p // planes != 1 and a != 1:
+            valid = exists(p // planes - 1)
+            tile = jnp.where(valid, tile, 0.0)
+            near = jnp.where(valid, near, 0.0)
         field = (c, r, u)[a]
         field[p, row : row + 8, :128] = tile
         field[p, row : row + 8, 128:] = near
@@ -216,8 +242,11 @@
 
     def conduct(p):
         if p // planes in whole:
-            return whole[p // planes][planes + p % planes]
-        return (far_low if p < first else far_high)[1 + p % planes]
+            plane = whole[p // planes][planes + p % planes]
+        else:
+            plane = (far_low if p < first else far_high)[1 + p % planes]
+        step = p // planes - 2
+        return jnp.where(exists(step), plane, 0.0) if step else plane
 
     def origin(p):
         if p // planes in whole:
@@ -259,7 +288,19 @@
     both[:tall] = 0.25 * (r[first] + r[first + 1])
     both[tall:] = 0.125 * (conduct(first) + conduct(first + 1))
     halved = both[pl.ds(0, tall, stride=2)] + both[pl.ds(1, tall, stride=2)]
-    packed = paired(halved[: tall // 2], pairing(0)) + paired(halved[tall // 2 :], pairing(64))
+    tall //= 2
+    wide, spare, kept, body, pieces = message_shape(tall)
+    both[:tall] = paired(halved[:tall], pairing(0, EDGE)) + paired(
+        halved[tall:], pairing(wide, EDGE)
+    )
+    rest = both[SKIP + body : SKIP + kept]
+    tail = 2 * tall
+    both[tail : tail + body] = jnp.zeros((body, 128), jnp.float32)
+    for k in range(pieces):
+        place = tail + k * (kept - body)
+        both[place : place + kept - body] = turned(rest, 2 * wide - spare * k)
+    lane = lax.broadcasted_iota(jnp.int32, (body, 128), 1)
+    packed = jnp.where(lane < 2 * wide, both[SKIP : SKIP + body], both[tail : tail + body])
     for copy in range(packed_ref.shape[0]):
         packed_ref[copy] = packed
 
@@ -310,23 +351,49 @@
 
 
 def coarse_kernel(
-    gathered_ref,
+    mine,
+    other,
     two_ref,
     three_ref,
     residual_ref,
     c, r, d, s, wx, wz, wy, inv, both,
     c3, r3, d3, s3, wx3, wz3, wy3, inv3,
 ):
-    inner = gathered_ref.shape[0]
     count = c.shape[0]
-    lane = lax.broadcasted_iota(jnp.int32, c.shape[1:], 1)
+    even = (lax.axis_index("gx") & 1) == 0
+
+    def message(x):
+        first, second = mine[x // 2], other[x // 2]
+        return jnp.where(even if x % 2 == 0 else ~even, first, second)
+
+    wide, spare, kept, body, pieces = message_shape(c.shape[1])
+
+    def spread(p, place, front, back):
+        lane = lax.broadcasted_iota(jnp.int32, front.shape, 1)
+        inside = (lane & 63) < wide
+        conduct = jnp.where(lane < 64, turned(front, -wide), turned(back, 64 - wide))
+        r[p, place] = jnp.where(lane < 64, front, turned(back, 64))
+        c[p, place] = jnp.where(inside, conduct, 0.0)
+
+    def rest(message):
+        rows = kept - body
+        lane = lax.broadcasted_iota(jnp.int32, (rows, 128), 1)
+        found = jnp.zeros((rows, 128), jnp.float32)
+        for k in range(pieces):
+            piece = turned(message[k * rows : (k + 1) * rows], spare * k - 2 * wide)
+            found = jnp.where((lane >= spare * k) & (lane < spare * (k + 1)), piece, found)
+        return found
+
+    edge = jnp.zeros((SKIP, 128), jnp.float32)
     for p in range(count):
-        front = gathered_ref[p % inner, p // inner]
-        back = gathered_ref[(p + count) % inner, (p + count) // inner]
-        r[p] = jnp.where(lane < 64, front, pltpu.roll(back, 64, 1))
-        c[p] = jnp.where(lane < 64, pltpu.roll(front, 64, 1), back)
+        front, back = message(p), message(p + count)
+        for field in (r, c):
+            field[p, :SKIP] = edge
+            field[p, SKIP + kept :] = edge
+        spread(p, slice(SKIP, SKIP + body), front, back)
+        spread(p, slice(SKIP + body, SKIP + kept), rest(front), rest(back))
     smooth_folded(64, c, r, d, s, wx, wz, wy, inv)
-    unfold(s, 64, ROWS // 2, COLUMNS // 2, two_ref)
+    unfold(s, 64, ROWS // 2, REACH, two_ref)
     tall = c.shape[1]
     half = count // 2
     for p in range(half):
@@ -340,8 +407,8 @@
         r3[p] = coarse[p * low : (p + 1) * low]
         c3[p] = coarse[(half + p) * low : (half + p + 1) * low]
     smooth_folded(32, c3, r3, d3, s3, wx3, wz3, wy3, inv3)
-    unfold(s3, 32, ROWS // 4, COLUMNS // 4, three_ref)
-    unfold(r3, 32, ROWS // 4, COLUMNS // 4, residual_ref)
+    unfold(s3, 32, ROWS // 4, REACH // 2, three_ref)
+    unfold(r3, 32, ROWS // 4, REACH // 2, residual_ref)
 
 
 def f32(*shape):
@@ -396,7 +463,7 @@
     total = planes * len(parts)
     return pl.pallas_call(
         level_one_kernel,
-        out_shape=(f32(planes, rows, columns), f32(lax.axis_size("gx") // INNER, tall // 2, wide)),
+        out_shape=(f32(planes, rows, columns), f32(lax.axis_size("gx") // 2, message_shape(tall // 2)[3], wide)),
         in_specs=in_vmem(5),
         out_specs=tuple(in_vmem(2)),
         scratch_shapes=[pltpu.VMEM((total, tall, wide), jnp.float32)] * 6
@@ -405,9 +472,9 @@
     )(*parts)
 
 
-def coarse_call(everyone, rows, columns):
-    inner, outer, tall, wide = everyone.shape
-    count = inner * outer // 2
+def coarse_call(halves, rows, columns):
+    count, _, wide = halves[0].shape
+    tall = rows + ROWS
 
     def scratch(planes, height):
         field = pltpu.VMEM((planes, height, wide), jnp.float32)
@@ -421,26 +488,26 @@
             f32(count, rows // 2, columns // 2),
             f32(count, rows // 2, columns // 2),
         ),
-        in_specs=in_vmem(1),
+        in_specs=in_vmem(2),
         out_specs=tuple(in_vmem(3)),
         scratch_shapes=scratch(count, tall)
         + [pltpu.VMEM((count * tall, wide), jnp.float32)]
         + scratch(count // 2, tall // 2),
         compiler_params=pltpu.CompilerParams(vmem_limit_bytes=8 * 2**20),
-    )(everyone)
+    )(*halves)
 
 
 def shards(conductivity, initial_guess, right_side):
     seen = near_halo(jnp.stack([conductivity, right_side, initial_guess]))
+    rows = conductivity.shape[1] // 2
+    row, *seen = lax.optimization_barrier(((lax.axis_index("gz") * rows).astype(jnp.uint32), *seen))
     fine_solution, copies = fine_call(seen, lax.axis_size("gz"))
     planes, rows, columns = copies.shape[1:]
     columns //= 2
     everyone = lax.all_to_all(copies, "gz", 0, 0, tiled=True)
     everyone = jnp.moveaxis(everyone, 0, 1).reshape(planes, -1, 2 * columns)
     everyone = jnp.pad(everyone, ((0, 0), (ROWS, ROWS), (0, 0)))
-    packed = lax.dynamic_slice_in_dim(
-        everyone, lax.axis_index("gz") * rows, rows + 2 * ROWS, axis=1
-    )
+    packed = lax.dynamic_slice_in_dim(everyone, row, rows + 2 * ROWS, axis=1)
     pieces = [packed[p, :, q * columns : (q + 1) * columns] for q in (0, 1) for p in range(planes)]
     left, right = shifted(
         jnp.concatenate([piece[:, -COLUMNS:] for piece in pieces], axis=1),
@@ -467,9 +534,9 @@
     level_one_solution, packed = level_one_call(
         (far[0], near[0], own, near[1], far[1]), rows, columns
     )
-    everyone = gathered(packed, "gx")
+    halves = gathered(packed, "gx")
     level_two_solution, level_three_solution, level_three_residual = coarse_call(
-        everyone, rows // 2, columns // 2
+        halves, rows // 2, columns // 2
     )
     return (
         fine_solution,

time: 125 us -> 113 us (0.904)
  blocking collectives: 45 us -> 19.7 us
  starting transfers between devices: 47.6 us -> 58.2 us
  waiting for transfers between devices: 20.9 us -> 22.6 us
    all_to_all x1, blocking collectives: 34.4 us -> 19.7 us  [gathered(): lax.all_to_all(copies, axis, 0, 0, axis_index_groups=apart, tiled=True)]
    all_to_all x1 -> x0, blocking collectives: 10.6 us -> none  [gathered(): lax.all_to_all(copies, axis, 0, 0, axis_index_groups=beside, tiled=True)]
    ppermute x6, starting transfers between devices: 26.5 us -> 36.9 us  [shifted(): lax.ppermute(high_side, axis, backward)]
    ppermute x6, starting transfers between devices: 17.7 us -> 13.8 us  [shifted(): lax.ppermute(low_side, axis, forward)]
    ppermute x0 -> x1, starting transfers between devices: none -> 3.87 us  [gathered(): lax.ppermute(mine, axis, [(i, i ^ 1) for i in range(2 * outer)])]
    ppermute x6, waiting for transfers between devices: 5.27 us -> 6.92 us  [shifted(): lax.ppermute(low_side, axis, forward)]
  transfers between devices with their start and end apart: 13 -> 14, of which waited for: 8 -> 8; matrix products, arithmetic and copies ran while one was open for 0% -> 0% of each run, Pallas kernels for 0% -> 0%
where the time goes in v5:
time: 113 us; the launch traced here: 112 us
  starting transfers between devices  58.2 us (52%)
  waiting for transfers between devices  22.6 us (20%)
  blocking collectives  19.7 us (17%)
  Pallas kernels  8.74 us (8%)
  other arithmetic  1.37 us (1%)
    ppermute x6, starting transfers between devices, shifted(): lax.ppermute(high_side, axis, backward)  36.9 us
    all_to_all x1, blocking collectives, gathered(): lax.all_to_all(copies, axis, 0, 0, axis_index_groups=apart, tiled=True)  19.7 us
    ppermute x6, starting transfers between devices, shifted(): lax.ppermute(low_side, axis, forward)  13.8 us
    all_to_all x1, waiting for transfers between devices, shards(): everyone = lax.all_to_all(copies, 'gz', 0, 0, tiled=True)  7.93 us
    ppermute x6, waiting for transfers between devices, shifted(): lax.ppermute(low_side, axis, forward)  6.92 us
    ppermute x6, waiting for transfers between devices, shifted(): lax.ppermute(high_side, axis, backward)  6.67 us
    ppermute x1, starting transfers between devices, gathered(): lax.ppermute(mine, axis, [(i, i ^ 1) for i in range(2 * outer)])  3.87 us
    all_to_all x1, starting transfers between devices, shards(): everyone = lax.all_to_all(copies, 'gz', 0, 0, tiled=True)  3.71 us
  transfers between devices with their start and end apart: 14, of which 8 were waited for; matrix products, arithmetic and copies ran while one was open for 0% of the time, Pallas kernels for 0%

profile of v5, /device:TPU:1, one launch (start us, length us, event | category | flops | bytes accessed | tf_op | source)
XLA Modules:
  0.0 112.0 jit_solution(14377423367979931292)
XLA Ops:
  0.6 0.9 pad_maximum_fusion.own
  1.6 3.5 %collective-permute-start = (f32[3,4,32,128]{3,2,1,0:T(8,128)S(1)}, f32[3,4,32,128]{3,2,1,0:T(8,128)S(1)}, u32[]{:S(2)}, u32[]{:S(2)}) collective-permute-start(f32[3,4,32,128]{3,2,1,0:T(8,128)S(1)} %pad_maximum_fusion.own), channel_id=1, source_target_pairs={{0,32},{32,64},{64,96},{96,128},{128,160},{160,192},{192,224},{224... | collective-permute-start | bytes 589832 | tf_op jit(solution)/shard_map/ppermute | solution.py:35
  5.0 10.7 %collective-permute-start.1 = (f32[3,4,32,128]{3,2,1,0:T(8,128)S(1)}, f32[3,4,32,128]{3,2,1,0:T(8,128)S(1)}, u32[]{:S(2)}, u32[]{:S(2)}) collective-permute-start(f32[3,4,32,128]{3,2,1,0:T(8,128)S(1)} %pad_maximum_fusion.own), channel_id=1, source_target_pairs={{32,0},{64,32},{96,64},{128,96},{160,128},{192,160},{224,192},{256... | collective-permute-start | bytes 589832 | tf_op jit(solution)/shard_map/ppermute | solution.py:35
  15.7 0.9 collective-permute-done.low
  16.6 0.1 collective-permute-done.1.high
  16.8 1.3 %collective-permute-start.3 = (f32[3,12,4,128]{3,2,1,0:T(4,128)S(1)}, f32[3,12,4,128]{3,2,1,0:T(4,128)S(1)}, u32[]{:S(2)}, u32[]{:S(2)}) collective-permute-start(f32[3,12,4,128]{3,2,1,0:T(4,128)S(1)} %pad_maximum_fusion.7), channel_id=1, source_target_pairs={{1,0},{2,1},{3,2},{4,3},{5,4},{6,5},{7,6},{9,8},{10,9},{11,10},{12... | collective-permute-start | bytes 221192 | tf_op jit(solution)/shard_map/ppermute | solution.py:35
  18.1 4.0 %collective-permute-start.2 = (f32[3,12,4,128]{3,2,1,0:T(4,128)S(1)}, f32[3,12,4,128]{3,2,1,0:T(4,128)S(1)}, u32[]{:S(2)}, u32[]{:S(2)}) collective-permute-start(f32[3,12,4,128]{3,2,1,0:T(4,128)S(1)} %pad_maximum_fusion.6), channel_id=1, source_target_pairs={{0,1},{1,2},{2,3},{3,4},{4,5},{5,6},{6,7},{8,9},{9,10},{10,11},{11... | collective-permute-start | bytes 221192 | tf_op jit(solution)/shard_map/ppermute | solution.py:35
  22.2 1.4 %collective-permute-done.2.below = f32[3,12,4,128]{3,2,1,0:T(4,128)S(1)} collective-permute-done((f32[3,12,4,128]{3,2,1,0:T(4,128)S(1)}, f32[3,12,4,128]{3,2,1,0:T(4,128)S(1)}, u32[]{:S(2)}, u32[]{:S(2)}) %collective-permute-start.2) | collective-permute-done | bytes 73760 | tf_op jit(solution)/shard_map/ppermute | solution.py:35
  23.5 0.5 shard_map.74
  24.0 1.3 %collective-permute-start.4 = (f32[48,128]{1,0:T(8,128)S(1)}, f32[48,128]{1,0:T(8,128)S(1)}, u32[]{:S(2)}, u32[]{:S(2)}) collective-permute-start(f32[48,128]{1,0:T(8,128)S(1)} %get-tuple-element.22), channel_id=1, source_target_pairs={{0,8},{8,16},{16,24},{1,9},{9,17},{17,25},{2,10},{10,18},{18,26},{... | collective-permute-start | bytes 73736 | tf_op jit(solution)/shard_map/ppermute | solution.py:35
  25.3 1.3 %collective-permute-start.5 = (f32[48,128]{1,0:T(8,128)S(1)}, f32[48,128]{1,0:T(8,128)S(1)}, u32[]{:S(2)}, u32[]{:S(2)}) collective-permute-start(f32[48,128]{1,0:T(8,128)S(1)} %get-tuple-element.23), channel_id=1, source_target_pairs={{8,0},{16,8},{24,16},{9,1},{17,9},{25,17},{10,2},{18,10},{26,18},{... | collective-permute-start | bytes 73736 | tf_op jit(solution)/shard_map/ppermute | solution.py:35
  26.6 3.3 %collective-permute-done.5.right = f32[48,128]{1,0:T(8,128)S(1)} collective-permute-done((f32[48,128]{1,0:T(8,128)S(1)}, f32[48,128]{1,0:T(8,128)S(1)}, u32[]{:S(2)}, u32[]{:S(2)}) %collective-permute-start.5) | collective-permute-done | bytes 24608 | tf_op jit(solution)/shard_map/ppermute | solution.py:35
  29.9 3.3 %shard_map.75 = (f32[4,32,128]{2,1,0:T(8,128)}, f32[8,2,16,128]{3,2,1,0:T(8,128)}) custom-call(f32[3,4,32,128]{3,2,1,0:T(8,128)S(1)} %collective-permute-done.low, f32[3,4,32,128]{3,2,1,0:T(8,128)S(1)} %pad_maximum_fusion.own, f32[3,4,32,128]{3,2,1,0:T(8,128)S(1)} %collective-permute-done.1.high, f32[3,12,4,128]{3,2,1,0:T(4,128)S(1)} %collective-permute-done.2.below, ...), custom_call_target="tpu_custom_call" | custom-call | tf_op jit(solution)/shard_map/pallas_call | solution.py:443
  33.2 3.7 %all-to-all-start = ((f32[8,2,16,128]{3,2,1,0:T(8,128)}), f32[8,2,16,128]{3,2,1,0:T(8,128)S(1)}, u32[]{:S(2)}, u32[]{:S(2)}) async-start(f32[8,2,16,128]{3,2,1,0:T(8,128)} %get-tuple-element.32), calls=%async_computation | async-start | bytes 262144 | tf_op jit(solution)/shard_map/all_to_all | solution.py:507
  36.9 7.9 %all-to-all-done = f32[8,2,16,128]{3,2,1,0:T(8,128)S(1)} async-done(((f32[8,2,16,128]{3,2,1,0:T(8,128)}), f32[8,2,16,128]{3,2,1,0:T(8,128)S(1)}, u32[]{:S(2)}, u32[]{:S(2)}) %all-to-all-start) | async-done | bytes 131104 | tf_op jit(solution)/shard_map/all_to_all | solution.py:507
  44.8 0.1 fusion.1
  45.2 0.1 pad_maximum_fusion.8
  45.3 3.1 %collective-permute-start.6 = (f32[64,128]{1,0:T(8,128)S(1)}, f32[64,128]{1,0:T(8,128)S(1)}, u32[]{:S(2)}, u32[]{:S(2)}) collective-permute-start(f32[64,128]{1,0:T(8,128)S(1)} %pad_maximum_fusion.8), channel_id=1, source_target_pairs={{0,8},{8,16},{16,24},{1,9},{9,17},{17,25},{2,10},{10,18},{18,26},{... | collective-permute-start | bytes 98312 | tf_op jit(solution)/shard_map/ppermute | solution.py:35
  48.5 0.1 pad_maximum_fusion.9
  48.6 1.3 %collective-permute-start.7 = (f32[64,128]{1,0:T(8,128)S(1)}, f32[64,128]{1,0:T(8,128)S(1)}, u32[]{:S(2)}, u32[]{:S(2)}) collective-permute-start(f32[64,128]{1,0:T(8,128)S(1)} %pad_maximum_fusion.9), channel_id=1, source_target_pairs={{8,0},{16,8},{24,16},{9,1},{17,9},{25,17},{10,2},{18,10},{26,18},{... | collective-permute-start | bytes 98312 | tf_op jit(solution)/shard_map/ppermute | solution.py:35
  50.0 3.3 %collective-permute-done.7 = f32[64,128]{1,0:T(8,128)S(1)} collective-permute-done((f32[64,128]{1,0:T(8,128)S(1)}, f32[64,128]{1,0:T(8,128)S(1)}, u32[]{:S(2)}, u32[]{:S(2)}) %collective-permute-start.7) | collective-permute-done | bytes 32800 | tf_op jit(solution)/shard_map/ppermute | solution.py:35
  53.3 0.1 maximum_bitcast_fusion
  53.4 0.1 maximum_bitcast_fusion.2
  53.6 17.8 %collective-permute-start.10 = (f32[4,64,128]{2,1,0:T(8,128)S(1)}, f32[4,64,128]{2,1,0:T(8,128)S(1)}, u32[]{:S(2)}, u32[]{:S(2)}) collective-permute-start(f32[4,64,128]{2,1,0:T(8,128)S(1)} %pad_maximum_fusion.1.own), channel_id=1, source_target_pairs={{32,0},{64,32},{96,64},{128,96},{160,128},{192,160},{224,192},{256... | collective-permute-start | bytes 393224 | tf_op jit(solution)/shard_map/ppermute | solution.py:35
  71.4 4.5 %collective-permute-start.11 = (f32[3,64,128]{2,1,0:T(8,128)S(1)}, f32[3,64,128]{2,1,0:T(8,128)S(1)}, u32[]{:S(2)}, u32[]{:S(2)}) collective-permute-start(f32[3,64,128]{2,1,0:T(8,128)S(1)} %get-tuple-element.49), channel_id=1, source_target_pairs={{64,0},{96,32},{128,64},{160,96},{192,128},{224,160},{256,192},{28... | collective-permute-start | bytes 294920 | tf_op jit(solution)/shard_map/ppermute | solution.py:35
  75.9 1.9 %collective-permute-start.8 = (f32[3,64,128]{2,1,0:T(8,128)S(1)}, f32[3,64,128]{2,1,0:T(8,128)S(1)}, u32[]{:S(2)}, u32[]{:S(2)}) collective-permute-start(f32[3,64,128]{2,1,0:T(8,128)S(1)} %get-tuple-element.50), channel_id=1, source_target_pairs={{0,64},{32,96},{64,128},{96,160},{128,192},{160,224},{192,256},{22... | collective-permute-start | bytes 294920 | tf_op jit(solution)/shard_map/ppermute | solution.py:35
  77.8 4.6 %collective-permute-done.8.far_low = f32[3,64,128]{2,1,0:T(8,128)S(1)} collective-permute-done((f32[3,64,128]{2,1,0:T(8,128)S(1)}, f32[3,64,128]{2,1,0:T(8,128)S(1)}, u32[]{:S(2)}, u32[]{:S(2)}) %collective-permute-start.8) | collective-permute-done | bytes 98336 | tf_op jit(solution)/shard_map/ppermute | solution.py:35
  82.5 1.7 %shard_map.76 = (f32[2,16,64]{2,1,0:T(8,128)}, f32[16,24,128]{2,1,0:T(8,128)S(1)}) custom-call(f32[3,64,128]{2,1,0:T(8,128)S(1)} %collective-permute-done.8.far_low, f32[4,64,128]{2,1,0:T(8,128)S(1)} %collective-permute-done.9.low, f32[4,64,128]{2,1,0:T(8,128)S(1)} %pad_maximum_fusion.1.own, f32[4,64,128]{2,1,0:T(8,128)S(1)} %collective-permute-done.10.high, ...), custom_call_target="tpu_custom_call" | custom-call | tf_op jit(solution)/shard_map/pallas_call | solution.py:464
  84.1 19.7 %all_to_all.10.mine = f32[16,24,128]{2,1,0:T(8,128)S(1)} all-to-all(f32[16,24,128]{2,1,0:T(8,128)S(1)} %get-tuple-element.35), channel_id=1, replica_groups={{0,64,128,192,256,320,384,448,512,576,640,704,768,832,896,960},{32,96,1..., dimensions={0} | all-to-all | bytes 393216 | tf_op jit(solution)/shard_map/all_to_all | solution.py:54
  103.8 3.9 %collective-permute-start.12 = (f32[16,24,128]{2,1,0:T(8,128)S(1)}, f32[16,24,128]{2,1,0:T(8,128)S(1)}, u32[]{:S(2)}, u32[]{:S(2)}) collective-permute-start(f32[16,24,128]{2,1,0:T(8,128)S(1)} %all_to_all.10.mine), channel_id=1, source_target_pairs={{0,32},{32,0},{64,96},{96,64},{128,160},{160,128},{192,224},{224,1... | collective-permute-start | bytes 589832 | tf_op jit(solution)/shard_map/ppermute | solution.py:55
  107.7 1.0 collective-permute-done.12.other
  108.7 3.3 %shard_map.77 = (f32[32,8,32]{2,1,0:T(8,128)}, f32[16,4,16]{2,1,0:T(4,128)}, f32[16,4,16]{2,1,0:T(4,128)}) custom-call(f32[16,24,128]{2,1,0:T(8,128)S(1)} %all_to_all.10.mine, f32[16,24,128]{2,1,0:T(8,128)S(1)} %collective-permute-done.12.other), custom_call_target="tpu_custom_call" | custom-call | tf_op jit(solution)/shard_map/pallas_call | solution.py:484
  (21 shorter events, 0.6 us)
Async XLA Ops:
  1.6 15.1 %collective-permute-start = (f32[3,4,32,128]{3,2,1,0:T(8,128)S(1)}, f32[3,4,32,128]{3,2,1,0:T(8,128)S(1)}, u32[]{:S(2)}, u32[]{:S(2)}) collective-permute-start(f32[3,4,32,128]{3,2,1,0:T(8,128)S(1)} %pad_maximum_fusion.own), channel_id=1, source_target_pairs={{0,32},{32,64},{64,96},{96,128},{128,160},{160,192},{192,224},{224... | collective-permute-start | bytes 589832 | tf_op jit(solution)/shard_map/ppermute | solution.py:35
  5.0 11.7 %collective-permute-start.1 = (f32[3,4,32,128]{3,2,1,0:T(8,128)S(1)}, f32[3,4,32,128]{3,2,1,0:T(8,128)S(1)}, u32[]{:S(2)}, u32[]{:S(2)}) collective-permute-start(f32[3,4,32,128]{3,2,1,0:T(8,128)S(1)} %pad_maximum_fusion.own), channel_id=1, source_target_pairs={{32,0},{64,32},{96,64},{128,96},{160,128},{192,160},{224,192},{256... | collective-permute-start | bytes 589832 | tf_op jit(solution)/shard_map/ppermute | solution.py:35
  16.8 5.3 %collective-permute-start.3 = (f32[3,12,4,128]{3,2,1,0:T(4,128)S(1)}, f32[3,12,4,128]{3,2,1,0:T(4,128)S(1)}, u32[]{:S(2)}, u32[]{:S(2)}) collective-permute-start(f32[3,12,4,128]{3,2,1,0:T(4,128)S(1)} %pad_maximum_fusion.7), channel_id=1, source_target_pairs={{1,0},{2,1},{3,2},{4,3},{5,4},{6,5},{7,6},{9,8},{10,9},{11,10},{12... | collective-permute-start | bytes 221192 | tf_op jit(solution)/shard_map/ppermute | solution.py:35
  18.1 5.4 %collective-permute-start.2 = (f32[3,12,4,128]{3,2,1,0:T(4,128)S(1)}, f32[3,12,4,128]{3,2,1,0:T(4,128)S(1)}, u32[]{:S(2)}, u32[]{:S(2)}) collective-permute-start(f32[3,12,4,128]{3,2,1,0:T(4,128)S(1)} %pad_maximum_fusion.6), channel_id=1, source_target_pairs={{0,1},{1,2},{2,3},{3,4},{4,5},{5,6},{6,7},{8,9},{9,10},{10,11},{11... | collective-permute-start | bytes 221192 | tf_op jit(solution)/shard_map/ppermute | solution.py:35
  24.0 2.6 %collective-permute-start.4 = (f32[48,128]{1,0:T(8,128)S(1)}, f32[48,128]{1,0:T(8,128)S(1)}, u32[]{:S(2)}, u32[]{:S(2)}) collective-permute-start(f32[48,128]{1,0:T(8,128)S(1)} %get-tuple-element.22), channel_id=1, source_target_pairs={{0,8},{8,16},{16,24},{1,9},{9,17},{17,25},{2,10},{10,18},{18,26},{... | collective-permute-start | bytes 73736 | tf_op jit(solution)/shard_map/ppermute | solution.py:35
  25.3 4.6 %collective-permute-start.5 = (f32[48,128]{1,0:T(8,128)S(1)}, f32[48,128]{1,0:T(8,128)S(1)}, u32[]{:S(2)}, u32[]{:S(2)}) collective-permute-start(f32[48,128]{1,0:T(8,128)S(1)} %get-tuple-element.23), channel_id=1, source_target_pairs={{8,0},{16,8},{24,16},{9,1},{17,9},{25,17},{10,2},{18,10},{26,18},{... | collective-permute-start | bytes 73736 | tf_op jit(solution)/shard_map/ppermute | solution.py:35
  33.2 11.6 %all-to-all-start = ((f32[8,2,16,128]{3,2,1,0:T(8,128)}), f32[8,2,16,128]{3,2,1,0:T(8,128)S(1)}, u32[]{:S(2)}, u32[]{:S(2)}) async-start(f32[8,2,16,128]{3,2,1,0:T(8,128)} %get-tuple-element.32), calls=%async_computation | async-start | bytes 262144 | tf_op jit(solution)/shard_map/all_to_all | solution.py:507
  45.3 4.5 %collective-permute-start.6 = (f32[64,128]{1,0:T(8,128)S(1)}, f32[64,128]{1,0:T(8,128)S(1)}, u32[]{:S(2)}, u32[]{:S(2)}) collective-permute-start(f32[64,128]{1,0:T(8,128)S(1)} %pad_maximum_fusion.8), channel_id=1, source_target_pairs={{0,8},{8,16},{16,24},{1,9},{9,17},{17,25},{2,10},{10,18},{18,26},{... | collective-permute-start | bytes 98312 | tf_op jit(solution)/shard_map/ppermute | solution.py:35
  48.6 4.7 %collective-permute-start.7 = (f32[64,128]{1,0:T(8,128)S(1)}, f32[64,128]{1,0:T(8,128)S(1)}, u32[]{:S(2)}, u32[]{:S(2)}) collective-permute-start(f32[64,128]{1,0:T(8,128)S(1)} %pad_maximum_fusion.9), channel_id=1, source_target_pairs={{8,0},{16,8},{24,16},{9,1},{17,9},{25,17},{10,2},{18,10},{26,18},{... | collective-permute-start | bytes 98312 | tf_op jit(solution)/shard_map/ppermute | solution.py:35
  53.6 28.9 %collective-permute-start.10 = (f32[4,64,128]{2,1,0:T(8,128)S(1)}, f32[4,64,128]{2,1,0:T(8,128)S(1)}, u32[]{:S(2)}, u32[]{:S(2)}) collective-permute-start(f32[4,64,128]{2,1,0:T(8,128)S(1)} %pad_maximum_fusion.1.own), channel_id=1, source_target_pairs={{32,0},{64,32},{96,64},{128,96},{160,128},{192,160},{224,192},{256... | collective-permute-start | bytes 393224 | tf_op jit(solution)/shard_map/ppermute | solution.py:35
  71.3 11.1 %collective-permute-start.9 = (f32[4,64,128]{2,1,0:T(8,128)S(1)}, f32[4,64,128]{2,1,0:T(8,128)S(1)}, u32[]{:S(2)}, u32[]{:S(2)}) collective-permute-start(f32[4,64,128]{2,1,0:T(8,128)S(1)} %pad_maximum_fusion.1.own), channel_id=1, source_target_pairs={{0,32},{32,64},{64,96},{96,128},{128,160},{160,192},{192,224},{224... | collective-permute-start | bytes 393224 | tf_op jit(solution)/shard_map/ppermute | solution.py:35
  71.4 6.5 %collective-permute-start.11 = (f32[3,64,128]{2,1,0:T(8,128)S(1)}, f32[3,64,128]{2,1,0:T(8,128)S(1)}, u32[]{:S(2)}, u32[]{:S(2)}) collective-permute-start(f32[3,64,128]{2,1,0:T(8,128)S(1)} %get-tuple-element.49), channel_id=1, source_target_pairs={{64,0},{96,32},{128,64},{160,96},{192,128},{224,160},{256,192},{28... | collective-permute-start | bytes 294920 | tf_op jit(solution)/shard_map/ppermute | solution.py:35
  75.9 6.6 %collective-permute-start.8 = (f32[3,64,128]{2,1,0:T(8,128)S(1)}, f32[3,64,128]{2,1,0:T(8,128)S(1)}, u32[]{:S(2)}, u32[]{:S(2)}) collective-permute-start(f32[3,64,128]{2,1,0:T(8,128)S(1)} %get-tuple-element.50), channel_id=1, source_target_pairs={{0,64},{32,96},{64,128},{96,160},{128,192},{160,224},{192,256},{22... | collective-permute-start | bytes 294920 | tf_op jit(solution)/shard_map/ppermute | solution.py:35
  103.8 4.9 %collective-permute-start.12 = (f32[16,24,128]{2,1,0:T(8,128)S(1)}, f32[16,24,128]{2,1,0:T(8,128)S(1)}, u32[]{:S(2)}, u32[]{:S(2)}) collective-permute-start(f32[16,24,128]{2,1,0:T(8,128)S(1)} %all_to_all.10.mine), channel_id=1, source_target_pairs={{0,32},{32,0},{64,96},{96,64},{128,160},{160,128},{192,224},{224,1... | collective-permute-start | bytes 589832 | tf_op jit(solution)/shard_map/ppermute | solution.py:55

commit v6 on v5

--- a/solution.py
+++ b/solution.py
@@ -18,12 +18,6 @@
 EDGE = COLUMNS // 2 - REACH
 
 
-def steps(axis, by):
-    count = lax.axis_size(axis)
-    forward = [(i, i + by) for i in range(count - by)]
-    return forward, [(b, a) for a, b in forward]
-
-
 def around(axis, by):
     count = lax.axis_size(axis)
     forward = [(i, (i + by) % count) for i in range(count)]
@@ -31,7 +25,7 @@
 
 
 def shifted(low_side, high_side, axis, by=1):
-    forward, backward = around(axis, by) if axis == "gx" else steps(axis, by)
+    forward, backward = around(axis, by)
     return lax.ppermute(low_side, axis, forward), lax.ppermute(high_side, axis, backward)
 
 
@@ -135,14 +129,14 @@
             part = parts[p // planes]
             for row in range(0, rows, 8):
                 yield a, p, row, part[a, p % planes, row : row + 8]
-            corner[:NEAR] = above[a, p]
-            corner[NEAR:] = below[a, p]
+            corner[:NEAR] = jnp.where(exists(1, "gz"), above[a, p], 0.0)
+            corner[NEAR:] = jnp.where(exists(-1, "gz"), below[a, p], 0.0)
             yield a, p, rows, corner[...]
 
 
-def exists(step):
-    index = lax.axis_index("gx") + step
-    return (index >= 0) & (index < lax.axis_size("gx"))
+def exists(step, axis="gx"):
+    index = lax.axis_index(axis) + step
+    return (index >= 0) & (index < lax.axis_size(axis))
 
 
 def edges_kernel(low, own, high, below, above, right_edge, left_edge, corner):
@@ -171,8 +165,10 @@
     for t, (a, p, row, tile) in enumerate(fine_tiles(low, own, high, below, above, corner)):
         k = t % slots
         place = pl.ds(8 * (t // slots), 8)
-        near = jnp.where(lane < NEAR, turned(right[place], -NEAR * k), 0.0)
-        near = jnp.where(lane >= 128 - NEAR, turned(left[place], -NEAR * (k + 1)), near)
+        near = jnp.where((lane < NEAR) & exists(1, "gy"), turned(right[place], -NEAR * k), 0.0)
+        near = jnp.where(
+            (lane >= 128 - NEAR) & exists(-1, "gy"), turned(left[place], -NEAR * (k + 1)), near
+        )
         if p // planes != 1 and a != 1:
             valid = exists(p // planes - 1)
             tile = jnp.where(valid, tile, 0.0)
@@ -514,6 +510,8 @@
         jnp.concatenate([piece[:, :COLUMNS] for piece in pieces], axis=1),
         "gy",
     )
+    left = jnp.where(exists(-1, "gy"), left, 0.0)
+    right = jnp.where(exists(1, "gy"), right, 0.0)
     pieces = [
         jnp.concatenate(
             [

time: 113 us -> 113 us (level)
  waiting for transfers between devices: 22.6 us -> 19.3 us
  starting transfers between devices: 58.2 us -> 61.5 us
    ppermute x6, starting transfers between devices: 36.9 us -> 41.6 us  [shifted(): lax.ppermute(high_side, axis, backward)]
    ppermute x6, waiting for transfers between devices: 6.67 us -> 1.94 us  [shifted(): lax.ppermute(high_side, axis, backward)]
    ppermute x6, waiting for transfers between devices: 6.92 us -> 8.47 us  [shifted(): lax.ppermute(low_side, axis, forward)]
    ppermute x6, starting transfers between devices: 13.8 us -> 12.6 us  [shifted(): lax.ppermute(low_side, axis, forward)]
where the time goes in v6:
time: 113 us; the launch traced here: 112 us
  starting transfers between devices  61.5 us (54%)
  blocking collectives  19.7 us (17%)
  waiting for transfers between devices  19.3 us (17%)
  Pallas kernels  8.74 us (8%)
  other arithmetic  1.39 us (1%)
    ppermute x6, starting transfers between devices, shifted(): lax.ppermute(high_side, axis, backward)  41.6 us
    all_to_all x1, blocking collectives, gathered(): lax.all_to_all(copies, axis, 0, 0, axis_index_groups=apart, tiled=True)  19.7 us
    ppermute x6, starting transfers between devices, shifted(): lax.ppermute(low_side, axis, forward)  12.6 us
    ppermute x6, waiting for transfers between devices, shifted(): lax.ppermute(low_side, axis, forward)  8.47 us
    all_to_all x1, waiting for transfers between devices, shards(): everyone = lax.all_to_all(copies, 'gz', 0, 0, tiled=True)  7.82 us
    ppermute x1, starting transfers between devices, gathered(): lax.ppermute(mine, axis, [(i, i ^ 1) for i in range(2 * outer)])  3.87 us
    all_to_all x1, starting transfers between devices, shards(): everyone = lax.all_to_all(copies, 'gz', 0, 0, tiled=True)  3.37 us
    pallas_call x1, Pallas kernels, coarse_call(): pl.pallas_call(coarse_kernel, out_shape=(f32(2 * count, rows, columns), f...  3.3 us
  transfers between devices with their start and end apart: 14, of which 8 were waited for; matrix products, arithmetic and copies ran while one was open for 0% of the time, Pallas kernels for 0%

profile of v6, /device:TPU:1, one launch (start us, length us, event | category | flops | bytes accessed | tf_op | source)
XLA Modules:
  0.0 112.0 jit_solution(18106998844910083067)
XLA Ops:
  0.6 0.9 pad_maximum_fusion.own
  1.6 3.5 %collective-permute-start = (f32[3,4,32,128]{3,2,1,0:T(8,128)S(1)}, f32[3,4,32,128]{3,2,1,0:T(8,128)S(1)}, u32[]{:S(2)}, u32[]{:S(2)}) collective-permute-start(f32[3,4,32,128]{3,2,1,0:T(8,128)S(1)} %pad_maximum_fusion.own), channel_id=1, source_target_pairs={{0,32},{32,64},{64,96},{96,128},{128,160},{160,192},{192,224},{224... | collective-permute-start | bytes 589832 | tf_op jit(solution)/shard_map/ppermute | solution.py:29
  5.0 10.7 %collective-permute-start.1 = (f32[3,4,32,128]{3,2,1,0:T(8,128)S(1)}, f32[3,4,32,128]{3,2,1,0:T(8,128)S(1)}, u32[]{:S(2)}, u32[]{:S(2)}) collective-permute-start(f32[3,4,32,128]{3,2,1,0:T(8,128)S(1)} %pad_maximum_fusion.own), channel_id=1, source_target_pairs={{32,0},{64,32},{96,64},{128,96},{160,128},{192,160},{224,192},{256... | collective-permute-start | bytes 589832 | tf_op jit(solution)/shard_map/ppermute | solution.py:29
  15.7 0.9 collective-permute-done.low
  16.6 0.1 collective-permute-done.1.high
  16.8 1.9 %collective-permute-start.3 = (f32[3,12,4,128]{3,2,1,0:T(4,128)S(1)}, f32[3,12,4,128]{3,2,1,0:T(4,128)S(1)}, u32[]{:S(2)}, u32[]{:S(2)}) collective-permute-start(f32[3,12,4,128]{3,2,1,0:T(4,128)S(1)} %pad_maximum_fusion.7), channel_id=1, source_target_pairs={{1,0},{2,1},{3,2},{4,3},{5,4},{6,5},{7,6},{0,7},{9,8},{10,9},{11,1... | collective-permute-start | bytes 221192 | tf_op jit(solution)/shard_map/ppermute | solution.py:29
  18.8 3.4 %collective-permute-start.2 = (f32[3,12,4,128]{3,2,1,0:T(4,128)S(1)}, f32[3,12,4,128]{3,2,1,0:T(4,128)S(1)}, u32[]{:S(2)}, u32[]{:S(2)}) collective-permute-start(f32[3,12,4,128]{3,2,1,0:T(4,128)S(1)} %pad_maximum_fusion.6), channel_id=1, source_target_pairs={{0,1},{1,2},{2,3},{3,4},{4,5},{5,6},{6,7},{7,0},{8,9},{9,10},{10,1... | collective-permute-start | bytes 221192 | tf_op jit(solution)/shard_map/ppermute | solution.py:29
  22.2 2.9 %collective-permute-done.2.below = f32[3,12,4,128]{3,2,1,0:T(4,128)S(1)} collective-permute-done((f32[3,12,4,128]{3,2,1,0:T(4,128)S(1)}, f32[3,12,4,128]{3,2,1,0:T(4,128)S(1)}, u32[]{:S(2)}, u32[]{:S(2)}) %collective-permute-start.2) | collective-permute-done | bytes 73760 | tf_op jit(solution)/shard_map/ppermute | solution.py:29
  25.1 0.5 shard_map.74
  25.6 1.9 %collective-permute-start.4 = (f32[48,128]{1,0:T(8,128)S(1)}, f32[48,128]{1,0:T(8,128)S(1)}, u32[]{:S(2)}, u32[]{:S(2)}) collective-permute-start(f32[48,128]{1,0:T(8,128)S(1)} %get-tuple-element.22), channel_id=1, source_target_pairs={{0,8},{8,16},{16,24},{24,0},{1,9},{9,17},{17,25},{25,1},{2,10},{10... | collective-permute-start | bytes 73736 | tf_op jit(solution)/shard_map/ppermute | solution.py:29
  27.5 4.6 %collective-permute-start.5 = (f32[48,128]{1,0:T(8,128)S(1)}, f32[48,128]{1,0:T(8,128)S(1)}, u32[]{:S(2)}, u32[]{:S(2)}) collective-permute-start(f32[48,128]{1,0:T(8,128)S(1)} %get-tuple-element.23), channel_id=1, source_target_pairs={{8,0},{16,8},{24,16},{0,24},{9,1},{17,9},{25,17},{1,25},{10,2},{18... | collective-permute-start | bytes 73736 | tf_op jit(solution)/shard_map/ppermute | solution.py:29
  32.1 0.9 collective-permute-done.5.right
  33.0 3.3 %shard_map.75 = (f32[4,32,128]{2,1,0:T(8,128)}, f32[8,2,16,128]{3,2,1,0:T(8,128)}) custom-call(f32[3,4,32,128]{3,2,1,0:T(8,128)S(1)} %collective-permute-done.low, f32[3,4,32,128]{3,2,1,0:T(8,128)S(1)} %pad_maximum_fusion.own, f32[3,4,32,128]{3,2,1,0:T(8,128)S(1)} %collective-permute-done.1.high, f32[3,12,4,128]{3,2,1,0:T(4,128)S(1)} %collective-permute-done.2.below, ...), custom_call_target="tpu_custom_call" | custom-call | tf_op jit(solution)/shard_map/pallas_call | solution.py:439
  36.3 3.4 %all-to-all-start = ((f32[8,2,16,128]{3,2,1,0:T(8,128)}), f32[8,2,16,128]{3,2,1,0:T(8,128)S(1)}, u32[]{:S(2)}, u32[]{:S(2)}) async-start(f32[8,2,16,128]{3,2,1,0:T(8,128)} %get-tuple-element.32), calls=%async_computation | async-start | bytes 262144 | tf_op jit(solution)/shard_map/all_to_all | solution.py:503
  39.7 7.8 %all-to-all-done = f32[8,2,16,128]{3,2,1,0:T(8,128)S(1)} async-done(((f32[8,2,16,128]{3,2,1,0:T(8,128)}), f32[8,2,16,128]{3,2,1,0:T(8,128)S(1)}, u32[]{:S(2)}, u32[]{:S(2)}) %all-to-all-start) | async-done | bytes 131104 | tf_op jit(solution)/shard_map/all_to_all | solution.py:503
  47.5 0.1 fusion.1
  47.9 0.1 pad_maximum_fusion.8
  48.0 1.9 %collective-permute-start.6 = (f32[64,128]{1,0:T(8,128)S(1)}, f32[64,128]{1,0:T(8,128)S(1)}, u32[]{:S(2)}, u32[]{:S(2)}) collective-permute-start(f32[64,128]{1,0:T(8,128)S(1)} %pad_maximum_fusion.8), channel_id=1, source_target_pairs={{0,8},{8,16},{16,24},{24,0},{1,9},{9,17},{17,25},{25,1},{2,10},{10... | collective-permute-start | bytes 98312 | tf_op jit(solution)/shard_map/ppermute | solution.py:29
  50.0 0.1 pad_maximum_fusion.9
  50.0 4.8 %collective-permute-start.7 = (f32[64,128]{1,0:T(8,128)S(1)}, f32[64,128]{1,0:T(8,128)S(1)}, u32[]{:S(2)}, u32[]{:S(2)}) collective-permute-start(f32[64,128]{1,0:T(8,128)S(1)} %pad_maximum_fusion.9), channel_id=1, source_target_pairs={{8,0},{16,8},{24,16},{0,24},{9,1},{17,9},{25,17},{1,25},{10,2},{18... | collective-permute-start | bytes 98312 | tf_op jit(solution)/shard_map/ppermute | solution.py:29
  55.0 0.9 collective-permute-done.7
  56.0 0.1 maximum_bitcast_fusion
  56.1 0.1 maximum_bitcast_fusion.2
  56.2 15.1 %collective-permute-start.10 = (f32[4,64,128]{2,1,0:T(8,128)S(1)}, f32[4,64,128]{2,1,0:T(8,128)S(1)}, u32[]{:S(2)}, u32[]{:S(2)}) collective-permute-start(f32[4,64,128]{2,1,0:T(8,128)S(1)} %pad_maximum_fusion.1.own), channel_id=1, source_target_pairs={{32,0},{64,32},{96,64},{128,96},{160,128},{192,160},{224,192},{256... | collective-permute-start | bytes 393224 | tf_op jit(solution)/shard_map/ppermute | solution.py:29
  71.4 4.5 %collective-permute-start.11 = (f32[3,64,128]{2,1,0:T(8,128)S(1)}, f32[3,64,128]{2,1,0:T(8,128)S(1)}, u32[]{:S(2)}, u32[]{:S(2)}) collective-permute-start(f32[3,64,128]{2,1,0:T(8,128)S(1)} %get-tuple-element.49), channel_id=1, source_target_pairs={{64,0},{96,32},{128,64},{160,96},{192,128},{224,160},{256,192},{28... | collective-permute-start | bytes 294920 | tf_op jit(solution)/shard_map/ppermute | solution.py:29
  75.9 1.9 %collective-permute-start.8 = (f32[3,64,128]{2,1,0:T(8,128)S(1)}, f32[3,64,128]{2,1,0:T(8,128)S(1)}, u32[]{:S(2)}, u32[]{:S(2)}) collective-permute-start(f32[3,64,128]{2,1,0:T(8,128)S(1)} %get-tuple-element.50), channel_id=1, source_target_pairs={{0,64},{32,96},{64,128},{96,160},{128,192},{160,224},{192,256},{22... | collective-permute-start | bytes 294920 | tf_op jit(solution)/shard_map/ppermute | solution.py:29
  77.8 4.6 %collective-permute-done.8.far_low = f32[3,64,128]{2,1,0:T(8,128)S(1)} collective-permute-done((f32[3,64,128]{2,1,0:T(8,128)S(1)}, f32[3,64,128]{2,1,0:T(8,128)S(1)}, u32[]{:S(2)}, u32[]{:S(2)}) %collective-permute-start.8) | collective-permute-done | bytes 98336 | tf_op jit(solution)/shard_map/ppermute | solution.py:29
  82.5 1.7 %shard_map.76 = (f32[2,16,64]{2,1,0:T(8,128)}, f32[16,24,128]{2,1,0:T(8,128)S(1)}) custom-call(f32[3,64,128]{2,1,0:T(8,128)S(1)} %collective-permute-done.8.far_low, f32[4,64,128]{2,1,0:T(8,128)S(1)} %collective-permute-done.9.low, f32[4,64,128]{2,1,0:T(8,128)S(1)} %pad_maximum_fusion.1.own, f32[4,64,128]{2,1,0:T(8,128)S(1)} %collective-permute-done.10.high, ...), custom_call_target="tpu_custom_call" | custom-call | tf_op jit(solution)/shard_map/pallas_call | solution.py:460
  84.1 19.7 %all_to_all.10.mine = f32[16,24,128]{2,1,0:T(8,128)S(1)} all-to-all(f32[16,24,128]{2,1,0:T(8,128)S(1)} %get-tuple-element.35), channel_id=1, replica_groups={{0,64,128,192,256,320,384,448,512,576,640,704,768,832,896,960},{32,96,1..., dimensions={0} | all-to-all | bytes 393216 | tf_op jit(solution)/shard_map/all_to_all | solution.py:48
  103.8 3.9 %collective-permute-start.12 = (f32[16,24,128]{2,1,0:T(8,128)S(1)}, f32[16,24,128]{2,1,0:T(8,128)S(1)}, u32[]{:S(2)}, u32[]{:S(2)}) collective-permute-start(f32[16,24,128]{2,1,0:T(8,128)S(1)} %all_to_all.10.mine), channel_id=1, source_target_pairs={{0,32},{32,0},{64,96},{96,64},{128,160},{160,128},{192,224},{224,1... | collective-permute-start | bytes 589832 | tf_op jit(solution)/shard_map/ppermute | solution.py:49
  107.7 1.0 collective-permute-done.12.other
  108.7 3.3 %shard_map.77 = (f32[32,8,32]{2,1,0:T(8,128)}, f32[16,4,16]{2,1,0:T(4,128)}, f32[16,4,16]{2,1,0:T(4,128)}) custom-call(f32[16,24,128]{2,1,0:T(8,128)S(1)} %all_to_all.10.mine, f32[16,24,128]{2,1,0:T(8,128)S(1)} %collective-permute-done.12.other), custom_call_target="tpu_custom_call" | custom-call | tf_op jit(solution)/shard_map/pallas_call | solution.py:480
  (23 shorter events, 0.6 us)
Async XLA Ops:
  1.6 15.1 %collective-permute-start = (f32[3,4,32,128]{3,2,1,0:T(8,128)S(1)}, f32[3,4,32,128]{3,2,1,0:T(8,128)S(1)}, u32[]{:S(2)}, u32[]{:S(2)}) collective-permute-start(f32[3,4,32,128]{3,2,1,0:T(8,128)S(1)} %pad_maximum_fusion.own), channel_id=1, source_target_pairs={{0,32},{32,64},{64,96},{96,128},{128,160},{160,192},{192,224},{224... | collective-permute-start | bytes 589832 | tf_op jit(solution)/shard_map/ppermute | solution.py:29
  5.0 11.7 %collective-permute-start.1 = (f32[3,4,32,128]{3,2,1,0:T(8,128)S(1)}, f32[3,4,32,128]{3,2,1,0:T(8,128)S(1)}, u32[]{:S(2)}, u32[]{:S(2)}) collective-permute-start(f32[3,4,32,128]{3,2,1,0:T(8,128)S(1)} %pad_maximum_fusion.own), channel_id=1, source_target_pairs={{32,0},{64,32},{96,64},{128,96},{160,128},{192,160},{224,192},{256... | collective-permute-start | bytes 589832 | tf_op jit(solution)/shard_map/ppermute | solution.py:29
  16.8 5.3 %collective-permute-start.3 = (f32[3,12,4,128]{3,2,1,0:T(4,128)S(1)}, f32[3,12,4,128]{3,2,1,0:T(4,128)S(1)}, u32[]{:S(2)}, u32[]{:S(2)}) collective-permute-start(f32[3,12,4,128]{3,2,1,0:T(4,128)S(1)} %pad_maximum_fusion.7), channel_id=1, source_target_pairs={{1,0},{2,1},{3,2},{4,3},{5,4},{6,5},{7,6},{0,7},{9,8},{10,9},{11,1... | collective-permute-start | bytes 221192 | tf_op jit(solution)/shard_map/ppermute | solution.py:29
  18.8 6.3 %collective-permute-start.2 = (f32[3,12,4,128]{3,2,1,0:T(4,128)S(1)}, f32[3,12,4,128]{3,2,1,0:T(4,128)S(1)}, u32[]{:S(2)}, u32[]{:S(2)}) collective-permute-start(f32[3,12,4,128]{3,2,1,0:T(4,128)S(1)} %pad_maximum_fusion.6), channel_id=1, source_target_pairs={{0,1},{1,2},{2,3},{3,4},{4,5},{5,6},{6,7},{7,0},{8,9},{9,10},{10,1... | collective-permute-start | bytes 221192 | tf_op jit(solution)/shard_map/ppermute | solution.py:29
  25.6 6.5 %collective-permute-start.4 = (f32[48,128]{1,0:T(8,128)S(1)}, f32[48,128]{1,0:T(8,128)S(1)}, u32[]{:S(2)}, u32[]{:S(2)}) collective-permute-start(f32[48,128]{1,0:T(8,128)S(1)} %get-tuple-element.22), channel_id=1, source_target_pairs={{0,8},{8,16},{16,24},{24,0},{1,9},{9,17},{17,25},{25,1},{2,10},{10... | collective-permute-start | bytes 73736 | tf_op jit(solution)/shard_map/ppermute | solution.py:29
  27.5 5.5 %collective-permute-start.5 = (f32[48,128]{1,0:T(8,128)S(1)}, f32[48,128]{1,0:T(8,128)S(1)}, u32[]{:S(2)}, u32[]{:S(2)}) collective-permute-start(f32[48,128]{1,0:T(8,128)S(1)} %get-tuple-element.23), channel_id=1, source_target_pairs={{8,0},{16,8},{24,16},{0,24},{9,1},{17,9},{25,17},{1,25},{10,2},{18... | collective-permute-start | bytes 73736 | tf_op jit(solution)/shard_map/ppermute | solution.py:29
  36.3 11.2 %all-to-all-start = ((f32[8,2,16,128]{3,2,1,0:T(8,128)}), f32[8,2,16,128]{3,2,1,0:T(8,128)S(1)}, u32[]{:S(2)}, u32[]{:S(2)}) async-start(f32[8,2,16,128]{3,2,1,0:T(8,128)} %get-tuple-element.32), calls=%async_computation | async-start | bytes 262144 | tf_op jit(solution)/shard_map/all_to_all | solution.py:503
  48.0 6.9 %collective-permute-start.6 = (f32[64,128]{1,0:T(8,128)S(1)}, f32[64,128]{1,0:T(8,128)S(1)}, u32[]{:S(2)}, u32[]{:S(2)}) collective-permute-start(f32[64,128]{1,0:T(8,128)S(1)} %pad_maximum_fusion.8), channel_id=1, source_target_pairs={{0,8},{8,16},{16,24},{24,0},{1,9},{9,17},{17,25},{25,1},{2,10},{10... | collective-permute-start | bytes 98312 | tf_op jit(solution)/shard_map/ppermute | solution.py:29
  50.0 5.9 %collective-permute-start.7 = (f32[64,128]{1,0:T(8,128)S(1)}, f32[64,128]{1,0:T(8,128)S(1)}, u32[]{:S(2)}, u32[]{:S(2)}) collective-permute-start(f32[64,128]{1,0:T(8,128)S(1)} %pad_maximum_fusion.9), channel_id=1, source_target_pairs={{8,0},{16,8},{24,16},{0,24},{9,1},{17,9},{25,17},{1,25},{10,2},{18... | collective-permute-start | bytes 98312 | tf_op jit(solution)/shard_map/ppermute | solution.py:29
  56.2 26.2 %collective-permute-start.10 = (f32[4,64,128]{2,1,0:T(8,128)S(1)}, f32[4,64,128]{2,1,0:T(8,128)S(1)}, u32[]{:S(2)}, u32[]{:S(2)}) collective-permute-start(f32[4,64,128]{2,1,0:T(8,128)S(1)} %pad_maximum_fusion.1.own), channel_id=1, source_target_pairs={{32,0},{64,32},{96,64},{128,96},{160,128},{192,160},{224,192},{256... | collective-permute-start | bytes 393224 | tf_op jit(solution)/shard_map/ppermute | solution.py:29
  71.4 11.1 %collective-permute-start.9 = (f32[4,64,128]{2,1,0:T(8,128)S(1)}, f32[4,64,128]{2,1,0:T(8,128)S(1)}, u32[]{:S(2)}, u32[]{:S(2)}) collective-permute-start(f32[4,64,128]{2,1,0:T(8,128)S(1)} %pad_maximum_fusion.1.own), channel_id=1, source_target_pairs={{0,32},{32,64},{64,96},{96,128},{128,160},{160,192},{192,224},{224... | collective-permute-start | bytes 393224 | tf_op jit(solution)/shard_map/ppermute | solution.py:29
  71.4 6.5 %collective-permute-start.11 = (f32[3,64,128]{2,1,0:T(8,128)S(1)}, f32[3,64,128]{2,1,0:T(8,128)S(1)}, u32[]{:S(2)}, u32[]{:S(2)}) collective-permute-start(f32[3,64,128]{2,1,0:T(8,128)S(1)} %get-tuple-element.49), channel_id=1, source_target_pairs={{64,0},{96,32},{128,64},{160,96},{192,128},{224,160},{256,192},{28... | collective-permute-start | bytes 294920 | tf_op jit(solution)/shard_map/ppermute | solution.py:29
  75.9 6.6 %collective-permute-start.8 = (f32[3,64,128]{2,1,0:T(8,128)S(1)}, f32[3,64,128]{2,1,0:T(8,128)S(1)}, u32[]{:S(2)}, u32[]{:S(2)}) collective-permute-start(f32[3,64,128]{2,1,0:T(8,128)S(1)} %get-tuple-element.50), channel_id=1, source_target_pairs={{0,64},{32,96},{64,128},{96,160},{128,192},{160,224},{192,256},{22... | collective-permute-start | bytes 294920 | tf_op jit(solution)/shard_map/ppermute | solution.py:29
  103.8 4.9 %collective-permute-start.12 = (f32[16,24,128]{2,1,0:T(8,128)S(1)}, f32[16,24,128]{2,1,0:T(8,128)S(1)}, u32[]{:S(2)}, u32[]{:S(2)}) collective-permute-start(f32[16,24,128]{2,1,0:T(8,128)S(1)} %all_to_all.10.mine), channel_id=1, source_target_pairs={{0,32},{32,0},{64,96},{96,64},{128,160},{160,128},{192,224},{224,1... | collective-permute-start | bytes 589832 | tf_op jit(solution)/shard_map/ppermute | solution.py:49
